TPU v7x, 768 devices: a whole 4x8x12 slice. The times are simulated.
768 devices in a mesh: lat: 96 (over y, z), lon: 8 (over x, core).
Axes of the slice: x: 4, y: 8, z: 12, core: 2. Of those that a mesh axis runs over, the one named last changes fastest.
Arguments:
- prognostic: bfloat16 [9, 768, 3072], P(None, 'lat', 'lon'), may hold values from -6 to 6
- departure: int32 [768, 3072], P('lat', 'lon'), may hold values from 0 to 63
- lat_weight: float32 [768, 3072], P('lat', 'lon'), may hold values from 0 to 1
- lon_weight: float32 [768, 3072], P('lat', 'lon'), may hold values from 0 to 1
- cycle_waves: int32 [768], P('lat'), may hold values from 192 to 768
- wave_order: int32 [768], replicated, may hold values from 0 to 767, each once
Outputs:
- spectral: float32 [768, 2, 9, 768], P(('lat', 'lon'))
Inputs may be any that keep to these rules, and one draw needn't show every extreme that they name: `wave_order`: each of the 768 wavenumbers stands in exactly one slot.
All inputs are finite; a program needn't handle non-finite values.
Results may differ from a plain program's by a relative error of at most 0.0025.
The roundings to bfloat16 on the way count: a program that leaves them out, or rounds other values in their place, can miss the bound.
Values may be sent and summed in bfloat16 or wider, within the bound.
No kernel may reach another device: no remote copies, remote signals or barrier semaphores. Data moves between devices by JAX's collectives and lax.ppermute only.
A program may use at most 128 MiB of HBM per device.

v0:
```python
import math

import jax
import jax.numpy as jnp
from jax import lax
from jax.sharding import PartitionSpec as P

HALO = 4


LGAMMA_HALF_THREE = 0.5 * math.log(math.pi) - math.log(2.0)


def with_halo(cells, sides, width):
    for axis, dim in sides:
        count = lax.axis_size(axis)
        head = lax.slice_in_dim(cells, 0, width, axis=dim)
        tail = lax.slice_in_dim(cells, cells.shape[dim] - width, cells.shape[dim], axis=dim)
        cells = jnp.concatenate(
            [
                lax.ppermute(tail, axis, [(i, (i + 1) % count) for i in range(count)]),
                cells,
                lax.ppermute(head, axis, [((i + 1) % count, i) for i in range(count)]),
            ],
            axis=dim,
        )
    return cells


def legendre_rows(orders, angles, length, ceiling, unroll):
    order_real = orders.astype(jnp.float32)
    cosine = jnp.cos(angles)
    log_start = (
        0.5 * math.log(0.5)
        + 0.5 * (lax.lgamma(order_real + 1.5) - LGAMMA_HALF_THREE - lax.lgamma(order_real + 1.0))
        + order_real * jnp.log(jnp.sin(angles))
    )

    def advance(carry, offset):
        previous, second, log_scale = carry
        degree = order_real + offset
        factor_a = jnp.sqrt(
            (4.0 * degree * degree - 1.0) / (degree * degree - order_real * order_real)
        )
        factor_b = jnp.sqrt(
            jnp.maximum(
                ((degree - 1.0) * (degree - 1.0) - order_real * order_real)
                / (4.0 * (degree - 1.0) * (degree - 1.0) - 1.0),
                0.0,
            )
        )
        fresh = factor_a * (cosine * previous - factor_b * second)
        result = fresh * jnp.exp(log_scale + log_start)
        factor = jnp.maximum(jnp.maximum(jnp.abs(fresh), jnp.abs(previous)), 1.0)
        return ((fresh / factor, previous / factor, log_scale + jnp.log(factor)), result)

    indices = jnp.arange(1, length, dtype=jnp.int32).astype(jnp.float32)
    initial = (jnp.ones_like(cosine), jnp.zeros_like(cosine), jnp.zeros_like(cosine))
    _, later = lax.scan(advance, initial, indices, unroll=unroll)
    values = jnp.concatenate([jnp.exp(log_start)[None, :], later], axis=0)
    inside = jnp.arange(length, dtype=jnp.int32)[:, None] < (ceiling - orders)[None, :]
    return jnp.where(inside, values, 0.0)


def legendre_table(orders, cycle_ids, lat_total, wave_count, unroll):
    cycle_angles = (cycle_ids.astype(jnp.float32) + 0.5) * (math.pi / lat_total)
    slot_count = orders.shape[0]
    cycle_count = cycle_ids.shape[0]
    orders_flat = jnp.repeat(orders, cycle_count)
    angles_flat = jnp.tile(cycle_angles, slot_count)
    values = legendre_rows(orders_flat, angles_flat, wave_count, wave_count, unroll)
    scaled = values * (jnp.sin(angles_flat) * (math.pi / math.sqrt(lat_total)))[None, :]
    return scaled.reshape(wave_count, slot_count, cycle_count).astype(jnp.bfloat16)


def fourier_table(wave_order, points):
    doubled = jnp.repeat(wave_order, 2)
    column = lax.broadcasted_iota(jnp.int32, (points, doubled.shape[0]), 0)
    parity = lax.broadcasted_iota(jnp.int32, (points, doubled.shape[0]), 1) % 2
    phases = column * doubled[None, :] % points
    angles = phases.astype(jnp.float32) * (2.0 * math.pi / points) + parity.astype(jnp.float32) * (
        0.5 * math.pi
    )
    return (jnp.cos(angles) * (1.0 / math.sqrt(points))).astype(jnp.bfloat16)


def shards(prognostic, departure, lat_weight, lon_weight, cycle_waves, wave_order):
    channels, band_rows, sector_cols = prognostic.shape
    lat_devices = lax.axis_size("lat")
    lon_devices = lax.axis_size("lon")
    total_lat = band_rows * lat_devices
    total_lon = sector_cols * lon_devices
    wave_count = wave_order.shape[0]
    margin = HALO
    band_index = lax.axis_index("lat")
    sector_index = lax.axis_index("lon")
    padded = with_halo(prognostic, (("lat", 1), ("lon", 2)), margin)
    ext_rows = band_rows + 2 * margin
    ext_cols = sector_cols + 2 * margin
    global_rows = band_index * band_rows - margin + jnp.arange(ext_rows, dtype=jnp.int32)
    inside = (global_rows >= 0) & (global_rows < total_lat)
    padded = padded * inside.astype(jnp.bfloat16)[None, :, None]
    flat_field = padded.reshape(channels, ext_rows * ext_cols)
    stencil = 2 * margin
    row_shift = departure // stencil - margin
    col_shift = departure % stencil - margin
    row_grid = lax.broadcasted_iota(jnp.int32, (band_rows, sector_cols), 0)
    col_grid = lax.broadcasted_iota(jnp.int32, (band_rows, sector_cols), 1)
    corner = (row_grid + margin + row_shift) * ext_cols + col_grid + margin + col_shift
    corners = jnp.stack([corner, corner + ext_cols, corner + 1, corner + ext_cols + 1]).reshape(-1)
    picked = (
        jnp.take(flat_field, corners, axis=1)
        .reshape(channels, 4, band_rows, sector_cols)
        .astype(jnp.float32)
    )
    arrival = (
        (1.0 - lat_weight) * (1.0 - lon_weight) * picked[:, 0]
        + lat_weight * (1.0 - lon_weight) * picked[:, 1]
        + (1.0 - lat_weight) * lon_weight * picked[:, 2]
        + lat_weight * lon_weight * picked[:, 3]
    ).astype(jnp.bfloat16)
    full_cycles = lax.all_to_all(arrival, "lon", split_axis=1, concat_axis=2, tiled=True)
    per_cycle = band_rows // lon_devices
    fourier = fourier_table(wave_order, total_lon)
    spectrum = jnp.einsum(
        "crj,jq->qcr", full_cycles, fourier, preferred_element_type=jnp.float32
    ).reshape(wave_count, 2, channels, per_cycle)
    band_waves = lax.dynamic_slice_in_dim(cycle_waves, sector_index * per_cycle, per_cycle)
    resolved = wave_order[:, None] < band_waves[None, :]
    masked = jnp.where(resolved[:, None, None, :], spectrum, 0.0).astype(jnp.bfloat16)
    slab_data = lax.all_to_all(masked, "lat", split_axis=0, concat_axis=3, tiled=True)
    slab_slots = slab_data.shape[0]
    cycle_place = jnp.arange(slab_data.shape[3], dtype=jnp.int32)
    cycle_ids = (
        cycle_place // per_cycle * band_rows + sector_index * per_cycle + cycle_place % per_cycle
    )
    slot_ids = band_index * slab_slots + jnp.arange(slab_slots, dtype=jnp.int32)
    functions = legendre_table(wave_order[slot_ids], cycle_ids, total_lat, wave_count, 32)
    return lax.psum_scatter(
        jnp.einsum("sacr,ksr->sack", slab_data, functions, preferred_element_type=jnp.float32),
        "lon",
        scatter_dimension=0,
        tiled=True,
    )


def solution(mesh):
    in_specs = (
        P(None, "lat", "lon"),
        P("lat", "lon"),
        P("lat", "lon"),
        P("lat", "lon"),
        P("lat"),
        P(),
    )
    out_specs = P(("lat", "lon"), None, None, None)
    return jax.shard_map(shards, mesh=mesh, in_specs=in_specs, out_specs=out_specs, check_vma=False)
```

profile of v0, /device:TPU:1, one launch (start us, length us, event | category | flops | bytes accessed | tf_op | source)
XLA Modules:
  0.0 892.9 jit_solution(2072829553301593188)
XLA Ops:
  7.5 18.0 %collective-permute-start.1 = (bf16[9,4,384]{2,1,0:T(4,128)(2,1)S(1)}, bf16[9,4,384]{2,1,0:T(4,128)(2,1)S(1)}, u32[]{:S(2)}, u32[]{:S(2)}) collective-permute-start(bf16[9,4,384]{2,1,0:T(4,128)(2,1)S(1)} %get-tuple-element.574), channel_id=1, source_target_pairs={{8,0},{16,8},{24,16},{32,24},{40,32},{48,40},{56,48},{64,56},{72,6... | collective-permute-start | bytes 82952 | tf_op jit(solution)/shard_map/ppermute | solution.py:23
  25.5 1.9 collective-permute-start
  27.5 1.3 gather_fusion.1
  31.3 542.6 %while.22 = (s32[]{:T(128)}, f32[768]{0:T(1024)S(1)}, f32[768]{0:T(1024)S(1)}, f32[768]{0:T(1024)S(1)}, f32[23,32,768]{2,1,0:T(8,128)}, /*index=5*/f32[23,32]{1,...) while((s32[]{:T(128)}, f32[768]{0:T(1024)S(1)}, ...), condition=%wide.region_1.2_spmd.clone.clone.clone, body=%wide.region_0.1_spmd.clone.clone.clone.sunk | while | flops 732675 | bytes 1131688 | solution.py:59
  33.0 20.5 %exponential_multiply_fusion.66 = (f32[768]{0:T(1024)S(1)}, f32[768]{0:T(1024)S(1)}, f32[768]{0:T(1024)S(1)}, f32[768]{0:T(1024)S(1)}, f32[768]{0:T(1024)S(1)}, ...) fusion(f32[768]{0:T(1024)S(1)} %get-tuple-element.1022, ...), kind=kLoop, calls=%fused_computation.390.clone.1 | loop fusion | flops 661248 | bytes 212097 | tf_op jit(solution)/shard_map/while/body/eval_jaxpr/mul | solution.py:53
  56.5 20.5 %exponential_multiply_fusion.66 = (f32[768]{0:T(1024)S(1)}, f32[768]{0:T(1024)S(1)}, f32[768]{0:T(1024)S(1)}, f32[768]{0:T(1024)S(1)}, f32[768]{0:T(1024)S(1)}, ...) fusion(f32[768]{0:T(1024)S(1)} %get-tuple-element.1022, ...), kind=kLoop, calls=%fused_computation.390.clone.1 | loop fusion | flops 661248 | bytes 212097 | tf_op jit(solution)/shard_map/while/body/eval_jaxpr/mul | solution.py:53
  80.1 20.5 %exponential_multiply_fusion.66 = (f32[768]{0:T(1024)S(1)}, f32[768]{0:T(1024)S(1)}, f32[768]{0:T(1024)S(1)}, f32[768]{0:T(1024)S(1)}, f32[768]{0:T(1024)S(1)}, ...) fusion(f32[768]{0:T(1024)S(1)} %get-tuple-element.1022, ...), kind=kLoop, calls=%fused_computation.390.clone.1 | loop fusion | flops 661248 | bytes 212097 | tf_op jit(solution)/shard_map/while/body/eval_jaxpr/mul | solution.py:53
  103.7 20.5 %exponential_multiply_fusion.66 = (f32[768]{0:T(1024)S(1)}, f32[768]{0:T(1024)S(1)}, f32[768]{0:T(1024)S(1)}, f32[768]{0:T(1024)S(1)}, f32[768]{0:T(1024)S(1)}, ...) fusion(f32[768]{0:T(1024)S(1)} %get-tuple-element.1022, ...), kind=kLoop, calls=%fused_computation.390.clone.1 | loop fusion | flops 661248 | bytes 212097 | tf_op jit(solution)/shard_map/while/body/eval_jaxpr/mul | solution.py:53
  127.3 20.5 %exponential_multiply_fusion.66 = (f32[768]{0:T(1024)S(1)}, f32[768]{0:T(1024)S(1)}, f32[768]{0:T(1024)S(1)}, f32[768]{0:T(1024)S(1)}, f32[768]{0:T(1024)S(1)}, ...) fusion(f32[768]{0:T(1024)S(1)} %get-tuple-element.1022, ...), kind=kLoop, calls=%fused_computation.390.clone.1 | loop fusion | flops 661248 | bytes 212097 | tf_op jit(solution)/shard_map/while/body/eval_jaxpr/mul | solution.py:53
  150.9 20.5 %exponential_multiply_fusion.66 = (f32[768]{0:T(1024)S(1)}, f32[768]{0:T(1024)S(1)}, f32[768]{0:T(1024)S(1)}, f32[768]{0:T(1024)S(1)}, f32[768]{0:T(1024)S(1)}, ...) fusion(f32[768]{0:T(1024)S(1)} %get-tuple-element.1022, ...), kind=kLoop, calls=%fused_computation.390.clone.1 | loop fusion | flops 661248 | bytes 212097 | tf_op jit(solution)/shard_map/while/body/eval_jaxpr/mul | solution.py:53
  174.5 20.5 %exponential_multiply_fusion.66 = (f32[768]{0:T(1024)S(1)}, f32[768]{0:T(1024)S(1)}, f32[768]{0:T(1024)S(1)}, f32[768]{0:T(1024)S(1)}, f32[768]{0:T(1024)S(1)}, ...) fusion(f32[768]{0:T(1024)S(1)} %get-tuple-element.1022, ...), kind=kLoop, calls=%fused_computation.390.clone.1 | loop fusion | flops 661248 | bytes 212097 | tf_op jit(solution)/shard_map/while/body/eval_jaxpr/mul | solution.py:53
  198.1 20.5 %exponential_multiply_fusion.66 = (f32[768]{0:T(1024)S(1)}, f32[768]{0:T(1024)S(1)}, f32[768]{0:T(1024)S(1)}, f32[768]{0:T(1024)S(1)}, f32[768]{0:T(1024)S(1)}, ...) fusion(f32[768]{0:T(1024)S(1)} %get-tuple-element.1022, ...), kind=kLoop, calls=%fused_computation.390.clone.1 | loop fusion | flops 661248 | bytes 212097 | tf_op jit(solution)/shard_map/while/body/eval_jaxpr/mul | solution.py:53
  221.7 20.5 %exponential_multiply_fusion.66 = (f32[768]{0:T(1024)S(1)}, f32[768]{0:T(1024)S(1)}, f32[768]{0:T(1024)S(1)}, f32[768]{0:T(1024)S(1)}, f32[768]{0:T(1024)S(1)}, ...) fusion(f32[768]{0:T(1024)S(1)} %get-tuple-element.1022, ...), kind=kLoop, calls=%fused_computation.390.clone.1 | loop fusion | flops 661248 | bytes 212097 | tf_op jit(solution)/shard_map/while/body/eval_jaxpr/mul | solution.py:53
  245.3 20.5 %exponential_multiply_fusion.66 = (f32[768]{0:T(1024)S(1)}, f32[768]{0:T(1024)S(1)}, f32[768]{0:T(1024)S(1)}, f32[768]{0:T(1024)S(1)}, f32[768]{0:T(1024)S(1)}, ...) fusion(f32[768]{0:T(1024)S(1)} %get-tuple-element.1022, ...), kind=kLoop, calls=%fused_computation.390.clone.1 | loop fusion | flops 661248 | bytes 212097 | tf_op jit(solution)/shard_map/while/body/eval_jaxpr/mul | solution.py:53
  268.9 20.5 %exponential_multiply_fusion.66 = (f32[768]{0:T(1024)S(1)}, f32[768]{0:T(1024)S(1)}, f32[768]{0:T(1024)S(1)}, f32[768]{0:T(1024)S(1)}, f32[768]{0:T(1024)S(1)}, ...) fusion(f32[768]{0:T(1024)S(1)} %get-tuple-element.1022, ...), kind=kLoop, calls=%fused_computation.390.clone.1 | loop fusion | flops 661248 | bytes 212097 | tf_op jit(solution)/shard_map/while/body/eval_jaxpr/mul | solution.py:53
  292.4 20.5 %exponential_multiply_fusion.66 = (f32[768]{0:T(1024)S(1)}, f32[768]{0:T(1024)S(1)}, f32[768]{0:T(1024)S(1)}, f32[768]{0:T(1024)S(1)}, f32[768]{0:T(1024)S(1)}, ...) fusion(f32[768]{0:T(1024)S(1)} %get-tuple-element.1022, ...), kind=kLoop, calls=%fused_computation.390.clone.1 | loop fusion | flops 661248 | bytes 212097 | tf_op jit(solution)/shard_map/while/body/eval_jaxpr/mul | solution.py:53
  316.0 20.5 %exponential_multiply_fusion.66 = (f32[768]{0:T(1024)S(1)}, f32[768]{0:T(1024)S(1)}, f32[768]{0:T(1024)S(1)}, f32[768]{0:T(1024)S(1)}, f32[768]{0:T(1024)S(1)}, ...) fusion(f32[768]{0:T(1024)S(1)} %get-tuple-element.1022, ...), kind=kLoop, calls=%fused_computation.390.clone.1 | loop fusion | flops 661248 | bytes 212097 | tf_op jit(solution)/shard_map/while/body/eval_jaxpr/mul | solution.py:53
  339.6 20.5 %exponential_multiply_fusion.66 = (f32[768]{0:T(1024)S(1)}, f32[768]{0:T(1024)S(1)}, f32[768]{0:T(1024)S(1)}, f32[768]{0:T(1024)S(1)}, f32[768]{0:T(1024)S(1)}, ...) fusion(f32[768]{0:T(1024)S(1)} %get-tuple-element.1022, ...), kind=kLoop, calls=%fused_computation.390.clone.1 | loop fusion | flops 661248 | bytes 212097 | tf_op jit(solution)/shard_map/while/body/eval_jaxpr/mul | solution.py:53
  363.2 20.5 %exponential_multiply_fusion.66 = (f32[768]{0:T(1024)S(1)}, f32[768]{0:T(1024)S(1)}, f32[768]{0:T(1024)S(1)}, f32[768]{0:T(1024)S(1)}, f32[768]{0:T(1024)S(1)}, ...) fusion(f32[768]{0:T(1024)S(1)} %get-tuple-element.1022, ...), kind=kLoop, calls=%fused_computation.390.clone.1 | loop fusion | flops 661248 | bytes 212097 | tf_op jit(solution)/shard_map/while/body/eval_jaxpr/mul | solution.py:53
  386.8 20.5 %exponential_multiply_fusion.66 = (f32[768]{0:T(1024)S(1)}, f32[768]{0:T(1024)S(1)}, f32[768]{0:T(1024)S(1)}, f32[768]{0:T(1024)S(1)}, f32[768]{0:T(1024)S(1)}, ...) fusion(f32[768]{0:T(1024)S(1)} %get-tuple-element.1022, ...), kind=kLoop, calls=%fused_computation.390.clone.1 | loop fusion | flops 661248 | bytes 212097 | tf_op jit(solution)/shard_map/while/body/eval_jaxpr/mul | solution.py:53
  410.4 20.5 %exponential_multiply_fusion.66 = (f32[768]{0:T(1024)S(1)}, f32[768]{0:T(1024)S(1)}, f32[768]{0:T(1024)S(1)}, f32[768]{0:T(1024)S(1)}, f32[768]{0:T(1024)S(1)}, ...) fusion(f32[768]{0:T(1024)S(1)} %get-tuple-element.1022, ...), kind=kLoop, calls=%fused_computation.390.clone.1 | loop fusion | flops 661248 | bytes 212097 | tf_op jit(solution)/shard_map/while/body/eval_jaxpr/mul | solution.py:53
  434.0 20.5 %exponential_multiply_fusion.66 = (f32[768]{0:T(1024)S(1)}, f32[768]{0:T(1024)S(1)}, f32[768]{0:T(1024)S(1)}, f32[768]{0:T(1024)S(1)}, f32[768]{0:T(1024)S(1)}, ...) fusion(f32[768]{0:T(1024)S(1)} %get-tuple-element.1022, ...), kind=kLoop, calls=%fused_computation.390.clone.1 | loop fusion | flops 661248 | bytes 212097 | tf_op jit(solution)/shard_map/while/body/eval_jaxpr/mul | solution.py:53
  457.6 20.5 %exponential_multiply_fusion.66 = (f32[768]{0:T(1024)S(1)}, f32[768]{0:T(1024)S(1)}, f32[768]{0:T(1024)S(1)}, f32[768]{0:T(1024)S(1)}, f32[768]{0:T(1024)S(1)}, ...) fusion(f32[768]{0:T(1024)S(1)} %get-tuple-element.1022, ...), kind=kLoop, calls=%fused_computation.390.clone.1 | loop fusion | flops 661248 | bytes 212097 | tf_op jit(solution)/shard_map/while/body/eval_jaxpr/mul | solution.py:53
  481.2 20.5 %exponential_multiply_fusion.66 = (f32[768]{0:T(1024)S(1)}, f32[768]{0:T(1024)S(1)}, f32[768]{0:T(1024)S(1)}, f32[768]{0:T(1024)S(1)}, f32[768]{0:T(1024)S(1)}, ...) fusion(f32[768]{0:T(1024)S(1)} %get-tuple-element.1022, ...), kind=kLoop, calls=%fused_computation.390.clone.1 | loop fusion | flops 661248 | bytes 212097 | tf_op jit(solution)/shard_map/while/body/eval_jaxpr/mul | solution.py:53
  504.8 20.5 %exponential_multiply_fusion.66 = (f32[768]{0:T(1024)S(1)}, f32[768]{0:T(1024)S(1)}, f32[768]{0:T(1024)S(1)}, f32[768]{0:T(1024)S(1)}, f32[768]{0:T(1024)S(1)}, ...) fusion(f32[768]{0:T(1024)S(1)} %get-tuple-element.1022, ...), kind=kLoop, calls=%fused_computation.390.clone.1 | loop fusion | flops 661248 | bytes 212097 | tf_op jit(solution)/shard_map/while/body/eval_jaxpr/mul | solution.py:53
  528.4 20.5 %exponential_multiply_fusion.66 = (f32[768]{0:T(1024)S(1)}, f32[768]{0:T(1024)S(1)}, f32[768]{0:T(1024)S(1)}, f32[768]{0:T(1024)S(1)}, f32[768]{0:T(1024)S(1)}, ...) fusion(f32[768]{0:T(1024)S(1)} %get-tuple-element.1022, ...), kind=kLoop, calls=%fused_computation.390.clone.1 | loop fusion | flops 661248 | bytes 212097 | tf_op jit(solution)/shard_map/while/body/eval_jaxpr/mul | solution.py:53
  552.0 20.5 %exponential_multiply_fusion.66 = (f32[768]{0:T(1024)S(1)}, f32[768]{0:T(1024)S(1)}, f32[768]{0:T(1024)S(1)}, f32[768]{0:T(1024)S(1)}, f32[768]{0:T(1024)S(1)}, ...) fusion(f32[768]{0:T(1024)S(1)} %get-tuple-element.1022, ...), kind=kLoop, calls=%fused_computation.390.clone.1 | loop fusion | flops 661248 | bytes 212097 | tf_op jit(solution)/shard_map/while/body/eval_jaxpr/mul | solution.py:53
  574.7 76.1 %fusion.333 = bf16[1536,3072]{1,0:T(8,128)(2,1)} fusion(s32[1536]{0:T(1024)S(1)} %get-tuple-element.679, s32[1536]{0:T(1024)S(1)} %get-tuple-element.680, s32[1536]{0:T(1024)S(1)} %mul.3486, pred[1536]{0:T(1024)(128)(4,1)S(1)} %fusion.425), kind=kLoop, calls=%fused_computation.520 | loop fusion | flops 70778880 | bytes 9457152 | tf_op jit(solution)/shard_map/convert_element_type | solution.py:84
  650.8 19.4 %fusion.730 = (f32[768]{0:T(1024)S(1)}, f32[768]{0:T(1024)S(1)}, f32[768]{0:T(1024)S(1)}, f32[768]{0:T(1024)S(1)}, f32[768]{0:T(1024)S(1)}, /*index=5*/f32[768]{...) fusion(f32[768]{0:T(1024)S(1)} %get-tuple-element.1028, ...), kind=kLoop, calls=%fused_computation.1032 | loop fusion | flops 638208 | bytes 187516 | tf_op jit(solution)/shard_map/eval_jaxpr/mul | solution.py:53
  670.8 1.3 add_exponential_fusion
  672.1 1.9 exponential_multiply_fusion.32
  676.4 1.1 collective-permute-start.2
  680.3 3.4 bitcast_multiply_fusion
  683.7 43.7 %gather_fusion = bf16[12288,9]{1,0:T(8,128)(2,1)} fusion(bf16[9,6272]{0,1:T(8,128)(2,1)S(1)} %bitcast_multiply_fusion, s32[12288]{0:T(1024)S(1)} %broadcast_clamp_fusion), kind=kCustom, calls=%fused_computation | custom fusion | bytes 491520 | tf_op jit(solution)/shard_map/jit(_take)/gather | solution.py:112
  727.4 3.3 copy.29
  731.5 7.6 all-to-all-start
  739.2 1.2 broadcast_compare_fusion
  740.4 3.0 concatenate.86
  743.4 2.4 copy.35
  748.3 1.7 concatenate.125
  750.0 1.7 concatenate.126
  751.7 1.7 concatenate.127
  753.4 1.7 concatenate.128
  755.1 1.7 concatenate.129
  756.8 1.7 concatenate.130
  758.6 1.7 concatenate.131
  760.3 1.7 concatenate.132
  762.0 1.7 concatenate.133
  763.7 1.0 concatenate.134
  770.9 1.0 concatenate.141
  772.0 1.0 concatenate.142
  777.1 1.0 concatenate.147
  778.2 1.0 concatenate.148
  780.2 1.1 concatenate.150
  782.3 1.0 concatenate.152
  783.4 19.0 %convert_element_type.81 = bf16[768,2,3072]{2,1,0:T(2,128)(2,1)} reshape(bf16[1536,3072]{1,0:T(8,128)(2,1)} %fusion.333) | data formatting | bytes 18874368 | tf_op jit(solution)/shard_map/convert_element_type | solution.py:84
  802.4 9.5 %concatenate.118 = f32[768,8,96]{0,2,1:T(8,128)S(1)} concatenate(f32[1,8,96]{0,2,1:T(8,128)S(1)} %copy-done.1, f32[736,8,96]{0,2,1:T(8,128)} %copy.35, f32[1,8,96]{0,2,1:T(8,128)S(1)} %concatenate.122, f32[1,8,96]{0,2,1:T(8,128)S(1)} %concatenate.123, f32[1,8,96]{0,2,1:T(8,128)} %concatenate.124, f32[1,8,96]{0,2,1:T(8,128)} %concatenate.125, f32[1,8,96]{0,2,1:T(8,128)} %concatenate.126, ...), dimensions={0} | concatenate | bytes 4718592 | tf_op jit(solution)/shard_map/concatenate | solution.py:60
  812.9 6.3 fusion.349
  819.2 1.1 copy.32
  820.3 9.1 %all-to-all-start.1 = ((bf16[768,2,9,1]{2,1,3,0:T(2,128)(2,1)}), bf16[768,2,9,1]{2,1,3,0:T(2,128)(2,1)S(1)}, u32[]{:S(2)}, u32[]{:S(2)}) async-start(bf16[768,2,9,1]{2,1,3,0:T(2,128)(2,1)} %copy.32), calls=%async_computation.1 | async-start | bytes 786432 | tf_op jit(solution)/shard_map/all_to_all | solution.py:131
  829.5 19.8 %all-to-all-done.1 = bf16[768,2,9,1]{2,1,3,0:T(2,128)(2,1)S(1)} async-done(((bf16[768,2,9,1]{2,1,3,0:T(2,128)(2,1)}), bf16[768,2,9,1]{2,1,3,0:T(2,128)(2,1)S(1)}, u32[]{:S(2)}, u32[]{:S(2)}) %all-to-all-start.1) | async-done | bytes 27680 | tf_op jit(solution)/shard_map/all_to_all | solution.py:131
  849.7 1.3 fusion.340
  851.0 33.5 %reduce-scatter.2.cloned.1.call-done = f32[1,2,9,768]{3,2,1,0:T(8,128)} async-done(((f32[8,2,9,768]{3,2,1,0:T(8,128)}), f32[1,2,9,768]{3,2,1,0:T(8,128)}) %reduce-scatter.2.cloned.1.call-update) | async-done | bytes 55312 | tf_op jit(solution)/shard_map/reduce_scatter | solution.py:139
  884.5 1.6 copy.67
  (1162 shorter events, 90.5 us)
Async XLA Ops:
  7.5 667.8 %collective-permute-start.1 = (bf16[9,4,384]{2,1,0:T(4,128)(2,1)S(1)}, bf16[9,4,384]{2,1,0:T(4,128)(2,1)S(1)}, u32[]{:S(2)}, u32[]{:S(2)}) collective-permute-start(bf16[9,4,384]{2,1,0:T(4,128)(2,1)S(1)} %get-tuple-element.574), channel_id=1, source_target_pairs={{8,0},{16,8},{24,16},{32,24},{40,32},{48,40},{56,48},{64,56},{72,6... | collective-permute-start | bytes 82952 | tf_op jit(solution)/shard_map/ppermute | solution.py:23
  25.5 649.8 %collective-permute-start = (bf16[9,4,384]{2,1,0:T(4,128)(2,1)S(1)}, bf16[9,4,384]{2,1,0:T(4,128)(2,1)S(1)}, u32[]{:S(2)}, u32[]{:S(2)}) collective-permute-start(bf16[9,4,384]{2,1,0:T(4,128)(2,1)S(1)} %get-tuple-element.573), channel_id=1, source_target_pairs={{0,8},{8,16},{16,24},{24,32},{32,40},{40,48},{48,56},{56,64},{64,7... | collective-permute-start | bytes 82952 | tf_op jit(solution)/shard_map/ppermute | solution.py:21
  27.4 546.5 %copy-start.22 = (s32[8,384]{1,0:T(8,128)S(1)}, s32[8,384]{1,0:T(8,128)}, u32[]{:S(2)}) copy-start(s32[8,384]{1,0:T(8,128)} %param.9) | copy-start | bytes 36868
  28.8 545.4 %copy-start = (s32[768]{0:T(1024)S(1)}, s32[768]{0:T(1024)}, u32[]{:S(2)}) copy-start(s32[768]{0:T(1024)} %param.13) | copy-start | bytes 9220
  31.2 543.4 %copy-start.20 = (f32[8,384]{1,0:T(8,128)S(1)}, f32[8,384]{1,0:T(8,128)}, u32[]{:S(2)}) copy-start(f32[8,384]{1,0:T(8,128)} %param.11) | copy-start | bytes 36868
  31.2 543.4 %copy-start.21 = (f32[8,384]{1,0:T(8,128)S(1)}, f32[8,384]{1,0:T(8,128)}, u32[]{:S(2)}) copy-start(f32[8,384]{1,0:T(8,128)} %param.10) | copy-start | bytes 36868
  574.6 100.7 %copy-start.2 = (bf16[9,8,384]{2,1,0:T(8,128)(2,1)S(1)}, bf16[9,8,384]{2,1,0:T(8,128)(2,1)}, u32[]{:S(2)}) copy-start(bf16[9,8,384]{2,1,0:T(8,128)(2,1)} %param.8) | copy-start | bytes 165892
  574.6 103.1 %copy-start.25 = (s32[8]{0:T(128)S(1)}, s32[8]{0:T(128)}, u32[]{:S(2)}) copy-start(s32[8]{0:T(128)} %param.12) | copy-start | bytes 100
  675.4 3.7 collective-permute-start.3
  676.4 2.7 collective-permute-start.2
  731.5 80.4 %all-to-all-start = ((bf16[9,8,384]{2,0,1:T(8,128)(2,1)}), bf16[9,8,384]{2,0,1:T(8,128)(2,1)}, u32[]{:S(2)}, u32[]{:S(2)}) async-start(bf16[9,8,384]{2,0,1:T(8,128)(2,1)} %fusion.404), calls=%async_computation | async-start | bytes 196608 | tf_op jit(solution)/shard_map/all_to_all | solution.py:122
  740.4 6.8 copy-start.9
  745.9 17.8 %copy-start.11 = (f32[768]{0:T(1024)S(1)}, f32[768]{0:T(1024)}, u32[]{:S(2)}) copy-start(f32[768]{0:T(1024)} %get-tuple-element.600) | copy-start | bytes 9220
  745.9 18.9 %copy-start.10 = (f32[768]{0:T(1024)S(1)}, f32[768]{0:T(1024)}, u32[]{:S(2)}) copy-start(f32[768]{0:T(1024)} %get-tuple-element.599) | copy-start | bytes 9220
  745.9 19.9 %copy-start.19 = (f32[768]{0:T(1024)S(1)}, f32[768]{0:T(1024)}, u32[]{:S(2)}) copy-start(f32[768]{0:T(1024)} %get-tuple-element.619) | copy-start | bytes 9220
  745.9 20.9 %copy-start.18 = (f32[768]{0:T(1024)S(1)}, f32[768]{0:T(1024)}, u32[]{:S(2)}) copy-start(f32[768]{0:T(1024)} %get-tuple-element.620) | copy-start | bytes 9220
  745.9 22.0 %copy-start.17 = (f32[768]{0:T(1024)S(1)}, f32[768]{0:T(1024)}, u32[]{:S(2)}) copy-start(f32[768]{0:T(1024)} %get-tuple-element.617) | copy-start | bytes 9220
  745.9 23.0 %copy-start.16 = (f32[768]{0:T(1024)S(1)}, f32[768]{0:T(1024)}, u32[]{:S(2)}) copy-start(f32[768]{0:T(1024)} %get-tuple-element.618) | copy-start | bytes 9220
  745.9 24.0 %copy-start.15 = (f32[768]{0:T(1024)S(1)}, f32[768]{0:T(1024)}, u32[]{:S(2)}) copy-start(f32[768]{0:T(1024)} %get-tuple-element.615) | copy-start | bytes 9220
  745.9 25.0 %copy-start.14 = (f32[768]{0:T(1024)S(1)}, f32[768]{0:T(1024)}, u32[]{:S(2)}) copy-start(f32[768]{0:T(1024)} %get-tuple-element.616) | copy-start | bytes 9220
  745.9 26.0 %copy-start.13 = (f32[768]{0:T(1024)S(1)}, f32[768]{0:T(1024)}, u32[]{:S(2)}) copy-start(f32[768]{0:T(1024)} %get-tuple-element.592) | copy-start | bytes 9220
  745.9 27.1 %copy-start.12 = (f32[768]{0:T(1024)S(1)}, f32[768]{0:T(1024)}, u32[]{:S(2)}) copy-start(f32[768]{0:T(1024)} %get-tuple-element.591) | copy-start | bytes 9220
  745.9 28.1 %copy-start.8 = (f32[768]{0:T(1024)S(1)}, f32[768]{0:T(1024)}, u32[]{:S(2)}) copy-start(f32[768]{0:T(1024)} %get-tuple-element.613) | copy-start | bytes 9220
  745.9 29.1 %copy-start.7 = (f32[768]{0:T(1024)S(1)}, f32[768]{0:T(1024)}, u32[]{:S(2)}) copy-start(f32[768]{0:T(1024)} %get-tuple-element.614) | copy-start | bytes 9220
  745.9 30.1 %copy-start.6 = (f32[768]{0:T(1024)S(1)}, f32[768]{0:T(1024)}, u32[]{:S(2)}) copy-start(f32[768]{0:T(1024)} %get-tuple-element.611) | copy-start | bytes 9220
  746.2 30.9 %copy-start.5 = (f32[768]{0:T(1024)S(1)}, f32[768]{0:T(1024)}, u32[]{:S(2)}) copy-start(f32[768]{0:T(1024)} %get-tuple-element.612) | copy-start | bytes 9220
  747.2 30.9 %copy-start.4 = (f32[768]{0:T(1024)S(1)}, f32[768]{0:T(1024)}, u32[]{:S(2)}) copy-start(f32[768]{0:T(1024)} %get-tuple-element.584) | copy-start | bytes 9220
  748.2 30.9 %copy-start.3 = (f32[768]{0:T(1024)S(1)}, f32[768]{0:T(1024)}, u32[]{:S(2)}) copy-start(f32[768]{0:T(1024)} %get-tuple-element.581) | copy-start | bytes 9220
  783.4 19.1 %copy-start.1 = (f32[1,8,96]{0,2,1:T(8,128)S(1)}, f32[1,8,96]{0,2,1:T(8,128)}, u32[]{:S(2)}) copy-start(f32[1,8,96]{0,2,1:T(8,128)} %add_exponential_fusion) | copy-start | bytes 9220
  802.4 10.5 %copy-start.23 = (pred[768]{0:T(1024)(128)(4,1)S(1)}, pred[768]{0:T(1024)(128)(4,1)}, u32[]{:S(2)}) copy-start(pred[768]{0:T(1024)(128)(4,1)} %broadcast_compare_fusion) | copy-start | bytes 2308
  812.9 36.7 %copy-start.24 = (s32[8]{0:T(128)S(1)}, s32[8]{0:T(128)}, u32[]{:S(2)}) copy-start(s32[8]{0:T(128)} %get-tuple-element.662) | copy-start | bytes 100
  820.3 28.9 %all-to-all-start.1 = ((bf16[768,2,9,1]{2,1,3,0:T(2,128)(2,1)}), bf16[768,2,9,1]{2,1,3,0:T(2,128)(2,1)S(1)}, u32[]{:S(2)}, u32[]{:S(2)}) async-start(bf16[768,2,9,1]{2,1,3,0:T(2,128)(2,1)} %copy.32), calls=%async_computation.1 | async-start | bytes 786432 | tf_op jit(solution)/shard_map/all_to_all | solution.py:131
  829.4 55.2 %reduce-scatter.2.cloned.1.call-start = ((), (), s32[]{:S(2)}) async-start(), calls=%async_computation.3 | async-start | bytes 884736 | tf_op jit(solution)/shard_map/reduce_scatter | solution.py:139
Sparse Core Ops, SparseCore 0:
  851.1 33.3 reduce-scatter.1
where the time goes:
time: 901 us; the launch traced here: 893 us
  other arithmetic  582 us (65%)
  local copies, waits for them, and re-layouts  190 us (21%)
  waiting for transfers between devices  54.1 us (6%)
  starting transfers between devices  38.8 us (4%)
  between operations  14 us (2%)
    mul x97, other arithmetic, advance(): result = fresh * jnp.exp(log_scale + log_start)  497 us
    convert_element_type x1, other arithmetic, fourier_table(): return (jnp.cos(angles) * (1.0 / math.sqrt(points))).astype(jnp.bfloat16)  76.1 us
    concatenate x34, local copies, waits for them, and re-layouts, legendre_rows(): values = jnp.concatenate([jnp.exp(log_start)[None, :], later], axis=0)  52.3 us
    gather x2, local copies, waits for them, and re-layouts, shards(): jnp.take(flat_field, corners, axis=1)  47 us
    slice x48, local copies, waits for them, and re-layouts, legendre_rows(): _, later = lax.scan(advance, initial, indices, unroll=unroll)  34.6 us
    reduce_scatter x1, waiting for transfers between devices, shards(): lax.psum_scatter(jnp.einsum('sacr,ksr->sack', slab_data, functions, prefe...  33.5 us
    all_to_all x1, waiting for transfers between devices, shards(): lax.all_to_all(masked, 'lat', split_axis=0, concat_axis=3, tiled=True)  19.8 us
    convert_element_type x1, local copies, waits for them, and re-layouts, fourier_table(): return (jnp.cos(angles) * (1.0 / math.sqrt(points))).astype(jnp.bfloat16)  19 us
  transfers between devices with their start and end apart: 7, of which 3 were waited for; matrix products, arithmetic and copies ran while one was open for 80% of the time, Pallas kernels for 0%

commit v1 on v0

v1 whole, which is shorter than its diff:
```python
import functools
import math

import jax
import jax.numpy as jnp
from jax import lax
from jax.experimental import pallas as pl
from jax.experimental.pallas import tpu as pltpu
from jax.sharding import PartitionSpec as P

HALO = 4
LANES = 128
BLOCK = 32
LGAMMA_HALF_THREE = 0.5 * math.log(math.pi) - math.log(2.0)
SINE = (
    3.1415926535897932,
    -5.1677127800499700,
    2.5501640398773455,
    -0.59926452932079211,
    0.082145886611128233,
    -0.0073704309457143504,
)


def fourier_kernel(waves, out, *, points):
    wave = waves[...].astype(jnp.float32)
    rows = wave.shape[0]
    turn = (lax.broadcasted_iota(jnp.int32, (rows, LANES), 0) % 2 * (points // 4)).astype(
        jnp.float32
    )
    lane = lax.broadcasted_iota(jnp.int32, (rows, LANES), 1)
    scale = 1.0 / math.sqrt(points)

    def tile(t, carry):
        column = (lane + t * LANES).astype(jnp.float32)
        phase = column * wave + turn
        phase = phase - jnp.floor(phase * (1.0 / points) + 0.5) * float(points)
        z = 0.5 - jnp.abs(phase) * (2.0 / points)
        square = z * z
        total = jnp.full_like(z, SINE[-1] * scale)
        for factor in SINE[-2::-1]:
            total = total * square + factor * scale
        start = pl.multiple_of(t * LANES, LANES)
        out[:, pl.ds(start, LANES)] = (total * z).astype(jnp.bfloat16)
        return carry

    lax.fori_loop(0, points // LANES, tile, 0)


def legendre_kernel(step_a, step_c, cosine, log_start, weight, out, stage, *, waves, band_rows):
    cos = cosine[...]
    start = log_start[...]
    scale = weight[...]

    def block(t, carry):
        current, last, log_scale = carry
        base = t * BLOCK
        size = jnp.exp(log_scale + start) * scale
        for u in range(BLOCK):
            stage[band_rows * u : band_rows * (u + 1), :] = current * size
            fresh = (step_a[base + u] * cos) * current - step_c[base + u] * last
            last = current
            current = fresh
        row = pl.multiple_of(base, BLOCK)
        for r in range(band_rows):
            out[pl.ds(row, BLOCK), r * LANES : (r + 1) * LANES] = stage[
                pl.ds(r, BLOCK, stride=band_rows), :
            ].astype(jnp.bfloat16)
        factor = jnp.maximum(jnp.maximum(jnp.abs(current), jnp.abs(last)), 1.0)
        inverse = 1.0 / factor
        return current * inverse, last * inverse, log_scale + jnp.log(factor)

    initial = (jnp.ones_like(cos), jnp.zeros_like(cos), jnp.zeros_like(cos))
    lax.fori_loop(0, waves // BLOCK, block, initial)


def arrival_kernel(
    field, north, south, west, east, departure, lat_weight, lon_weight, out, grid, shifted
):
    channels, rows, cols = field.shape
    tiles = cols // LANES
    copies = out.shape[0]
    stencil = 2 * HALO
    row_place = departure[...] // stencil
    col_place = departure[...] % stencil
    a = lat_weight[...]
    b = lon_weight[...]

    def spread(place, share):
        return [
            jnp.where(place == d, 1.0 - share, jnp.where(place == d - 1, share, 0.0))
            for d in range(stencil + 1)
        ]

    row_parts = spread(row_place, a)
    col_parts = spread(col_place, b)
    lane = lax.broadcasted_iota(jnp.int32, (rows + 2 * HALO, LANES), 1)
    for c in range(channels):
        grid[c, 0] = west[c].astype(jnp.float32)
        grid[c, tiles + 1] = east[c].astype(jnp.float32)
        up = north[c].astype(jnp.float32)
        mid = field[c].astype(jnp.float32)
        down = south[c].astype(jnp.float32)
        for t in range(tiles):
            span = slice(t * LANES, (t + 1) * LANES)
            grid[c, t + 1, 0:HALO, :] = up[:, span]
            grid[c, t + 1, HALO : HALO + rows, :] = mid[:, span]
            grid[c, t + 1, HALO + rows :, :] = down[:, span]

    def channel(c, carry):
        source = [grid[c, t] for t in range(tiles + 2)]
        for d in range(stencil + 1):
            move = d - HALO
            if move == 0:
                for t in range(tiles):
                    shifted[d, t] = source[t + 1]
                continue
            if move > 0:
                turned = [pltpu.roll(source[t], LANES - move, 1) for t in range(1, tiles + 2)]
                for t in range(tiles):
                    shifted[d, t] = jnp.where(lane < LANES - move, turned[t], turned[t + 1])
            else:
                turned = [pltpu.roll(source[t], -move, 1) for t in range(tiles + 1)]
                for t in range(tiles):
                    shifted[d, t] = jnp.where(lane < -move, turned[t], turned[t + 1])
        for t in range(tiles):
            span = slice(t * LANES, (t + 1) * LANES)
            total = None
            for e in range(stencil + 1):
                inner = None
                for d in range(stencil + 1):
                    term = col_parts[d][:, span] * shifted[d, t, e : e + rows, :]
                    inner = term if inner is None else inner + term
                term = row_parts[e][:, span] * inner
                total = term if total is None else total + term
            value = total.astype(jnp.bfloat16)
            for copy in range(copies):
                out[copy, c, :, span] = value
        return carry

    lax.fori_loop(0, channels, channel, 0)


def transform_kernel(cycles, fourier, waves, limits, out, gathered):
    sectors, channels, rows, cols = cycles.shape
    used = channels * rows
    gathered[used:, :] = jnp.zeros_like(gathered[used:, :])
    for sector in range(sectors):
        for c in range(channels):
            gathered[c * rows : (c + 1) * rows, sector * cols : (sector + 1) * cols] = cycles[
                sector, c
            ].astype(jnp.float32)
    spectrum = lax.dot_general(
        fourier[...],
        gathered[...].astype(jnp.bfloat16),
        (((1,), (1,)), ((), ())),
        preferred_element_type=jnp.float32,
    )
    out[...] = jnp.where(waves[...] < limits[...], spectrum, 0.0).astype(jnp.bfloat16)


def synthesis_kernel(order, data, functions, out, rows, turned, packed):
    channels, parts, waves = out.shape
    bands = data.shape[0] // parts
    band_rows = packed.shape[1] // LANES
    rows[parts * bands :, :] = jnp.zeros_like(rows[parts * bands :, :])
    rows[: parts * bands, :] = data[...].astype(jnp.float32)
    packed[...] = jnp.zeros_like(packed)
    step = packed.shape[0] // parts
    for e in range(parts):
        turned[e] = rows[pl.ds(e, LANES, stride=parts), :].T
        for r in range(band_rows):
            packed[e * step : e * step + channels, r * LANES : (r + 1) * LANES] = turned[
                e, pl.ds(r, channels, stride=band_rows), :
            ]
    result = lax.dot_general(
        packed[...].astype(jnp.bfloat16),
        functions[...],
        (((1,), (1,)), ((), ())),
        preferred_element_type=jnp.float32,
    )
    index = lax.broadcasted_iota(jnp.int32, (channels, waves), 1)
    inside = index < waves - order[0]
    for e in range(parts):
        out[:, e, :] = jnp.where(inside, result[e * step : e * step + channels, :], 0.0)


def legendre_inputs(order, bands, band_rows, waves, total_lat):
    spread = lax.optimization_barrier(jnp.broadcast_to(order, (band_rows, LANES)))
    order_real = spread.astype(jnp.float32)
    band = jnp.minimum(lax.broadcasted_iota(jnp.int32, (band_rows, LANES), 1), bands - 1)
    cycle = band * band_rows + lax.broadcasted_iota(jnp.int32, (band_rows, LANES), 0)
    angles = (cycle.astype(jnp.float32) + 0.5) * (math.pi / total_lat)
    sine = jnp.sin(angles)
    log_start = (
        0.5 * math.log(0.5)
        + 0.5 * (lax.lgamma(order_real + 1.5) - LGAMMA_HALF_THREE - lax.lgamma(order_real + 1.0))
        + order_real * jnp.log(sine)
    )
    order_real = order.astype(jnp.float32)
    degree = order_real + jnp.arange(1, waves + 1, dtype=jnp.int32).astype(jnp.float32)
    step_a = jnp.sqrt((4.0 * degree * degree - 1.0) / (degree * degree - order_real * order_real))
    before = degree - 1.0
    step_b = jnp.sqrt(
        jnp.maximum(
            (before * before - order_real * order_real) / (4.0 * before * before - 1.0), 0.0
        )
    )
    return (
        step_a,
        step_a * step_b,
        jnp.cos(angles),
        log_start,
        sine * (math.pi / math.sqrt(total_lat)),
    )


def smem():
    return pl.BlockSpec(memory_space=pltpu.SMEM)


def vmem():
    return pl.BlockSpec(memory_space=pltpu.VMEM)


def fourier_table(row_waves, points):
    return pl.pallas_call(
        functools.partial(fourier_kernel, points=points),
        out_shape=jax.ShapeDtypeStruct((row_waves.shape[0], points), jnp.bfloat16),
        in_specs=[vmem()],
        out_specs=vmem(),
        name="fourier",
    )(row_waves)


def legendre_table(order, bands, band_rows, waves):
    return pl.pallas_call(
        functools.partial(legendre_kernel, waves=waves, band_rows=band_rows),
        out_shape=jax.ShapeDtypeStruct((waves, band_rows * LANES), jnp.bfloat16),
        in_specs=[smem(), smem(), vmem(), vmem(), vmem()],
        out_specs=vmem(),
        scratch_shapes=[pltpu.VMEM((BLOCK * band_rows, LANES), jnp.float32)],
        name="legendre",
    )(*legendre_inputs(order, bands, band_rows, waves, bands * band_rows))


def interpolate(prognostic, north, south, west, east, departure, lat_weight, lon_weight, copies):
    channels, band_rows, sector_cols = prognostic.shape
    tall = band_rows + 2 * HALO
    tiles = sector_cols // LANES
    return pl.pallas_call(
        arrival_kernel,
        out_shape=jax.ShapeDtypeStruct((copies, channels, band_rows, sector_cols), jnp.bfloat16),
        in_specs=[vmem()] * 8,
        out_specs=vmem(),
        scratch_shapes=[
            pltpu.VMEM((channels, tiles + 2, tall, LANES), jnp.float32),
            pltpu.VMEM((2 * HALO + 1, tiles, tall, LANES), jnp.float32),
        ],
        name="arrival",
    )(prognostic, north, south, west, east, departure, lat_weight, lon_weight)


def transform(cycles, fourier, row_waves, limits):
    rows, points = fourier.shape
    return pl.pallas_call(
        transform_kernel,
        out_shape=jax.ShapeDtypeStruct((rows, LANES), jnp.bfloat16),
        in_specs=[vmem()] * 4,
        out_specs=vmem(),
        scratch_shapes=[pltpu.VMEM((LANES, points), jnp.float32)],
        name="transform",
    )(cycles, fourier, row_waves, limits)


def synthesize(order, data, functions, channels):
    waves, span = functions.shape
    return pl.pallas_call(
        synthesis_kernel,
        out_shape=jax.ShapeDtypeStruct((channels, 2, waves), jnp.float32),
        in_specs=[smem(), vmem(), vmem()],
        out_specs=vmem(),
        scratch_shapes=[
            pltpu.VMEM((2 * LANES, LANES), jnp.float32),
            pltpu.VMEM((2, LANES, LANES), jnp.float32),
            pltpu.VMEM((32, span), jnp.float32),
        ],
        name="synthesis",
    )(order, data, functions)


def shards(prognostic, departure, lat_weight, lon_weight, cycle_waves, wave_order):
    band_rows = prognostic.shape[1]
    bands = lax.axis_size("lat")
    sectors = lax.axis_size("lon")
    total_lon = prognostic.shape[2] * sectors
    waves = wave_order.shape[0]
    band_index = lax.axis_index("lat")
    sector_index = lax.axis_index("lon")

    north = lax.ppermute(
        prognostic[:, band_rows - HALO :, :], "lat", [(i, i + 1) for i in range(bands - 1)]
    )
    south = lax.ppermute(prognostic[:, :HALO, :], "lat", [(i + 1, i) for i in range(bands - 1)])

    slot_waves = wave_order.reshape(bands, sectors)
    own_waves = lax.dynamic_slice_in_dim(slot_waves, sector_index, 1, axis=1)
    row_waves = jnp.broadcast_to(own_waves[:, :, None], (bands, 2, LANES)).reshape(
        2 * bands, LANES
    )
    order = lax.dynamic_slice_in_dim(wave_order, band_index * sectors + sector_index, 1)
    limits = jnp.broadcast_to(
        cycle_waves[None, None, :], (1, LANES // band_rows, band_rows)
    ).reshape(1, LANES)
    fourier = fourier_table(row_waves, total_lon)
    functions = legendre_table(order, bands, band_rows, waves)

    tall_west = jnp.concatenate(
        [north[:, :, -LANES:], prognostic[:, :, -LANES:], south[:, :, -LANES:]], axis=1
    )
    tall_east = jnp.concatenate(
        [north[:, :, :LANES], prognostic[:, :, :LANES], south[:, :, :LANES]], axis=1
    )
    west = lax.ppermute(tall_west, "lon", [(i, (i + 1) % sectors) for i in range(sectors)])
    east = lax.ppermute(tall_east, "lon", [((i + 1) % sectors, i) for i in range(sectors)])
    arrival = interpolate(
        prognostic, north, south, west, east, departure, lat_weight, lon_weight, sectors
    )
    cycles = lax.all_to_all(arrival, "lon", split_axis=0, concat_axis=0, tiled=True)
    masked = transform(cycles, fourier, row_waves, limits)
    data = lax.all_to_all(
        masked.reshape(bands, 2, LANES), "lat", split_axis=0, concat_axis=0, tiled=True
    ).reshape(2 * bands, LANES)
    spectral = synthesize(order, data, functions, prognostic.shape[0])
    return spectral.transpose(1, 0, 2)[None]


def solution(mesh):
    in_specs = (
        P(None, "lat", "lon"),
        P("lat", "lon"),
        P("lat", "lon"),
        P("lat", "lon"),
        P("lat"),
        P(),
    )
    out_specs = P(("lat", "lon"), None, None, None)
    return jax.shard_map(shards, mesh=mesh, in_specs=in_specs, out_specs=out_specs, check_vma=False)
```

time: 901 us -> 76.6 us (0.09)
  other arithmetic: 582 us -> 1.35 us
  local copies, waits for them, and re-layouts: 190 us -> 7.09 us
  waiting for transfers between devices: 54.1 us -> 12.2 us
  Pallas kernels: 0 us -> 17.5 us
  between operations: 14 us -> 0.68 us
    mul x100 -> x2, other arithmetic: 501 us -> 0.69 us  [the longest x1 0.68 us: legendre_inputs(): sine * (math.pi / math.sqrt(total_lat))]
    convert_element_type x5 -> x0, other arithmetic: 76.9 us -> none  [the longest x1 76.1 us: fourier_table(): return (jnp.cos(angles) * (1.0 / math.sqrt(points))).astype(jnp.bfloat16)]
    concatenate x58 -> x0, local copies, waits for them, and re-layouts: 57.9 us -> none  [the longest x34 52.3 us: legendre_rows(): values = jnp.concatenate([jnp.exp(log_start)[None, :], later], axis=0)]
    gather x3 -> x0, local copies, waits for them, and re-layouts: 48.3 us -> none  [the longest x2 47 us: shards(): jnp.take(flat_field, corners, axis=1)]
    slice x49 -> x4, local copies, waits for them, and re-layouts: 35.5 us -> 1.68 us  [the longest x1 0.91 us: shards(): prognostic[:, :HALO, :]]
    reduce_scatter x1 -> x0, waiting for transfers between devices: 33.5 us -> none  [shards(): lax.psum_scatter(jnp.einsum('sacr,ksr->sack', slab_data, functions, prefe...]
    convert_element_type x26 -> x0, local copies, waits for them, and re-layouts: 21.9 us -> none  [the longest x1 19 us: fourier_table(): return (jnp.cos(angles) * (1.0 / math.sqrt(points))).astype(jnp.bfloat16)]
    pallas_call x0 -> x5, Pallas kernels: none -> 17.5 us  [the longest x1 4.38 us: legendre_table(): pl.pallas_call(functools.partial(legendre_kernel, waves=waves, band_rows=...]
  transfers between devices with their start and end apart: 7 -> 6, of which waited for: 3 -> 5; matrix products, arithmetic and copies ran while one was open for 80% -> 7% of each run, Pallas kernels for 0% -> 11%
where the time goes in v1:
time: 76.6 us; the launch traced here: 76 us
  starting transfers between devices  37.2 us (49%)
  Pallas kernels  17.5 us (23%)
  waiting for transfers between devices  12.2 us (16%)
  local copies, waits for them, and re-layouts  7.09 us (9%)
  other arithmetic  1.35 us (2%)
    all_to_all x1, starting transfers between devices, shards(): lax.all_to_all(masked.reshape(bands, 2, LANES), 'lat', split_axis=0, conc...  16 us
    all_to_all x1, starting transfers between devices, shards(): lax.all_to_all(arrival, 'lon', split_axis=0, concat_axis=0, tiled=True)  7.56 us
    all_to_all x1, waiting for transfers between devices, shards(): lax.all_to_all(masked.reshape(bands, 2, LANES), 'lat', split_axis=0, conc...  6.78 us
    ppermute x1, starting transfers between devices, shards(): lax.ppermute(prognostic[:, band_rows - HALO:, :], 'lat', [(i, i + 1) for...  4.82 us
    ppermute x1, starting transfers between devices, shards(): lax.ppermute(tall_east, 'lon', [((i + 1) % sectors, i) for i in range(sec...  4.57 us
    pallas_call x1, Pallas kernels, legendre_table(): pl.pallas_call(functools.partial(legendre_kernel, waves=waves, band_rows=...  4.38 us
    pallas_call x1, Pallas kernels, fourier_table(): pl.pallas_call(functools.partial(fourier_kernel, points=points), out_shap...  4.06 us
    pallas_call x1, Pallas kernels, interpolate(): pl.pallas_call(arrival_kernel, out_shape=jax.ShapeDtypeStruct((copies, ch...  3.34 us
  transfers between devices with their start and end apart: 6, of which 5 were waited for; matrix products, arithmetic and copies ran while one was open for 7% of the time, Pallas kernels for 11%

profile of v1, /device:TPU:1, one launch (start us, length us, event | category | flops | bytes accessed | tf_op | source)
XLA Modules:
  0.0 76.0 jit_solution(5085183510125989999)
XLA Ops:
  0.0 0.0 copy-start.6
  0.0 0.9 %fusion.22 = (bf16[9,4,384]{2,1,0:T(4,128)(2,1)S(1)}, bf16[9,4,384]{2,1,0:T(4,128)(2,1)S(1)}) fusion(bf16[9,8,384]{2,1,0:T(8,128)(2,1)} %field.1), kind=kLoop, calls=%fused_computation.37 | loop fusion | bytes 110592 | tf_op jit(solution)/shard_map/slice | solution.py:304
  0.9 4.8 %collective-permute-start = (bf16[9,4,384]{2,1,0:T(4,128)(2,1)S(1)}, bf16[9,4,384]{2,1,0:T(4,128)(2,1)S(1)}, u32[]{:S(2)}, u32[]{:S(2)}) collective-permute-start(bf16[9,4,384]{2,1,0:T(4,128)(2,1)S(1)} %get-tuple-element.8), channel_id=1, source_target_pairs={{0,8},{8,16},{16,24},{24,32},{32,40},{40,48},{48,56},{56,64},{64,7... | collective-permute-start | bytes 82952 | tf_op jit(solution)/shard_map/ppermute | solution.py:301
  5.7 1.3 %collective-permute-start.1 = (bf16[9,4,384]{2,1,0:T(4,128)(2,1)S(1)}, bf16[9,4,384]{2,1,0:T(4,128)(2,1)S(1)}, u32[]{:S(2)}, u32[]{:S(2)}) collective-permute-start(bf16[9,4,384]{2,1,0:T(4,128)(2,1)S(1)} %get-tuple-element.7), channel_id=1, source_target_pairs={{8,0},{16,8},{24,16},{32,24},{40,32},{48,40},{56,48},{64,56},{72,6... | collective-permute-start | bytes 82952 | tf_op jit(solution)/shard_map/ppermute | solution.py:304
  7.0 0.7 fusion.21
  7.8 3.2 %collective-permute-done.1.south = bf16[9,4,384]{2,1,0:T(4,128)(2,1)S(1)} collective-permute-done((bf16[9,4,384]{2,1,0:T(4,128)(2,1)S(1)}, bf16[9,4,384]{2,1,0:T(4,128)(2,1)S(1)}, u32[]{:S(2)}, u32[]{:S(2)}) %collective-permute-start.1) | collective-permute-done | bytes 27680 | tf_op jit(solution)/shard_map/ppermute | solution.py:304
  11.0 0.0 copy-start.3
  11.0 0.0 collective-permute-done.north
  11.0 0.0 copy-start.2
  11.1 2.9 %collective-permute-start.2 = (bf16[9,16,128]{2,1,0:T(8,128)(2,1)S(1)}, bf16[9,16,128]{2,1,0:T(8,128)(2,1)S(1)}, u32[]{:S(2)}, u32[]{:S(2)}) collective-permute-start(bf16[9,16,128]{2,1,0:T(8,128)(2,1)S(1)} %pad_maximum_fusion), channel_id=1, source_target_pairs={{0,1},{1,2},{2,3},{3,4},{4,5},{5,6},{6,7},{7,0},{8,9},{9,10},{10,1... | collective-permute-start | bytes 110600 | tf_op jit(solution)/shard_map/ppermute | solution.py:324
  14.0 0.0 copy-start.7
  14.0 4.6 %collective-permute-start.3 = (bf16[9,16,128]{2,1,0:T(8,128)(2,1)S(1)}, bf16[9,16,128]{2,1,0:T(8,128)(2,1)S(1)}, u32[]{:S(2)}, u32[]{:S(2)}) collective-permute-start(bf16[9,16,128]{2,1,0:T(8,128)(2,1)S(1)} %pad_maximum_fusion.1), channel_id=1, source_target_pairs={{1,0},{2,1},{3,2},{4,3},{5,4},{6,5},{7,6},{0,7},{9,8},{10,9},{11,1... | collective-permute-start | bytes 110600 | tf_op jit(solution)/shard_map/ppermute | solution.py:325
  18.6 0.6 collective-permute-done.2.west
  19.3 0.0 copy-start.4
  19.3 0.2 collective-permute-done.3.east
  19.5 0.0 copy-done.3
  19.5 0.0 copy-done.2
  19.5 0.4 copy-done.4
  19.9 0.0 copy-start.5
  19.9 0.6 copy-done.5
  20.5 3.3 %arrival.1 = bf16[8,9,8,384]{3,2,1,0:T(8,128)(2,1)} custom-call(bf16[9,8,384]{2,1,0:T(8,128)(2,1)} %field.1, bf16[9,4,384]{2,1,0:T(4,128)(2,1)} %copy-done.2, bf16[9,4,384]{2,1,0:T(4,128)(2,1)} %copy-done.3, bf16[9,16,128]{2,1,0:T(8,128)(2,1)} %copy-done.4, bf16[9,16,128]{2,1,0:T(8,128)(2,1)} %copy-done.5, s32[8,384]{1,0:T(8,128)} %departure.1, ...), custom_call_target="tpu_custom_call" | custom-call | tf_op jit(solution)/shard_map/arrival/pallas_call | solution.py:251
  23.8 7.6 %all-to-all-start = ((bf16[8,9,8,384]{3,2,1,0:T(8,128)(2,1)}), bf16[8,9,8,384]{3,2,1,0:T(8,128)(2,1)S(1)}, u32[]{:S(2)}, u32[]{:S(2)}) async-start(bf16[8,9,8,384]{3,2,1,0:T(8,128)(2,1)} %arrival.1), calls=%async_computation | async-start | bytes 884736 | tf_op jit(solution)/shard_map/all_to_all | solution.py:329
  31.4 0.0 copy-done.6
  31.4 0.1 reshape.20
  31.5 0.6 dynamic_slice.8.order
  32.0 0.2 dynamic-slice_reduce_fusion
  32.2 0.1 broadcast_in_dim.29
  32.3 0.2 broadcast_in_dim.30
  32.4 0.7 broadcast_in_dim.31.waves
  33.2 4.1 %fourier.1 = bf16[192,3072]{1,0:T(8,128)(2,1)} custom-call(s32[192,128]{1,0:T(8,128)} %broadcast_in_dim.31.waves), custom_call_target="tpu_custom_call" | custom-call | tf_op jit(solution)/shard_map/fourier/pallas_call | solution.py:227
  37.3 0.0 copy-done.7
  37.3 0.7 broadcast_in_dim.33.limits
  37.9 0.5 broadcast_in_dim.34
  38.5 1.3 %all-to-all-done.cycles = bf16[8,9,8,384]{3,2,1,0:T(8,128)(2,1)S(1)} async-done(((bf16[8,9,8,384]{3,2,1,0:T(8,128)(2,1)}), bf16[8,9,8,384]{3,2,1,0:T(8,128)(2,1)S(1)}, u32[]{:S(2)}, u32[]{:S(2)}) %all-to-all-start) | async-done | bytes 442400 | tf_op jit(solution)/shard_map/all_to_all | solution.py:329
  39.9 0.0 copy-start
  39.9 0.8 %copy-done = bf16[8,9,8,384]{3,2,1,0:T(8,128)(2,1)} copy-done((bf16[8,9,8,384]{3,2,1,0:T(8,128)(2,1)}, bf16[8,9,8,384]{3,2,1,0:T(8,128)(2,1)S(1)}, u32[]{:S(2)}) %copy-start) | copy-done | bytes 442392
  40.6 2.5 %transform.1 = bf16[192,128]{1,0:T(8,128)(2,1)} custom-call(bf16[8,9,8,384]{3,2,1,0:T(8,128)(2,1)} %copy-done, bf16[192,3072]{1,0:T(8,128)(2,1)} %fourier.1, s32[192,128]{1,0:T(8,128)} %broadcast_in_dim.31.waves, s32[1,128]{1,0:T(1,128)} %broadcast_in_dim.33.limits), custom_call_target="tpu_custom_call" | custom-call | tf_op jit(solution)/shard_map/transform/pallas_call | solution.py:266
  43.1 16.0 %all-to-all-start.1 = ((bf16[96,2,128]{2,1,0:T(2,128)(2,1)}), bf16[96,2,128]{2,1,0:T(2,128)(2,1)S(1)}, u32[]{:S(2)}, u32[]{:S(2)}) async-start(bf16[96,2,128]{2,1,0:T(2,128)(2,1)} %bitcast.9), calls=%async_computation.1 | async-start | bytes 98304 | tf_op jit(solution)/shard_map/all_to_all | solution.py:331
  59.1 0.7 fusion.20
  60.4 0.6 fusion.2
  61.0 4.4 %legendre.1.functions = bf16[768,1024]{1,0:T(8,128)(2,1)} custom-call(f32[768]{0:T(1024)} %get-tuple-element.16.step_a, f32[768]{0:T(1024)} %get-tuple-element.17.step_c, f32[8,128]{1,0:T(8,128)} %get-tuple-element.15.cosine, f32[8,128]{1,0:T(8,128)} %get-tuple-element.14.log_start, f32[8,128]{1,0:T(8,128)} %get-tuple-element.13.weight), custom_call_target="tpu_custom_call" | custom-call | tf_op jit(solution)/shard_map/legendre/pallas_call | solution.py:237
  65.4 6.8 %all-to-all-done.1 = bf16[96,2,128]{2,1,0:T(2,128)(2,1)S(1)} async-done(((bf16[96,2,128]{2,1,0:T(2,128)(2,1)}), bf16[96,2,128]{2,1,0:T(2,128)(2,1)S(1)}, u32[]{:S(2)}, u32[]{:S(2)}) %all-to-all-start.1) | async-done | bytes 49184 | tf_op jit(solution)/shard_map/all_to_all | solution.py:331
  72.1 0.0 copy-start.1
  72.1 0.6 copy-done.1
  72.8 3.2 %synthesis.1 = f32[9,2,768]{2,1,0:T(2,128)} custom-call(s32[1]{0:T(128)} %dynamic_slice.8.order, bf16[192,128]{1,0:T(8,128)(2,1)} %bitcast.8, bf16[768,1024]{1,0:T(8,128)(2,1)} %legendre.1.functions), custom_call_target="tpu_custom_call" | custom-call | tf_op jit(solution)/shard_map/synthesis/pallas_call | solution.py:278
  (6 shorter events, 0.1 us)
Async XLA Ops:
  0.0 31.4 %copy-start.6 = (s32[768]{0:T(1024)S(1)}, s32[768]{0:T(1024)}, u32[]{:S(2)}) copy-start(s32[768]{0:T(1024)} %param.11) | copy-start | bytes 9220
  0.9 10.1 %collective-permute-start = (bf16[9,4,384]{2,1,0:T(4,128)(2,1)S(1)}, bf16[9,4,384]{2,1,0:T(4,128)(2,1)S(1)}, u32[]{:S(2)}, u32[]{:S(2)}) collective-permute-start(bf16[9,4,384]{2,1,0:T(4,128)(2,1)S(1)} %get-tuple-element.8), channel_id=1, source_target_pairs={{0,8},{8,16},{16,24},{24,32},{32,40},{40,48},{48,56},{56,64},{64,7... | collective-permute-start | bytes 82952 | tf_op jit(solution)/shard_map/ppermute | solution.py:301
  5.7 5.2 %collective-permute-start.1 = (bf16[9,4,384]{2,1,0:T(4,128)(2,1)S(1)}, bf16[9,4,384]{2,1,0:T(4,128)(2,1)S(1)}, u32[]{:S(2)}, u32[]{:S(2)}) collective-permute-start(bf16[9,4,384]{2,1,0:T(4,128)(2,1)S(1)} %get-tuple-element.7), channel_id=1, source_target_pairs={{8,0},{16,8},{24,16},{32,24},{40,32},{48,40},{56,48},{64,56},{72,6... | collective-permute-start | bytes 82952 | tf_op jit(solution)/shard_map/ppermute | solution.py:304
  11.0 8.5 %copy-start.3 = (bf16[9,4,384]{2,1,0:T(4,128)(2,1)}, bf16[9,4,384]{2,1,0:T(4,128)(2,1)S(1)}, u32[]{:S(2)}) copy-start(bf16[9,4,384]{2,1,0:T(4,128)(2,1)S(1)} %collective-permute-done.1.south) | copy-start | bytes 82948
  11.0 8.5 %copy-start.2 = (bf16[9,4,384]{2,1,0:T(4,128)(2,1)}, bf16[9,4,384]{2,1,0:T(4,128)(2,1)S(1)}, u32[]{:S(2)}) copy-start(bf16[9,4,384]{2,1,0:T(4,128)(2,1)S(1)} %collective-permute-done.north) | copy-start | bytes 82948
  11.1 8.2 %collective-permute-start.2 = (bf16[9,16,128]{2,1,0:T(8,128)(2,1)S(1)}, bf16[9,16,128]{2,1,0:T(8,128)(2,1)S(1)}, u32[]{:S(2)}, u32[]{:S(2)}) collective-permute-start(bf16[9,16,128]{2,1,0:T(8,128)(2,1)S(1)} %pad_maximum_fusion), channel_id=1, source_target_pairs={{0,1},{1,2},{2,3},{3,4},{4,5},{5,6},{6,7},{7,0},{8,9},{9,10},{10,1... | collective-permute-start | bytes 110600 | tf_op jit(solution)/shard_map/ppermute | solution.py:324
  14.0 23.2 %copy-start.7 = (s32[8]{0:T(128)S(1)}, s32[8]{0:T(128)}, u32[]{:S(2)}) copy-start(s32[8]{0:T(128)} %param.10) | copy-start | bytes 100
  14.0 5.4 %collective-permute-start.3 = (bf16[9,16,128]{2,1,0:T(8,128)(2,1)S(1)}, bf16[9,16,128]{2,1,0:T(8,128)(2,1)S(1)}, u32[]{:S(2)}, u32[]{:S(2)}) collective-permute-start(bf16[9,16,128]{2,1,0:T(8,128)(2,1)S(1)} %pad_maximum_fusion.1), channel_id=1, source_target_pairs={{1,0},{2,1},{3,2},{4,3},{5,4},{6,5},{7,6},{0,7},{9,8},{10,9},{11,1... | collective-permute-start | bytes 110600 | tf_op jit(solution)/shard_map/ppermute | solution.py:325
  19.3 0.6 copy-start.4
  19.9 0.6 copy-start.5
  23.8 16.0 %all-to-all-start = ((bf16[8,9,8,384]{3,2,1,0:T(8,128)(2,1)}), bf16[8,9,8,384]{3,2,1,0:T(8,128)(2,1)S(1)}, u32[]{:S(2)}, u32[]{:S(2)}) async-start(bf16[8,9,8,384]{3,2,1,0:T(8,128)(2,1)} %arrival.1), calls=%async_computation | async-start | bytes 884736 | tf_op jit(solution)/shard_map/all_to_all | solution.py:329
  39.9 0.8 %copy-start = (bf16[8,9,8,384]{3,2,1,0:T(8,128)(2,1)}, bf16[8,9,8,384]{3,2,1,0:T(8,128)(2,1)S(1)}, u32[]{:S(2)}) copy-start(bf16[8,9,8,384]{3,2,1,0:T(8,128)(2,1)S(1)} %all-to-all-done.cycles) | copy-start | bytes 1327108
  43.1 29.1 %all-to-all-start.1 = ((bf16[96,2,128]{2,1,0:T(2,128)(2,1)}), bf16[96,2,128]{2,1,0:T(2,128)(2,1)S(1)}, u32[]{:S(2)}, u32[]{:S(2)}) async-start(bf16[96,2,128]{2,1,0:T(2,128)(2,1)} %bitcast.9), calls=%async_computation.1 | async-start | bytes 98304 | tf_op jit(solution)/shard_map/all_to_all | solution.py:331
  72.1 0.6 copy-start.1

commit v2 on v1

--- a/solution.py
+++ b/solution.py
@@ -23,28 +23,39 @@
 
 
 def fourier_kernel(waves, out, *, points):
-    wave = waves[...].astype(jnp.float32)
-    rows = wave.shape[0]
-    turn = (lax.broadcasted_iota(jnp.int32, (rows, LANES), 0) % 2 * (points // 4)).astype(
-        jnp.float32
-    )
-    lane = lax.broadcasted_iota(jnp.int32, (rows, LANES), 1)
+    rows, group = waves.shape[0], 64
     scale = 1.0 / math.sqrt(points)
-
-    def tile(t, carry):
-        column = (lane + t * LANES).astype(jnp.float32)
-        phase = column * wave + turn
+    row = lax.broadcasted_iota(jnp.int32, (group, LANES), 0)
+    turn = (row % 2 * (points // 4)).astype(jnp.float32)
+    lane = lax.broadcasted_iota(jnp.int32, (group, LANES), 1).astype(jnp.float32)
+
+    def cosine(phase):
         phase = phase - jnp.floor(phase * (1.0 / points) + 0.5) * float(points)
         z = 0.5 - jnp.abs(phase) * (2.0 / points)
         square = z * z
-        total = jnp.full_like(z, SINE[-1] * scale)
+        total = jnp.full_like(z, SINE[-1])
         for factor in SINE[-2::-1]:
-            total = total * square + factor * scale
-        start = pl.multiple_of(t * LANES, LANES)
-        out[:, pl.ds(start, LANES)] = (total * z).astype(jnp.bfloat16)
+            total = total * square + factor
+        return total * z
+
+    def block(g, carry):
+        first = pl.multiple_of(g * group, group)
+        wave = waves[pl.ds(first, group), :].astype(jnp.float32)
+        phase = lane * wave + turn
+        real = cosine(phase) * scale
+        imag = cosine(phase - points / 4) * scale
+        ahead = wave * float(LANES)
+        turn_real = cosine(ahead)
+        turn_imag = cosine(ahead - points / 4)
+        for t in range(points // LANES):
+            out[pl.ds(first, group), t * LANES : (t + 1) * LANES] = real.astype(jnp.bfloat16)
+            real, imag = (
+                real * turn_real - imag * turn_imag,
+                imag * turn_real + real * turn_imag,
+            )
         return carry
 
-    lax.fori_loop(0, points // LANES, tile, 0)
+    lax.fori_loop(0, rows // group, block, 0)
 
 
 def legendre_kernel(step_a, step_c, cosine, log_start, weight, out, stage, *, waves, band_rows):
@@ -75,7 +86,7 @@
 
 
 def arrival_kernel(
-    field, north, south, west, east, departure, lat_weight, lon_weight, out, grid, shifted
+    field, north, south, west, east, departure, lat_weight, lon_weight, out, grid, shifted, stage
 ):
     channels, rows, cols = field.shape
     tiles = cols // LANES
@@ -96,11 +107,11 @@
     col_parts = spread(col_place, b)
     lane = lax.broadcasted_iota(jnp.int32, (rows + 2 * HALO, LANES), 1)
     for c in range(channels):
-        grid[c, 0] = west[c].astype(jnp.float32)
-        grid[c, tiles + 1] = east[c].astype(jnp.float32)
-        up = north[c].astype(jnp.float32)
+        grid[c, 0] = west[c].astype(jnp.float32)[rows - HALO : 2 * rows + HALO]
+        grid[c, tiles + 1] = east[c].astype(jnp.float32)[rows - HALO : 2 * rows + HALO]
+        up = north[c].astype(jnp.float32)[rows - HALO :]
         mid = field[c].astype(jnp.float32)
-        down = south[c].astype(jnp.float32)
+        down = south[c].astype(jnp.float32)[:HALO]
         for t in range(tiles):
             span = slice(t * LANES, (t + 1) * LANES)
             grid[c, t + 1, 0:HALO, :] = up[:, span]
@@ -133,30 +144,26 @@
                     inner = term if inner is None else inner + term
                 term = row_parts[e][:, span] * inner
                 total = term if total is None else total + term
-            value = total.astype(jnp.bfloat16)
-            for copy in range(copies):
-                out[copy, c, :, span] = value
+            stage[pl.ds(pl.multiple_of(c * rows, rows), rows), span] = total
         return carry
 
+    used = channels * rows
+    stage[used:, :] = jnp.zeros_like(stage[used:, :])
     lax.fori_loop(0, channels, channel, 0)
-
-
-def transform_kernel(cycles, fourier, waves, limits, out, gathered):
-    sectors, channels, rows, cols = cycles.shape
-    used = channels * rows
-    gathered[used:, :] = jnp.zeros_like(gathered[used:, :])
-    for sector in range(sectors):
-        for c in range(channels):
-            gathered[c * rows : (c + 1) * rows, sector * cols : (sector + 1) * cols] = cycles[
-                sector, c
-            ].astype(jnp.float32)
+    value = stage[...].astype(jnp.bfloat16)
+    for copy in range(copies):
+        out[copy] = value
+
+
+def transform_kernel(cycles, fourier, waves, limits, out):
+    sectors, used, _ = cycles.shape
+    gathered = jnp.concatenate([cycles[sector] for sector in range(sectors)], axis=1)
     spectrum = lax.dot_general(
-        fourier[...],
-        gathered[...].astype(jnp.bfloat16),
-        (((1,), (1,)), ((), ())),
-        preferred_element_type=jnp.float32,
-    )
-    out[...] = jnp.where(waves[...] < limits[...], spectrum, 0.0).astype(jnp.bfloat16)
+        fourier[...], gathered, (((1,), (1,)), ((), ())), preferred_element_type=jnp.float32
+    )
+    inside = waves[:, :used] < limits[:, :used]
+    out[:, :used] = jnp.where(inside, spectrum, 0.0).astype(jnp.bfloat16)
+    out[:, used:] = jnp.zeros((out.shape[0], out.shape[1] - used), jnp.bfloat16)
 
 
 def synthesis_kernel(order, data, functions, out, rows, turned, packed):
@@ -215,6 +222,10 @@
     )
 
 
+def near(array):
+    return pltpu.with_memory_space_constraint(array, pltpu.VMEM)
+
+
 def smem():
     return pl.BlockSpec(memory_space=pltpu.SMEM)
 
@@ -226,51 +237,52 @@
 def fourier_table(row_waves, points):
     return pl.pallas_call(
         functools.partial(fourier_kernel, points=points),
-        out_shape=jax.ShapeDtypeStruct((row_waves.shape[0], points), jnp.bfloat16),
+        out_shape=pltpu.VMEM((row_waves.shape[0], points), jnp.bfloat16),
         in_specs=[vmem()],
         out_specs=vmem(),
         name="fourier",
-    )(row_waves)
+    )(near(row_waves))
 
 
 def legendre_table(order, bands, band_rows, waves):
+    step_a, step_c, *planes = legendre_inputs(order, bands, band_rows, waves, bands * band_rows)
     return pl.pallas_call(
         functools.partial(legendre_kernel, waves=waves, band_rows=band_rows),
-        out_shape=jax.ShapeDtypeStruct((waves, band_rows * LANES), jnp.bfloat16),
+        out_shape=pltpu.VMEM((waves, band_rows * LANES), jnp.bfloat16),
         in_specs=[smem(), smem(), vmem(), vmem(), vmem()],
         out_specs=vmem(),
         scratch_shapes=[pltpu.VMEM((BLOCK * band_rows, LANES), jnp.float32)],
         name="legendre",
-    )(*legendre_inputs(order, bands, band_rows, waves, bands * band_rows))
+    )(step_a, step_c, *map(near, planes))
 
 
 def interpolate(prognostic, north, south, west, east, departure, lat_weight, lon_weight, copies):
     channels, band_rows, sector_cols = prognostic.shape
     tall = band_rows + 2 * HALO
     tiles = sector_cols // LANES
+    used = -(-channels * band_rows // 16) * 16
     return pl.pallas_call(
         arrival_kernel,
-        out_shape=jax.ShapeDtypeStruct((copies, channels, band_rows, sector_cols), jnp.bfloat16),
+        out_shape=pltpu.VMEM((copies, used, sector_cols), jnp.bfloat16),
         in_specs=[vmem()] * 8,
         out_specs=vmem(),
         scratch_shapes=[
             pltpu.VMEM((channels, tiles + 2, tall, LANES), jnp.float32),
             pltpu.VMEM((2 * HALO + 1, tiles, tall, LANES), jnp.float32),
+            pltpu.VMEM((used, sector_cols), jnp.float32),
         ],
         name="arrival",
-    )(prognostic, north, south, west, east, departure, lat_weight, lon_weight)
+    )(prognostic, near(north), near(south), near(west), near(east), departure, lat_weight, lon_weight)
 
 
 def transform(cycles, fourier, row_waves, limits):
-    rows, points = fourier.shape
     return pl.pallas_call(
         transform_kernel,
-        out_shape=jax.ShapeDtypeStruct((rows, LANES), jnp.bfloat16),
+        out_shape=pltpu.VMEM((fourier.shape[0], LANES), jnp.bfloat16),
         in_specs=[vmem()] * 4,
         out_specs=vmem(),
-        scratch_shapes=[pltpu.VMEM((LANES, points), jnp.float32)],
         name="transform",
-    )(cycles, fourier, row_waves, limits)
+    )(near(cycles), near(fourier), near(row_waves), near(limits))
 
 
 def synthesize(order, data, functions, channels):
@@ -286,7 +298,7 @@
             pltpu.VMEM((32, span), jnp.float32),
         ],
         name="synthesis",
-    )(order, data, functions)
+    )(order, near(data), near(functions))
 
 
 def shards(prognostic, departure, lat_weight, lon_weight, cycle_waves, wave_order):
@@ -298,11 +310,22 @@
     band_index = lax.axis_index("lat")
     sector_index = lax.axis_index("lon")
 
-    north = lax.ppermute(
-        prognostic[:, band_rows - HALO :, :], "lat", [(i, i + 1) for i in range(bands - 1)]
-    )
-    south = lax.ppermute(prognostic[:, :HALO, :], "lat", [(i + 1, i) for i in range(bands - 1)])
-
+    north = lax.ppermute(prognostic, "lat", [(i, i + 1) for i in range(bands - 1)])
+    south = lax.ppermute(prognostic, "lat", [(i + 1, i) for i in range(bands - 1)])
+
+    tall_west = jnp.concatenate(
+        [north[:, :, -LANES:], prognostic[:, :, -LANES:], south[:, :, -LANES:]], axis=1
+    )
+    tall_east = jnp.concatenate(
+        [north[:, :, :LANES], prognostic[:, :, :LANES], south[:, :, :LANES]], axis=1
+    )
+    west = lax.ppermute(tall_west, "lon", [(i, (i + 1) % sectors) for i in range(sectors)])
+    east = lax.ppermute(tall_east, "lon", [((i + 1) % sectors, i) for i in range(sectors)])
+    arrival = interpolate(
+        prognostic, north, south, west, east, departure, lat_weight, lon_weight, sectors
+    )
+    arrival, wave_order, cycle_waves = lax.optimization_barrier((arrival, wave_order, cycle_waves))
+    cycles = lax.all_to_all(arrival, "lon", split_axis=0, concat_axis=0, tiled=True)
     slot_waves = wave_order.reshape(bands, sectors)
     own_waves = lax.dynamic_slice_in_dim(slot_waves, sector_index, 1, axis=1)
     row_waves = jnp.broadcast_to(own_waves[:, :, None], (bands, 2, LANES)).reshape(
@@ -314,19 +337,7 @@
     ).reshape(1, LANES)
     fourier = fourier_table(row_waves, total_lon)
     functions = legendre_table(order, bands, band_rows, waves)
-
-    tall_west = jnp.concatenate(
-        [north[:, :, -LANES:], prognostic[:, :, -LANES:], south[:, :, -LANES:]], axis=1
-    )
-    tall_east = jnp.concatenate(
-        [north[:, :, :LANES], prognostic[:, :, :LANES], south[:, :, :LANES]], axis=1
-    )
-    west = lax.ppermute(tall_west, "lon", [(i, (i + 1) % sectors) for i in range(sectors)])
-    east = lax.ppermute(tall_east, "lon", [((i + 1) % sectors, i) for i in range(sectors)])
-    arrival = interpolate(
-        prognostic, north, south, west, east, departure, lat_weight, lon_weight, sectors
-    )
-    cycles = lax.all_to_all(arrival, "lon", split_axis=0, concat_axis=0, tiled=True)
+    cycles, functions = lax.optimization_barrier((cycles, functions))
     masked = transform(cycles, fourier, row_waves, limits)
     data = lax.all_to_all(
         masked.reshape(bands, 2, LANES), "lat", split_axis=0, concat_axis=0, tiled=True

time: 76.6 us -> 71.3 us (0.931)
  blocking collectives: 0 us -> 28.4 us
  starting transfers between devices: 37.2 us -> 25.2 us
  waiting for transfers between devices: 12.2 us -> 3.4 us
  Pallas kernels: 17.5 us -> 9.57 us
  local copies, waits for them, and re-layouts: 7.09 us -> 2.7 us
    all_to_all x0 -> x1, blocking collectives: none -> 28.4 us  [shards(): lax.all_to_all(masked.reshape(bands, 2, LANES), 'lat', split_axis=0, conc...]
    all_to_all x1 -> x0, starting transfers between devices: 16 us -> none  [shards(): lax.all_to_all(masked.reshape(bands, 2, LANES), 'lat', split_axis=0, conc...]
    all_to_all x1 -> x0, waiting for transfers between devices: 6.78 us -> none  [shards(): lax.all_to_all(masked.reshape(bands, 2, LANES), 'lat', split_axis=0, conc...]
    pallas_call x1, Pallas kernels: 4.06 us -> 0.83 us  [fourier_table(): pl.pallas_call(functools.partial(fourier_kernel, points=points), out_shap...]
    ppermute x1, starting transfers between devices: 4.57 us -> 7.56 us  [shards(): lax.ppermute(tall_east, 'lon', [((i + 1) % sectors, i) for i in range(sec...]
    ppermute x2, waiting for transfers between devices: 3.2 us -> 0.75 us  [the longest x1 0.74 us: shards(): lax.ppermute(prognostic, 'lat', [(i, i + 1) for i in range(bands - 1)])]
    unnamed x16 -> x4, local copies, waits for them, and re-layouts: 2.4 us -> 0.01 us
    pallas_call x2, Pallas kernels: 5.8 us -> 3.79 us  [the longest x1 3.34 us: interpolate(): pl.pallas_call(arrival_kernel, out_shape=pltpu.VMEM((copies, used, sector...]
  transfers between devices with their start and end apart: 6 -> 5, of which waited for: 5 -> 4; matrix products, arithmetic and copies ran while one was open for 7% -> 5% of each run, Pallas kernels for 11% -> 6%
where the time goes in v2:
time: 71.3 us; the launch traced here: 70.8 us
  blocking collectives  28.4 us (40%)
  starting transfers between devices  25.2 us (35%)
  Pallas kernels  9.57 us (13%)
  waiting for transfers between devices  3.4 us (5%)
  local copies, waits for them, and re-layouts  2.7 us (4%)
  between operations  0.75 us (1%)
  other arithmetic  0.74 us (1%)
    all_to_all x1, blocking collectives, shards(): lax.all_to_all(masked.reshape(bands, 2, LANES), 'lat', split_axis=0, conc...  28.4 us
    all_to_all x1, starting transfers between devices, shards(): lax.all_to_all(arrival, 'lon', split_axis=0, concat_axis=0, tiled=True)  8.11 us
    ppermute x1, starting transfers between devices, shards(): lax.ppermute(tall_east, 'lon', [((i + 1) % sectors, i) for i in range(sec...  7.56 us
    ppermute x1, starting transfers between devices, shards(): lax.ppermute(prognostic, 'lat', [(i, i + 1) for i in range(bands - 1)])  5.45 us
    pallas_call x1, Pallas kernels, interpolate(): pl.pallas_call(arrival_kernel, out_shape=pltpu.VMEM((copies, used, sector...  3.34 us
    pallas_call x1, Pallas kernels, legendre_table(): pl.pallas_call(functools.partial(legendre_kernel, waves=waves, band_rows=...  3.07 us
    ppermute x1, starting transfers between devices, shards(): lax.ppermute(tall_west, 'lon', [(i, (i + 1) % sectors) for i in range(sec...  2.64 us
    pallas_call x1, Pallas kernels, synthesize(): pl.pallas_call(synthesis_kernel, out_shape=jax.ShapeDtypeStruct((channels...  1.88 us
  transfers between devices with their start and end apart: 5, of which 4 were waited for; matrix products, arithmetic and copies ran while one was open for 5% of the time, Pallas kernels for 6%

profile of v2, /device:TPU:1, one launch (start us, length us, event | category | flops | bytes accessed | tf_op | source)
XLA Modules:
  0.0 70.8 jit_solution(11072242849947588713)
XLA Ops:
  0.0 0.0 copy-start
  0.0 0.0 copy-start.1
  0.0 1.4 %collective-permute-start.1 = (bf16[9,8,384]{2,1,0:T(8,128)(2,1)}, bf16[9,8,384]{2,1,0:T(8,128)(2,1)S(1)}, u32[]{:S(2)}, u32[]{:S(2)}) collective-permute-start(bf16[9,8,384]{2,1,0:T(8,128)(2,1)} %field.1), channel_id=1, source_target_pairs={{8,0},{16,8},{24,16},{32,24},{40,32},{48,40},{56,48},{64,56},{72,6... | collective-permute-start | bytes 165896 | tf_op jit(solution)/shard_map/ppermute | solution.py:314
  1.4 5.4 %collective-permute-start = (bf16[9,8,384]{2,1,0:T(8,128)(2,1)}, bf16[9,8,384]{2,1,0:T(8,128)(2,1)S(1)}, u32[]{:S(2)}, u32[]{:S(2)}) collective-permute-start(bf16[9,8,384]{2,1,0:T(8,128)(2,1)} %field.1), channel_id=1, source_target_pairs={{0,8},{8,16},{16,24},{24,32},{32,40},{40,48},{48,56},{56,64},{64,7... | collective-permute-start | bytes 165896 | tf_op jit(solution)/shard_map/ppermute | solution.py:313
  6.9 0.8 %fusion.22 = (bf16[9,8,128]{2,1,0:T(8,128)(2,1)S(1)}, bf16[9,8,128]{2,1,0:T(8,128)(2,1)S(1)}) fusion(bf16[9,8,384]{2,1,0:T(8,128)(2,1)} %field.1), kind=kLoop, calls=%fused_computation.37 | loop fusion | bytes 73728 | tf_op jit(solution)/shard_map/slice | solution.py:320
  7.7 0.0 collective-permute-done.1.south
  7.7 0.7 %collective-permute-done.north = bf16[9,8,384]{2,1,0:T(8,128)(2,1)S(1)} collective-permute-done((bf16[9,8,384]{2,1,0:T(8,128)(2,1)}, bf16[9,8,384]{2,1,0:T(8,128)(2,1)S(1)}, u32[]{:S(2)}, u32[]{:S(2)}) %collective-permute-start) | collective-permute-done | bytes 55328 | tf_op jit(solution)/shard_map/ppermute | solution.py:313
  8.4 2.6 %collective-permute-start.2 = (bf16[9,24,128]{2,1,0:T(8,128)(2,1)S(1)}, bf16[9,24,128]{2,1,0:T(8,128)(2,1)S(1)}, u32[]{:S(2)}, u32[]{:S(2)}) collective-permute-start(bf16[9,24,128]{2,1,0:T(8,128)(2,1)S(1)} %pad_maximum_fusion), channel_id=1, source_target_pairs={{0,1},{1,2},{2,3},{3,4},{4,5},{5,6},{6,7},{7,0},{8,9},{9,10},{10,1... | collective-permute-start | bytes 165896 | tf_op jit(solution)/shard_map/ppermute | solution.py:322
  11.1 7.6 %collective-permute-start.3 = (bf16[9,24,128]{2,1,0:T(8,128)(2,1)S(1)}, bf16[9,24,128]{2,1,0:T(8,128)(2,1)S(1)}, u32[]{:S(2)}, u32[]{:S(2)}) collective-permute-start(bf16[9,24,128]{2,1,0:T(8,128)(2,1)S(1)} %pad_maximum_fusion.1), channel_id=1, source_target_pairs={{1,0},{2,1},{3,2},{4,3},{5,4},{6,5},{7,6},{0,7},{9,8},{10,9},{11,1... | collective-permute-start | bytes 165896 | tf_op jit(solution)/shard_map/ppermute | solution.py:323
  18.6 0.7 collective-permute-done.2.west
  19.3 0.2 collective-permute-done.3.east
  19.5 3.3 %arrival.1 = bf16[8,80,384]{2,1,0:T(8,128)(2,1)} custom-call(bf16[9,8,384]{2,1,0:T(8,128)(2,1)} %field.1, bf16[9,8,384]{2,1,0:T(8,128)(2,1)S(1)} %collective-permute-done.north, bf16[9,8,384]{2,1,0:T(8,128)(2,1)S(1)} %collective-permute-done.1.south, bf16[9,24,128]{2,1,0:T(8,128)(2,1)S(1)} %collective-permute-done.2.west, ...), custom_call_target="tpu_custom_call" | custom-call | tf_op jit(solution)/shard_map/arrival/pallas_call | solution.py:264
  22.9 8.1 %all-to-all-start = ((bf16[8,80,384]{2,1,0:T(8,128)(2,1)}), bf16[8,80,384]{2,1,0:T(8,128)(2,1)S(1)}, u32[]{:S(2)}, u32[]{:S(2)}) async-start(bf16[8,80,384]{2,1,0:T(8,128)(2,1)} %arrival.1), calls=%async_computation | async-start | bytes 983040 | tf_op jit(solution)/shard_map/all_to_all | solution.py:328
  31.0 0.0 copy-done
  31.0 0.1 reshape.20
  31.1 0.6 dynamic_slice.8.order
  32.3 0.6 broadcast_in_dim.28
  33.0 0.0 copy-done.1
  33.0 0.1 broadcast_in_dim.34.limits
  33.1 0.2 dynamic-slice_reduce_fusion
  33.3 0.1 broadcast_in_dim.30
  33.3 0.2 broadcast_in_dim.31
  33.5 0.1 broadcast_in_dim.32.waves
  33.6 0.8 %fourier.1 = bf16[192,3072]{1,0:T(8,128)(2,1)S(1)} custom-call(s32[192,128]{1,0:T(8,128)S(1)} %broadcast_in_dim.32.waves), custom_call_target="tpu_custom_call" | custom-call | tf_op jit(solution)/shard_map/fourier/pallas_call | solution.py:238
  34.4 0.6 fusion.2
  35.1 0.1 fusion.20
  35.1 3.1 %legendre.1.functions = bf16[768,1024]{1,0:T(8,128)(2,1)S(1)} custom-call(f32[768]{0:T(1024)} %get-tuple-element.24.step_a, f32[768]{0:T(1024)} %get-tuple-element.25.step_c, f32[8,128]{1,0:T(8,128)S(1)} %get-tuple-element.23.cosine, f32[8,128]{1,0:T(8,128)S(1)} %get-tuple-element.22.log_start, f32[8,128]{1,0:T(8,128)S(1)} %get-tuple-element.21.weight), custom_call_target="tpu_custom_call" | custom-call | tf_op jit(solution)/shard_map/legendre/pallas_call | solution.py:249
  38.2 1.8 %all-to-all-done.cycles = bf16[8,80,384]{2,1,0:T(8,128)(2,1)S(1)} async-done(((bf16[8,80,384]{2,1,0:T(8,128)(2,1)}), bf16[8,80,384]{2,1,0:T(8,128)(2,1)S(1)}, u32[]{:S(2)}, u32[]{:S(2)}) %all-to-all-start) | async-done | bytes 491552 | tf_op jit(solution)/shard_map/all_to_all | solution.py:328
  40.0 0.5 transform.1
  40.4 28.4 %all_to_all.10 = bf16[96,2,128]{2,1,0:T(2,128)(2,1)S(1)} all-to-all(bf16[96,2,128]{2,1,0:T(2,128)(2,1)S(1)} %bitcast.9), channel_id=1, replica_groups=mesh['lat'=96,'lon'=8] {'lat'}, dimensions={0} | all-to-all | bytes 98304 | tf_op jit(solution)/shard_map/all_to_all | solution.py:342
  68.9 1.9 %synthesis.1 = f32[9,2,768]{2,1,0:T(2,128)} custom-call(s32[1]{0:T(128)} %dynamic_slice.8.order, bf16[192,128]{1,0:T(8,128)(2,1)S(1)} %bitcast.8, bf16[768,1024]{1,0:T(8,128)(2,1)S(1)} %legendre.1.functions), custom_call_target="tpu_custom_call" | custom-call | tf_op jit(solution)/shard_map/synthesis/pallas_call | solution.py:290
  (6 shorter events, 0.0 us)
Async XLA Ops:
  0.0 31.0 %copy-start = (s32[768]{0:T(1024)S(1)}, s32[768]{0:T(1024)}, u32[]{:S(2)}) copy-start(s32[768]{0:T(1024)} %param.11) | copy-start | bytes 9220
  0.0 33.0 %copy-start.1 = (s32[8]{0:T(128)S(1)}, s32[8]{0:T(128)}, u32[]{:S(2)}) copy-start(s32[8]{0:T(128)} %param.10) | copy-start | bytes 100
  0.0 7.7 %collective-permute-start.1 = (bf16[9,8,384]{2,1,0:T(8,128)(2,1)}, bf16[9,8,384]{2,1,0:T(8,128)(2,1)S(1)}, u32[]{:S(2)}, u32[]{:S(2)}) collective-permute-start(bf16[9,8,384]{2,1,0:T(8,128)(2,1)} %field.1), channel_id=1, source_target_pairs={{8,0},{16,8},{24,16},{32,24},{40,32},{48,40},{56,48},{64,56},{72,6... | collective-permute-start | bytes 165896 | tf_op jit(solution)/shard_map/ppermute | solution.py:314
  1.4 7.0 %collective-permute-start = (bf16[9,8,384]{2,1,0:T(8,128)(2,1)}, bf16[9,8,384]{2,1,0:T(8,128)(2,1)S(1)}, u32[]{:S(2)}, u32[]{:S(2)}) collective-permute-start(bf16[9,8,384]{2,1,0:T(8,128)(2,1)} %field.1), channel_id=1, source_target_pairs={{0,8},{8,16},{16,24},{24,32},{32,40},{40,48},{48,56},{56,64},{64,7... | collective-permute-start | bytes 165896 | tf_op jit(solution)/shard_map/ppermute | solution.py:313
  8.4 10.9 %collective-permute-start.2 = (bf16[9,24,128]{2,1,0:T(8,128)(2,1)S(1)}, bf16[9,24,128]{2,1,0:T(8,128)(2,1)S(1)}, u32[]{:S(2)}, u32[]{:S(2)}) collective-permute-start(bf16[9,24,128]{2,1,0:T(8,128)(2,1)S(1)} %pad_maximum_fusion), channel_id=1, source_target_pairs={{0,1},{1,2},{2,3},{3,4},{4,5},{5,6},{6,7},{7,0},{8,9},{9,10},{10,1... | collective-permute-start | bytes 165896 | tf_op jit(solution)/shard_map/ppermute | solution.py:322
  11.1 8.4 %collective-permute-start.3 = (bf16[9,24,128]{2,1,0:T(8,128)(2,1)S(1)}, bf16[9,24,128]{2,1,0:T(8,128)(2,1)S(1)}, u32[]{:S(2)}, u32[]{:S(2)}) collective-permute-start(bf16[9,24,128]{2,1,0:T(8,128)(2,1)S(1)} %pad_maximum_fusion.1), channel_id=1, source_target_pairs={{1,0},{2,1},{3,2},{4,3},{5,4},{6,5},{7,6},{0,7},{9,8},{10,9},{11,1... | collective-permute-start | bytes 165896 | tf_op jit(solution)/shard_map/ppermute | solution.py:323
  22.9 17.1 %all-to-all-start = ((bf16[8,80,384]{2,1,0:T(8,128)(2,1)}), bf16[8,80,384]{2,1,0:T(8,128)(2,1)S(1)}, u32[]{:S(2)}, u32[]{:S(2)}) async-start(bf16[8,80,384]{2,1,0:T(8,128)(2,1)} %arrival.1), calls=%async_computation | async-start | bytes 983040 | tf_op jit(solution)/shard_map/all_to_all | solution.py:328

commit v3 on v2

--- a/solution.py
+++ b/solution.py
@@ -11,6 +11,7 @@
 HALO = 4
 LANES = 128
 BLOCK = 32
+WINDOW = 4 * HALO
 LGAMMA_HALF_THREE = 0.5 * math.log(math.pi) - math.log(2.0)
 SINE = (
     3.1415926535897932,
@@ -27,7 +28,11 @@
     scale = 1.0 / math.sqrt(points)
     row = lax.broadcasted_iota(jnp.int32, (group, LANES), 0)
     turn = (row % 2 * (points // 4)).astype(jnp.float32)
-    lane = lax.broadcasted_iota(jnp.int32, (group, LANES), 1).astype(jnp.float32)
+    place = lax.broadcasted_iota(jnp.int32, (group, LANES), 1)
+    lane = place.astype(jnp.float32)
+    column = (
+        (place // WINDOW + 1) * (points * WINDOW // LANES) - 2 * HALO + place % WINDOW
+    ).astype(jnp.float32)
 
     def cosine(phase):
         phase = phase - jnp.floor(phase * (1.0 / points) + 0.5) * float(points)
@@ -53,6 +58,8 @@
                 real * turn_real - imag * turn_imag,
                 imag * turn_real + real * turn_imag,
             )
+        edge = cosine(column * wave + turn) * scale
+        out[pl.ds(first, group), points : points + LANES] = edge.astype(jnp.bfloat16)
         return carry
 
     lax.fori_loop(0, rows // group, block, 0)
@@ -85,84 +92,189 @@
     lax.fori_loop(0, waves // BLOCK, block, initial)
 
 
-def arrival_kernel(
-    field, north, south, west, east, departure, lat_weight, lon_weight, out, grid, shifted, stage
-):
+def spread(place, share):
+    return [
+        jnp.where(place == d, 1.0 - share, jnp.where(place == d - 1, share, 0.0))
+        for d in range(2 * HALO + 1)
+    ]
+
+
+def edges(tall, slot):
+    lane = lax.broadcasted_iota(jnp.int32, tall[0].shape, 1)
+    reach = 2 * HALO
+    ends = jnp.where(
+        lane < reach, tall[0], jnp.where(lane >= LANES - reach, tall[-1], jnp.zeros_like(tall[0]))
+    )
+    return pltpu.roll(ends, slot * WINDOW + reach, 1)
+
+
+def stencil(read, write, row_parts, col_parts, tiles, rows):
+    count = 2 * HALO + 1
+    source = read()
+    lane = lax.broadcasted_iota(jnp.int32, source[0].shape, 1)
+    for d in range(count):
+        move = d - HALO
+        if move == 0:
+            turned = source
+        else:
+            rolled = [pltpu.roll(tile, -move % LANES, 1) for tile in source]
+            if tiles == 1:
+                turned = rolled
+            elif move > 0:
+                turned = [
+                    jnp.where(lane < LANES - move, rolled[t], rolled[(t + 1) % tiles])
+                    for t in range(tiles)
+                ]
+            else:
+                turned = [
+                    jnp.where(lane < -move, rolled[t - 1], rolled[t]) for t in range(tiles)
+                ]
+        for t in range(tiles):
+            write[d, t] = turned[t]
+    sums = []
+    for t in range(tiles):
+        total = None
+        for e in range(count):
+            inner = None
+            for d in range(count):
+                term = col_parts(d, t) * write[d, t, e : e + rows, :]
+                inner = term if inner is None else inner + term
+            term = row_parts(e, t) * inner
+            total = term if total is None else total + term
+        sums.append(total)
+    return sums
+
+
+def split(value):
+    high = value.astype(jnp.bfloat16).astype(jnp.float32)
+    rest = value - high
+    middle = rest.astype(jnp.bfloat16).astype(jnp.float32)
+    return [high, middle, rest - middle]
+
+
+def prepare_kernel(field, departure, lat_weight, lon_weight, field_out, parts, planes):
+    cols = departure.shape[1]
+    field_out[...] = field[...]
+    cell = departure[...]
+    a = lat_weight[...]
+    b = lon_weight[...]
+    for d, part in enumerate(spread(cell // (2 * HALO), a) + spread(cell % (2 * HALO), b)):
+        parts[d] = part
+    total = None
+    for p, plane in enumerate([cell.astype(jnp.float32)] + split(a) + split(b)):
+        tall = [plane[:, t * LANES : (t + 1) * LANES] for t in range(cols // LANES)]
+        term = edges(tall, p + 1)
+        total = term if total is None else total + term
+    planes[...] = total
+
+
+def arrival_kernel(sector, field, north, south, parts, planes, out, grid, shifted, stage):
     channels, rows, cols = field.shape
     tiles = cols // LANES
-    copies = out.shape[0]
-    stencil = 2 * HALO
-    row_place = departure[...] // stencil
-    col_place = departure[...] % stencil
-    a = lat_weight[...]
-    b = lon_weight[...]
-
-    def spread(place, share):
-        return [
-            jnp.where(place == d, 1.0 - share, jnp.where(place == d - 1, share, 0.0))
-            for d in range(stencil + 1)
-        ]
-
-    row_parts = spread(row_place, a)
-    col_parts = spread(col_place, b)
-    lane = lax.broadcasted_iota(jnp.int32, (rows + 2 * HALO, LANES), 1)
+    count = 2 * HALO + 1
+    used = channels * rows
+    tall = rows + 2 * HALO
+    lane = lax.broadcasted_iota(jnp.int32, (rows, LANES), 1)
     for c in range(channels):
-        grid[c, 0] = west[c].astype(jnp.float32)[rows - HALO : 2 * rows + HALO]
-        grid[c, tiles + 1] = east[c].astype(jnp.float32)[rows - HALO : 2 * rows + HALO]
         up = north[c].astype(jnp.float32)[rows - HALO :]
         mid = field[c].astype(jnp.float32)
         down = south[c].astype(jnp.float32)[:HALO]
         for t in range(tiles):
             span = slice(t * LANES, (t + 1) * LANES)
-            grid[c, t + 1, 0:HALO, :] = up[:, span]
-            grid[c, t + 1, HALO : HALO + rows, :] = mid[:, span]
-            grid[c, t + 1, HALO + rows :, :] = down[:, span]
+            grid[c, t, 0:HALO, :] = up[:, span]
+            grid[c, t, HALO : HALO + rows, :] = mid[:, span]
+            grid[c, t, HALO + rows :, :] = down[:, span]
+
+    def part(first):
+        return lambda d, t: parts[first + d, :, t * LANES : (t + 1) * LANES]
 
     def channel(c, carry):
-        source = [grid[c, t] for t in range(tiles + 2)]
-        for d in range(stencil + 1):
-            move = d - HALO
-            if move == 0:
-                for t in range(tiles):
-                    shifted[d, t] = source[t + 1]
-                continue
-            if move > 0:
-                turned = [pltpu.roll(source[t], LANES - move, 1) for t in range(1, tiles + 2)]
-                for t in range(tiles):
-                    shifted[d, t] = jnp.where(lane < LANES - move, turned[t], turned[t + 1])
-            else:
-                turned = [pltpu.roll(source[t], -move, 1) for t in range(tiles + 1)]
-                for t in range(tiles):
-                    shifted[d, t] = jnp.where(lane < -move, turned[t], turned[t + 1])
+        sums = stencil(
+            lambda: [grid[c, t] for t in range(tiles)],
+            shifted,
+            part(0),
+            part(count),
+            tiles,
+            rows,
+        )
+        sums[0] = jnp.where(lane < HALO, 0.0, sums[0])
+        sums[-1] = jnp.where(lane >= LANES - HALO, 0.0, sums[-1])
         for t in range(tiles):
             span = slice(t * LANES, (t + 1) * LANES)
-            total = None
-            for e in range(stencil + 1):
-                inner = None
-                for d in range(stencil + 1):
-                    term = col_parts[d][:, span] * shifted[d, t, e : e + rows, :]
-                    inner = term if inner is None else inner + term
-                term = row_parts[e][:, span] * inner
-                total = term if total is None else total + term
-            stage[pl.ds(pl.multiple_of(c * rows, rows), rows), span] = total
+            stage[pl.ds(pl.multiple_of(c * rows, rows), rows), span] = sums[t]
         return carry
 
-    used = channels * rows
-    stage[used:, :] = jnp.zeros_like(stage[used:, :])
     lax.fori_loop(0, channels, channel, 0)
+    slots = LANES // WINDOW
+    turn = sector[0] * WINDOW
+    for g in range(2):
+        total = None
+        for c in range(g * slots, min((g + 1) * slots, channels)):
+            term = edges([grid[c, 0], grid[c, tiles - 1]], c - g * slots)
+            total = term if total is None else total + term
+        if g == 1:
+            total = total + jnp.concatenate([planes[...], jnp.zeros_like(planes[...])], axis=0)
+        stage[used : used + tall, g * LANES : (g + 1) * LANES] = pltpu.roll(total, turn, 1)
+    stage[used : used + tall, 2 * LANES :] = jnp.zeros((tall, cols - 2 * LANES), jnp.float32)
     value = stage[...].astype(jnp.bfloat16)
-    for copy in range(copies):
+    for copy in range(out.shape[0]):
         out[copy] = value
 
 
-def transform_kernel(cycles, fourier, waves, limits, out):
-    sectors, used, _ = cycles.shape
-    gathered = jnp.concatenate([cycles[sector] for sector in range(sectors)], axis=1)
+def transform_kernel(cycles, fourier, waves, limits, out, shifted, stage):
+    sectors = cycles.shape[0]
+    used, rows = stage.shape[0], shifted.shape[2] - 2 * HALO
+    tall = rows + 2 * HALO
+    channels = used // rows
+    slots = LANES // WINDOW
+    slot = lax.broadcasted_iota(jnp.int32, (tall, LANES), 1) // WINDOW
+    inner = lax.broadcasted_iota(jnp.int32, (tall, LANES), 1) % WINDOW
+    pieces = [
+        [
+            cycles[sector, used : used + tall, g * LANES : (g + 1) * LANES].astype(jnp.float32)
+            for sector in range(sectors)
+        ]
+        for g in range(2)
+    ]
+
+    def window(index, height):
+        g, c = divmod(index, slots)
+        total = pieces[g][0][:height]
+        for sector in range(1, sectors):
+            total = jnp.where(
+                slot[:height] == (c + sector) % slots, pieces[g][sector][:height], total
+            )
+        left = pltpu.roll(total, -c * WINDOW % LANES, 1) if c else total
+        right = pltpu.roll(total, -(c + 1) * WINDOW % LANES, 1) if c + 1 < slots else total
+        return jnp.where(inner[:height] < 2 * HALO, left, right)
+
+    cell, *weights = [window(channels + p, rows) for p in range(7)]
+    a = weights[0] + weights[1] + weights[2]
+    b = weights[3] + weights[4] + weights[5]
+    high = jnp.floor(cell * (1.0 / (2 * HALO)))
+    row_parts = spread(high, a)
+    col_parts = spread(cell - high * (2 * HALO), b)
+    inside = (inner[:rows] >= HALO) & (inner[:rows] < 3 * HALO)
+    for c in range(channels):
+        (total,) = stencil(
+            lambda: [window(c, tall)],
+            shifted,
+            lambda e, t: row_parts[e],
+            lambda d, t: col_parts[d],
+            1,
+            rows,
+        )
+        stage[c * rows : (c + 1) * rows, :] = jnp.where(inside, total, 0.0)
+    gathered = jnp.concatenate(
+        [cycles[sector, :used, :] for sector in range(sectors)]
+        + [stage[...].astype(jnp.bfloat16)],
+        axis=1,
+    )
     spectrum = lax.dot_general(
         fourier[...], gathered, (((1,), (1,)), ((), ())), preferred_element_type=jnp.float32
     )
-    inside = waves[:, :used] < limits[:, :used]
-    out[:, :used] = jnp.where(inside, spectrum, 0.0).astype(jnp.bfloat16)
+    resolved = waves[:, :used] < limits[:, :used]
+    out[:, :used] = jnp.where(resolved, spectrum, 0.0).astype(jnp.bfloat16)
     out[:, used:] = jnp.zeros((out.shape[0], out.shape[1] - used), jnp.bfloat16)
 
 
@@ -237,7 +349,7 @@
 def fourier_table(row_waves, points):
     return pl.pallas_call(
         functools.partial(fourier_kernel, points=points),
-        out_shape=pltpu.VMEM((row_waves.shape[0], points), jnp.bfloat16),
+        out_shape=pltpu.VMEM((row_waves.shape[0], points + LANES), jnp.bfloat16),
         in_specs=[vmem()],
         out_specs=vmem(),
         name="fourier",
@@ -256,33 +368,52 @@
     )(step_a, step_c, *map(near, planes))
 
 
-def interpolate(prognostic, north, south, west, east, departure, lat_weight, lon_weight, copies):
-    channels, band_rows, sector_cols = prognostic.shape
+def prepare(prognostic, departure, lat_weight, lon_weight):
+    _, band_rows, sector_cols = prognostic.shape
+    return pl.pallas_call(
+        prepare_kernel,
+        out_shape=(
+            pltpu.VMEM(prognostic.shape, jnp.bfloat16),
+            pltpu.VMEM((2 * (2 * HALO + 1), band_rows, sector_cols), jnp.float32),
+            pltpu.VMEM((band_rows, LANES), jnp.float32),
+        ),
+        in_specs=[vmem()] * 4,
+        out_specs=(vmem(),) * 3,
+        name="prepare",
+    )(prognostic, departure, lat_weight, lon_weight)
+
+
+def interpolate(sector, field, north, south, parts, planes, copies):
+    channels, band_rows, sector_cols = field.shape
     tall = band_rows + 2 * HALO
     tiles = sector_cols // LANES
-    used = -(-channels * band_rows // 16) * 16
+    height = channels * band_rows + tall
     return pl.pallas_call(
         arrival_kernel,
-        out_shape=pltpu.VMEM((copies, used, sector_cols), jnp.bfloat16),
-        in_specs=[vmem()] * 8,
+        out_shape=pltpu.VMEM((copies, height, sector_cols), jnp.bfloat16),
+        in_specs=[smem()] + [vmem()] * 5,
         out_specs=vmem(),
         scratch_shapes=[
-            pltpu.VMEM((channels, tiles + 2, tall, LANES), jnp.float32),
+            pltpu.VMEM((channels, tiles, tall, LANES), jnp.float32),
             pltpu.VMEM((2 * HALO + 1, tiles, tall, LANES), jnp.float32),
-            pltpu.VMEM((used, sector_cols), jnp.float32),
+            pltpu.VMEM((height, sector_cols), jnp.float32),
         ],
         name="arrival",
-    )(prognostic, near(north), near(south), near(west), near(east), departure, lat_weight, lon_weight)
-
-
-def transform(cycles, fourier, row_waves, limits):
+    )(sector, *map(near, (field, north, south, parts, planes)))
+
+
+def transform(cycles, fourier, row_waves, limits, channels, band_rows):
     return pl.pallas_call(
         transform_kernel,
         out_shape=pltpu.VMEM((fourier.shape[0], LANES), jnp.bfloat16),
         in_specs=[vmem()] * 4,
         out_specs=vmem(),
+        scratch_shapes=[
+            pltpu.VMEM((2 * HALO + 1, 1, band_rows + 2 * HALO, LANES), jnp.float32),
+            pltpu.VMEM((channels * band_rows, LANES), jnp.float32),
+        ],
         name="transform",
-    )(near(cycles), near(fourier), near(row_waves), near(limits))
+    )(*map(near, (cycles, fourier, row_waves, limits)))
 
 
 def synthesize(order, data, functions, channels):
@@ -313,35 +444,27 @@
     north = lax.ppermute(prognostic, "lat", [(i, i + 1) for i in range(bands - 1)])
     south = lax.ppermute(prognostic, "lat", [(i + 1, i) for i in range(bands - 1)])
 
-    tall_west = jnp.concatenate(
-        [north[:, :, -LANES:], prognostic[:, :, -LANES:], south[:, :, -LANES:]], axis=1
-    )
-    tall_east = jnp.concatenate(
-        [north[:, :, :LANES], prognostic[:, :, :LANES], south[:, :, :LANES]], axis=1
-    )
-    west = lax.ppermute(tall_west, "lon", [(i, (i + 1) % sectors) for i in range(sectors)])
-    east = lax.ppermute(tall_east, "lon", [((i + 1) % sectors, i) for i in range(sectors)])
+    field, parts, planes = prepare(prognostic, departure, lat_weight, lon_weight)
     arrival = interpolate(
-        prognostic, north, south, west, east, departure, lat_weight, lon_weight, sectors
-    )
-    arrival, wave_order, cycle_waves = lax.optimization_barrier((arrival, wave_order, cycle_waves))
+        sector_index.astype(jnp.int32).reshape(1), field, north, south, parts, planes, sectors
+    )
     cycles = lax.all_to_all(arrival, "lon", split_axis=0, concat_axis=0, tiled=True)
+
     slot_waves = wave_order.reshape(bands, sectors)
     own_waves = lax.dynamic_slice_in_dim(slot_waves, sector_index, 1, axis=1)
     row_waves = jnp.broadcast_to(own_waves[:, :, None], (bands, 2, LANES)).reshape(
         2 * bands, LANES
     )
-    order = lax.dynamic_slice_in_dim(wave_order, band_index * sectors + sector_index, 1)
     limits = jnp.broadcast_to(
         cycle_waves[None, None, :], (1, LANES // band_rows, band_rows)
     ).reshape(1, LANES)
     fourier = fourier_table(row_waves, total_lon)
-    functions = legendre_table(order, bands, band_rows, waves)
-    cycles, functions = lax.optimization_barrier((cycles, functions))
-    masked = transform(cycles, fourier, row_waves, limits)
+    masked = transform(cycles, fourier, row_waves, limits, prognostic.shape[0], band_rows)
     data = lax.all_to_all(
         masked.reshape(bands, 2, LANES), "lat", split_axis=0, concat_axis=0, tiled=True
     ).reshape(2 * bands, LANES)
+    order = lax.dynamic_slice_in_dim(wave_order, band_index * sectors + sector_index, 1)
+    functions = legendre_table(order, bands, band_rows, waves)
     spectral = synthesize(order, data, functions, prognostic.shape[0])
     return spectral.transpose(1, 0, 2)[None]
 

time: 71.3 us -> 67.5 us (0.947)
  blocking collectives: 28.4 us -> 0 us
  waiting for transfers between devices: 3.4 us -> 18.8 us
  starting transfers between devices: 25.2 us -> 34.1 us
  Pallas kernels: 9.57 us -> 10.8 us
  local copies, waits for them, and re-layouts: 2.7 us -> 1.91 us
    all_to_all x1 -> x0, blocking collectives: 28.4 us -> none  [shards(): lax.all_to_all(masked.reshape(bands, 2, LANES), 'lat', split_axis=0, conc...]
    all_to_all x0 -> x1, starting transfers between devices: none -> 16.9 us  [shards(): lax.all_to_all(masked.reshape(bands, 2, LANES), 'lat', split_axis=0, conc...]
    ppermute x2 -> x0, starting transfers between devices: 10.2 us -> none  [the longest x1 7.56 us: shards(): lax.ppermute(tall_east, 'lon', [((i + 1) % sectors, i) for i in range(sec...]
    all_to_all x0 -> x1, waiting for transfers between devices: none -> 8.59 us  [shards(): lax.all_to_all(masked.reshape(bands, 2, LANES), 'lat', split_axis=0, conc...]
    all_to_all x1, waiting for transfers between devices: 1.77 us -> 6.66 us  [shards(): lax.all_to_all(arrival, 'lon', split_axis=0, concat_axis=0, tiled=True)]
    ppermute x1, waiting for transfers between devices: 0.01 us -> 3.49 us  [shards(): lax.ppermute(prognostic, 'lat', [(i + 1, i) for i in range(bands - 1)])]
    all_to_all x1, starting transfers between devices: 8.11 us -> 11 us  [shards(): lax.all_to_all(arrival, 'lon', split_axis=0, concat_axis=0, tiled=True)]
    pallas_call x1, Pallas kernels: 0.45 us -> 1.38 us  [transform(): pl.pallas_call(transform_kernel, out_shape=pltpu.VMEM((fourier.shape[0],...]
  transfers between devices with their start and end apart: 5 -> 4, of which waited for: 4 -> 3; matrix products, arithmetic and copies ran while one was open for 5% -> 4% of each run, Pallas kernels for 6% -> 7%
where the time goes in v3:
time: 67.5 us; the launch traced here: 67.1 us
  starting transfers between devices  34.1 us (51%)
  waiting for transfers between devices  18.8 us (28%)
  Pallas kernels  10.8 us (16%)
  local copies, waits for them, and re-layouts  1.91 us (3%)
  between operations  0.77 us (1%)
  other arithmetic  0.71 us (1%)
    all_to_all x1, starting transfers between devices, shards(): lax.all_to_all(masked.reshape(bands, 2, LANES), 'lat', split_axis=0, conc...  16.9 us
    all_to_all x1, starting transfers between devices, shards(): lax.all_to_all(arrival, 'lon', split_axis=0, concat_axis=0, tiled=True)  11 us
    all_to_all x1, waiting for transfers between devices, shards(): lax.all_to_all(masked.reshape(bands, 2, LANES), 'lat', split_axis=0, conc...  8.59 us
    all_to_all x1, waiting for transfers between devices, shards(): lax.all_to_all(arrival, 'lon', split_axis=0, concat_axis=0, tiled=True)  6.66 us
    ppermute x1, starting transfers between devices, shards(): lax.ppermute(prognostic, 'lat', [(i, i + 1) for i in range(bands - 1)])  4.94 us
    ppermute x1, waiting for transfers between devices, shards(): lax.ppermute(prognostic, 'lat', [(i + 1, i) for i in range(bands - 1)])  3.49 us
    pallas_call x1, Pallas kernels, legendre_table(): pl.pallas_call(functools.partial(legendre_kernel, waves=waves, band_rows=...  3.06 us
    pallas_call x1, Pallas kernels, interpolate(): pl.pallas_call(arrival_kernel, out_shape=pltpu.VMEM((copies, height, sect...  2.62 us
  transfers between devices with their start and end apart: 4, of which 3 were waited for; matrix products, arithmetic and copies ran while one was open for 4% of the time, Pallas kernels for 7%

profile of v3, /device:TPU:1, one launch (start us, length us, event | category | flops | bytes accessed | tf_op | source)
XLA Modules:
  0.0 67.1 jit_solution(141144851606020826)
XLA Ops:
  0.0 0.0 copy-start
  0.0 4.9 %collective-permute-start = (bf16[9,8,384]{2,1,0:T(8,128)(2,1)}, bf16[9,8,384]{2,1,0:T(8,128)(2,1)S(1)}, u32[]{:S(2)}, u32[]{:S(2)}) collective-permute-start(bf16[9,8,384]{2,1,0:T(8,128)(2,1)} %field.1), channel_id=1, source_target_pairs={{0,8},{8,16},{16,24},{24,32},{32,40},{40,48},{48,56},{56,64},{64,7... | collective-permute-start | bytes 165896 | tf_op jit(solution)/shard_map/ppermute | solution.py:444
  4.9 1.3 %collective-permute-start.1 = (bf16[9,8,384]{2,1,0:T(8,128)(2,1)}, bf16[9,8,384]{2,1,0:T(8,128)(2,1)S(1)}, u32[]{:S(2)}, u32[]{:S(2)}) collective-permute-start(bf16[9,8,384]{2,1,0:T(8,128)(2,1)} %field.1), channel_id=1, source_target_pairs={{8,0},{16,8},{24,16},{32,24},{40,32},{48,40},{56,48},{64,56},{72,6... | collective-permute-start | bytes 165896 | tf_op jit(solution)/shard_map/ppermute | solution.py:445
  6.3 0.9 %prepare.1 = (bf16[9,8,384]{2,1,0:T(8,128)(2,1)S(1)}, f32[18,8,384]{2,1,0:T(8,128)S(1)}, f32[8,128]{1,0:T(8,128)S(1)}) custom-call(bf16[9,8,384]{2,1,0:T(8,128)(2,1)} %field.1, s32[8,384]{1,0:T(8,128)} %departure.1, f32[8,384]{1,0:T(8,128)} %lat_weight.1, f32[8,384]{1,0:T(8,128)} %lon_weight.1), custom_call_target="tpu_custom_call" | custom-call | tf_op jit(solution)/shard_map/prepare/pallas_call | solution.py:373
  7.2 0.0 collective-permute-done.north
  7.2 3.5 %collective-permute-done.1.south = bf16[9,8,384]{2,1,0:T(8,128)(2,1)S(1)} collective-permute-done((bf16[9,8,384]{2,1,0:T(8,128)(2,1)}, bf16[9,8,384]{2,1,0:T(8,128)(2,1)S(1)}, u32[]{:S(2)}, u32[]{:S(2)}) %collective-permute-start.1) | collective-permute-done | bytes 55328 | tf_op jit(solution)/shard_map/ppermute | solution.py:445
  10.7 2.6 %arrival.1 = bf16[8,88,384]{2,1,0:T(8,128)(2,1)} custom-call(s32[1]{0:T(128)} %bitcast.sector, bf16[9,8,384]{2,1,0:T(8,128)(2,1)S(1)} %get-tuple-element.8.field, bf16[9,8,384]{2,1,0:T(8,128)(2,1)S(1)} %collective-permute-done.north, bf16[9,8,384]{2,1,0:T(8,128)(2,1)S(1)} %collective-permute-done.1.south, f32[18,8,384]{2,1,0:T(8,128)S(1)} %get-tuple-element.9.parts, ...), custom_call_target="tpu_custom_call" | custom-call | tf_op jit(solution)/shard_map/arrival/pallas_call | solution.py:391
  13.3 0.0 copy-start.1
  13.3 11.0 %all-to-all-start = ((bf16[8,88,384]{2,1,0:T(8,128)(2,1)}), bf16[8,88,384]{2,1,0:T(8,128)(2,1)S(1)}, u32[]{:S(2)}, u32[]{:S(2)}) async-start(bf16[8,88,384]{2,1,0:T(8,128)(2,1)} %arrival.1), calls=%async_computation | async-start | bytes 1081344 | tf_op jit(solution)/shard_map/all_to_all | solution.py:451
  24.3 0.0 copy-done
  24.3 0.1 reshape.24
  24.4 0.6 dynamic_slice.8.order
  25.1 0.2 dynamic-slice_reduce_fusion
  25.2 0.1 broadcast_in_dim.29
  25.3 0.2 broadcast_in_dim.30
  25.5 0.1 broadcast_in_dim.31.waves
  25.6 0.9 %fourier.1 = bf16[192,3200]{1,0:T(8,128)(2,1)S(1)} custom-call(s32[192,128]{1,0:T(8,128)S(1)} %broadcast_in_dim.31.waves), custom_call_target="tpu_custom_call" | custom-call | tf_op jit(solution)/shard_map/fourier/pallas_call | solution.py:350
  26.5 0.0 copy-done.1
  26.5 0.1 broadcast_in_dim.33.limits
  26.6 0.6 broadcast_in_dim.34
  27.2 6.7 %all-to-all-done.cycles = bf16[8,88,384]{2,1,0:T(8,128)(2,1)S(1)} async-done(((bf16[8,88,384]{2,1,0:T(8,128)(2,1)}), bf16[8,88,384]{2,1,0:T(8,128)(2,1)S(1)}, u32[]{:S(2)}, u32[]{:S(2)}) %all-to-all-start) | async-done | bytes 540704 | tf_op jit(solution)/shard_map/all_to_all | solution.py:451
  33.9 1.4 %transform.1 = bf16[192,128]{1,0:T(8,128)(2,1)} custom-call(bf16[8,88,384]{2,1,0:T(8,128)(2,1)S(1)} %all-to-all-done.cycles, bf16[192,3200]{1,0:T(8,128)(2,1)S(1)} %fourier.1, s32[192,128]{1,0:T(8,128)S(1)} %broadcast_in_dim.31.waves, s32[1,128]{1,0:T(1,128)S(1)} %broadcast_in_dim.33.limits), custom_call_target="tpu_custom_call" | custom-call | tf_op jit(solution)/shard_map/transform/pallas_call | solution.py:406
  35.3 16.9 %all-to-all-start.1 = ((bf16[96,2,128]{2,1,0:T(2,128)(2,1)}), bf16[96,2,128]{2,1,0:T(2,128)(2,1)S(1)}, u32[]{:S(2)}, u32[]{:S(2)}) async-start(bf16[96,2,128]{2,1,0:T(2,128)(2,1)} %bitcast.1), calls=%async_computation.1 | async-start | bytes 98304 | tf_op jit(solution)/shard_map/all_to_all | solution.py:463
  52.2 0.1 fusion.20
  52.9 0.6 fusion.2
  53.5 3.1 %legendre.1.functions = bf16[768,1024]{1,0:T(8,128)(2,1)S(1)} custom-call(f32[768]{0:T(1024)} %get-tuple-element.14.step_a, f32[768]{0:T(1024)} %get-tuple-element.15.step_c, f32[8,128]{1,0:T(8,128)S(1)} %get-tuple-element.13.cosine, f32[8,128]{1,0:T(8,128)S(1)} %get-tuple-element.12.log_start, f32[8,128]{1,0:T(8,128)S(1)} %get-tuple-element.11.weight), custom_call_target="tpu_custom_call" | custom-call | tf_op jit(solution)/shard_map/legendre/pallas_call | solution.py:361
  56.6 8.6 %all-to-all-done.1 = bf16[96,2,128]{2,1,0:T(2,128)(2,1)S(1)} async-done(((bf16[96,2,128]{2,1,0:T(2,128)(2,1)}), bf16[96,2,128]{2,1,0:T(2,128)(2,1)S(1)}, u32[]{:S(2)}, u32[]{:S(2)}) %all-to-all-start.1) | async-done | bytes 49184 | tf_op jit(solution)/shard_map/all_to_all | solution.py:463
  65.2 1.9 %synthesis.1 = f32[9,2,768]{2,1,0:T(2,128)} custom-call(s32[1]{0:T(128)} %dynamic_slice.8.order, bf16[192,128]{1,0:T(8,128)(2,1)S(1)} %bitcast.9, bf16[768,1024]{1,0:T(8,128)(2,1)S(1)} %legendre.1.functions), custom_call_target="tpu_custom_call" | custom-call | tf_op jit(solution)/shard_map/synthesis/pallas_call | solution.py:421
  (2 shorter events, 0.0 us)
Async XLA Ops:
  0.0 24.3 %copy-start = (s32[768]{0:T(1024)S(1)}, s32[768]{0:T(1024)}, u32[]{:S(2)}) copy-start(s32[768]{0:T(1024)} %param.11) | copy-start | bytes 9220
  0.0 7.2 %collective-permute-start = (bf16[9,8,384]{2,1,0:T(8,128)(2,1)}, bf16[9,8,384]{2,1,0:T(8,128)(2,1)S(1)}, u32[]{:S(2)}, u32[]{:S(2)}) collective-permute-start(bf16[9,8,384]{2,1,0:T(8,128)(2,1)} %field.1), channel_id=1, source_target_pairs={{0,8},{8,16},{16,24},{24,32},{32,40},{40,48},{48,56},{56,64},{64,7... | collective-permute-start | bytes 165896 | tf_op jit(solution)/shard_map/ppermute | solution.py:444
  4.9 5.8 %collective-permute-start.1 = (bf16[9,8,384]{2,1,0:T(8,128)(2,1)}, bf16[9,8,384]{2,1,0:T(8,128)(2,1)S(1)}, u32[]{:S(2)}, u32[]{:S(2)}) collective-permute-start(bf16[9,8,384]{2,1,0:T(8,128)(2,1)} %field.1), channel_id=1, source_target_pairs={{8,0},{16,8},{24,16},{32,24},{40,32},{48,40},{56,48},{64,56},{72,6... | collective-permute-start | bytes 165896 | tf_op jit(solution)/shard_map/ppermute | solution.py:445
  13.3 13.2 %copy-start.1 = (s32[8]{0:T(128)S(1)}, s32[8]{0:T(128)}, u32[]{:S(2)}) copy-start(s32[8]{0:T(128)} %param.10) | copy-start | bytes 100
  13.3 20.6 %all-to-all-start = ((bf16[8,88,384]{2,1,0:T(8,128)(2,1)}), bf16[8,88,384]{2,1,0:T(8,128)(2,1)S(1)}, u32[]{:S(2)}, u32[]{:S(2)}) async-start(bf16[8,88,384]{2,1,0:T(8,128)(2,1)} %arrival.1), calls=%async_computation | async-start | bytes 1081344 | tf_op jit(solution)/shard_map/all_to_all | solution.py:451
  35.3 29.9 %all-to-all-start.1 = ((bf16[96,2,128]{2,1,0:T(2,128)(2,1)}), bf16[96,2,128]{2,1,0:T(2,128)(2,1)S(1)}, u32[]{:S(2)}, u32[]{:S(2)}) async-start(bf16[96,2,128]{2,1,0:T(2,128)(2,1)} %bitcast.1), calls=%async_computation.1 | async-start | bytes 98304 | tf_op jit(solution)/shard_map/all_to_all | solution.py:463

commit v4 on v3

--- a/solution.py
+++ b/solution.py
@@ -11,6 +11,7 @@
 HALO = 4
 LANES = 128
 BLOCK = 32
+GRANT = 16 << 20
 WINDOW = 4 * HALO
 LGAMMA_HALF_THREE = 0.5 * math.log(math.pi) - math.log(2.0)
 SINE = (
@@ -80,7 +81,7 @@
             last = current
             current = fresh
         row = pl.multiple_of(base, BLOCK)
-        for r in range(band_rows):
+        for r in range(band_rows // 2):
             out[pl.ds(row, BLOCK), r * LANES : (r + 1) * LANES] = stage[
                 pl.ds(r, BLOCK, stride=band_rows), :
             ].astype(jnp.bfloat16)
@@ -278,30 +279,47 @@
     out[:, used:] = jnp.zeros((out.shape[0], out.shape[1] - used), jnp.bfloat16)
 
 
-def synthesis_kernel(order, data, functions, out, rows, turned, packed):
+def synthesis_kernel(data, functions, out, turned, packed):
     channels, parts, waves = out.shape
     bands = data.shape[0] // parts
-    band_rows = packed.shape[1] // LANES
-    rows[parts * bands :, :] = jnp.zeros_like(rows[parts * bands :, :])
-    rows[: parts * bands, :] = data[...].astype(jnp.float32)
+    kept = packed.shape[1] // LANES
+    band_rows = 2 * kept
+    source = lax.broadcasted_iota(jnp.int32, (parts * bands, LANES), 0)
+    target = lax.broadcasted_iota(jnp.int32, (parts * bands, LANES), 1)
+    chosen = [
+        (source == parts * band + e).astype(jnp.float32).astype(jnp.bfloat16)
+        for band in (target, bands - 1 - target)
+        for e in range(parts)
+    ]
+    columns = lax.dot_general(
+        data[...],
+        jnp.concatenate(chosen, axis=1),
+        (((0,), (0,)), ((), ())),
+        preferred_element_type=jnp.float32,
+    )
+    for place in range(2 * parts):
+        turned[place] = columns[:, place * LANES : (place + 1) * LANES]
     packed[...] = jnp.zeros_like(packed)
-    step = packed.shape[0] // parts
-    for e in range(parts):
-        turned[e] = rows[pl.ds(e, LANES, stride=parts), :].T
-        for r in range(band_rows):
-            packed[e * step : e * step + channels, r * LANES : (r + 1) * LANES] = turned[
-                e, pl.ds(r, channels, stride=band_rows), :
-            ]
+    step = packed.shape[0] // (2 * parts)
+    for mirror in range(2):
+        for e in range(parts):
+            first = (mirror * parts + e) * step
+            for r in range(kept):
+                row = band_rows - 1 - r if mirror else r
+                packed[first : first + channels, r * LANES : (r + 1) * LANES] = turned[
+                    mirror * parts + e, pl.ds(row, channels, stride=band_rows), :
+                ]
     result = lax.dot_general(
         packed[...].astype(jnp.bfloat16),
         functions[...],
         (((1,), (1,)), ((), ())),
         preferred_element_type=jnp.float32,
     )
-    index = lax.broadcasted_iota(jnp.int32, (channels, waves), 1)
-    inside = index < waves - order[0]
+    even = lax.broadcasted_iota(jnp.int32, (channels, waves), 1) % 2 == 0
     for e in range(parts):
-        out[:, e, :] = jnp.where(inside, result[e * step : e * step + channels, :], 0.0)
+        near_half = result[e * step : e * step + channels, :]
+        far_half = result[(parts + e) * step : (parts + e) * step + channels, :]
+        out[:, e, :] = near_half + jnp.where(even, far_half, -far_half)
 
 
 def legendre_inputs(order, bands, band_rows, waves, total_lat):
@@ -325,9 +343,10 @@
             (before * before - order_real * order_real) / (4.0 * before * before - 1.0), 0.0
         )
     )
+    inside = jnp.arange(1, waves + 1, dtype=jnp.int32) < waves - order
     return (
-        step_a,
-        step_a * step_b,
+        jnp.where(inside, step_a, 0.0),
+        jnp.where(inside, step_a * step_b, 0.0),
         jnp.cos(angles),
         log_start,
         sine * (math.pi / math.sqrt(total_lat)),
@@ -353,6 +372,7 @@
         in_specs=[vmem()],
         out_specs=vmem(),
         name="fourier",
+        compiler_params=pltpu.CompilerParams(vmem_limit_bytes=GRANT),
     )(near(row_waves))
 
 
@@ -360,11 +380,12 @@
     step_a, step_c, *planes = legendre_inputs(order, bands, band_rows, waves, bands * band_rows)
     return pl.pallas_call(
         functools.partial(legendre_kernel, waves=waves, band_rows=band_rows),
-        out_shape=pltpu.VMEM((waves, band_rows * LANES), jnp.bfloat16),
+        out_shape=pltpu.VMEM((waves, band_rows // 2 * LANES), jnp.bfloat16),
         in_specs=[smem(), smem(), vmem(), vmem(), vmem()],
         out_specs=vmem(),
         scratch_shapes=[pltpu.VMEM((BLOCK * band_rows, LANES), jnp.float32)],
         name="legendre",
+        compiler_params=pltpu.CompilerParams(vmem_limit_bytes=GRANT),
     )(step_a, step_c, *map(near, planes))
 
 
@@ -413,23 +434,24 @@
             pltpu.VMEM((channels * band_rows, LANES), jnp.float32),
         ],
         name="transform",
+        compiler_params=pltpu.CompilerParams(vmem_limit_bytes=GRANT),
     )(*map(near, (cycles, fourier, row_waves, limits)))
 
 
-def synthesize(order, data, functions, channels):
+def synthesize(data, functions, channels):
     waves, span = functions.shape
     return pl.pallas_call(
         synthesis_kernel,
         out_shape=jax.ShapeDtypeStruct((channels, 2, waves), jnp.float32),
-        in_specs=[smem(), vmem(), vmem()],
+        in_specs=[vmem()] * 2,
         out_specs=vmem(),
         scratch_shapes=[
-            pltpu.VMEM((2 * LANES, LANES), jnp.float32),
-            pltpu.VMEM((2, LANES, LANES), jnp.float32),
-            pltpu.VMEM((32, span), jnp.float32),
+            pltpu.VMEM((4, LANES, LANES), jnp.float32),
+            pltpu.VMEM((64, span), jnp.float32),
         ],
         name="synthesis",
-    )(order, near(data), near(functions))
+        compiler_params=pltpu.CompilerParams(vmem_limit_bytes=GRANT),
+    )(near(data), near(functions))
 
 
 def shards(prognostic, departure, lat_weight, lon_weight, cycle_waves, wave_order):
@@ -459,13 +481,14 @@
         cycle_waves[None, None, :], (1, LANES // band_rows, band_rows)
     ).reshape(1, LANES)
     fourier = fourier_table(row_waves, total_lon)
+    order = lax.dynamic_slice_in_dim(wave_order, band_index * sectors + sector_index, 1)
+    functions = legendre_table(order, bands, band_rows, waves)
+    cycles, functions = lax.optimization_barrier((cycles, functions))
     masked = transform(cycles, fourier, row_waves, limits, prognostic.shape[0], band_rows)
     data = lax.all_to_all(
         masked.reshape(bands, 2, LANES), "lat", split_axis=0, concat_axis=0, tiled=True
     ).reshape(2 * bands, LANES)
-    order = lax.dynamic_slice_in_dim(wave_order, band_index * sectors + sector_index, 1)
-    functions = legendre_table(order, bands, band_rows, waves)
-    spectral = synthesize(order, data, functions, prognostic.shape[0])
+    spectral = synthesize(data, functions, prognostic.shape[0])
     return spectral.transpose(1, 0, 2)[None]
 
 

time: 67.5 us -> 65.8 us (0.975)
  blocking collectives: 0 us -> 29.3 us
  waiting for transfers between devices: 18.8 us -> 2.94 us
  starting transfers between devices: 34.1 us -> 20.4 us
  Pallas kernels: 10.8 us -> 9.31 us
    all_to_all x0 -> x1, blocking collectives: none -> 29.3 us  [shards(): lax.all_to_all(masked.reshape(bands, 2, LANES), 'lat', split_axis=0, conc...]
    all_to_all x1 -> x0, starting transfers between devices: 16.9 us -> none  [shards(): lax.all_to_all(masked.reshape(bands, 2, LANES), 'lat', split_axis=0, conc...]
    all_to_all x1 -> x0, waiting for transfers between devices: 8.59 us -> none  [shards(): lax.all_to_all(masked.reshape(bands, 2, LANES), 'lat', split_axis=0, conc...]
    all_to_all x1, waiting for transfers between devices: 6.66 us -> 2.38 us  [shards(): lax.all_to_all(arrival, 'lon', split_axis=0, concat_axis=0, tiled=True)]
    ppermute x1, waiting for transfers between devices: 3.49 us -> 0.02 us  [shards(): lax.ppermute(prognostic, 'lat', [(i + 1, i) for i in range(bands - 1)])]
    all_to_all x1, starting transfers between devices: 11 us -> 13.6 us  [shards(): lax.all_to_all(arrival, 'lon', split_axis=0, concat_axis=0, tiled=True)]
    pallas_call x1, Pallas kernels: 1.88 us -> 1.15 us  [synthesize(): pl.pallas_call(synthesis_kernel, out_shape=jax.ShapeDtypeStruct((channels...]
  transfers between devices with their start and end apart: 4 -> 3, of which waited for: 3 -> 2; matrix products, arithmetic and copies ran while one was open for 4% -> 3% of each run, Pallas kernels for 7% -> 7%
where the time goes in v4:
time: 65.8 us; the launch traced here: 65.3 us
  blocking collectives  29.3 us (45%)
  starting transfers between devices  20.4 us (31%)
  Pallas kernels  9.31 us (14%)
  waiting for transfers between devices  2.94 us (4%)
  local copies, waits for them, and re-layouts  1.88 us (3%)
  between operations  1.37 us (2%)
    all_to_all x1, blocking collectives, shards(): lax.all_to_all(masked.reshape(bands, 2, LANES), 'lat', split_axis=0, conc...  29.3 us
    all_to_all x1, starting transfers between devices, shards(): lax.all_to_all(arrival, 'lon', split_axis=0, concat_axis=0, tiled=True)  13.6 us
    ppermute x1, starting transfers between devices, shards(): lax.ppermute(prognostic, 'lat', [(i, i + 1) for i in range(bands - 1)])  5.44 us
    pallas_call x1, Pallas kernels, legendre_table(): pl.pallas_call(functools.partial(legendre_kernel, waves=waves, band_rows=...  2.93 us
    pallas_call x1, Pallas kernels, interpolate(): pl.pallas_call(arrival_kernel, out_shape=pltpu.VMEM((copies, height, sect...  2.62 us
    all_to_all x1, waiting for transfers between devices, shards(): lax.all_to_all(arrival, 'lon', split_axis=0, concat_axis=0, tiled=True)  2.38 us
    ppermute x1, starting transfers between devices, shards(): lax.ppermute(prognostic, 'lat', [(i + 1, i) for i in range(bands - 1)])  1.41 us
  transfers between devices with their start and end apart: 3, of which 2 were waited for; matrix products, arithmetic and copies ran while one was open for 3% of the time, Pallas kernels for 7%

profile of v4, /device:TPU:1, one launch (start us, length us, event | category | flops | bytes accessed | tf_op | source)
XLA Modules:
  0.0 65.3 jit_solution(14945191695530623894)
XLA Ops:
  0.0 0.0 copy-start
  0.0 0.0 copy-start.1
  0.0 1.4 %collective-permute-start.1 = (bf16[9,8,384]{2,1,0:T(8,128)(2,1)}, bf16[9,8,384]{2,1,0:T(8,128)(2,1)S(1)}, u32[]{:S(2)}, u32[]{:S(2)}) collective-permute-start(bf16[9,8,384]{2,1,0:T(8,128)(2,1)} %field.1), channel_id=1, source_target_pairs={{8,0},{16,8},{24,16},{32,24},{40,32},{48,40},{56,48},{64,56},{72,6... | collective-permute-start | bytes 165896 | tf_op jit(solution)/shard_map/ppermute | solution.py:467
  1.4 5.4 %collective-permute-start = (bf16[9,8,384]{2,1,0:T(8,128)(2,1)}, bf16[9,8,384]{2,1,0:T(8,128)(2,1)S(1)}, u32[]{:S(2)}, u32[]{:S(2)}) collective-permute-start(bf16[9,8,384]{2,1,0:T(8,128)(2,1)} %field.1), channel_id=1, source_target_pairs={{0,8},{8,16},{16,24},{24,32},{32,40},{40,48},{48,56},{56,64},{64,7... | collective-permute-start | bytes 165896 | tf_op jit(solution)/shard_map/ppermute | solution.py:466
  6.9 1.0 %prepare.1 = (bf16[9,8,384]{2,1,0:T(8,128)(2,1)S(1)}, f32[18,8,384]{2,1,0:T(8,128)S(1)}, f32[8,128]{1,0:T(8,128)S(1)}) custom-call(bf16[9,8,384]{2,1,0:T(8,128)(2,1)} %field.1, s32[8,384]{1,0:T(8,128)} %departure.1, f32[8,384]{1,0:T(8,128)} %lat_weight.1, f32[8,384]{1,0:T(8,128)} %lon_weight.1), custom_call_target="tpu_custom_call" | custom-call | tf_op jit(solution)/shard_map/prepare/pallas_call | solution.py:394
  7.8 0.0 collective-permute-done.1.south
  7.9 0.5 collective-permute-done.north
  8.4 2.6 %arrival.1 = bf16[8,88,384]{2,1,0:T(8,128)(2,1)} custom-call(s32[1]{0:T(128)} %bitcast.sector, bf16[9,8,384]{2,1,0:T(8,128)(2,1)S(1)} %get-tuple-element.10.field, bf16[9,8,384]{2,1,0:T(8,128)(2,1)S(1)} %collective-permute-done.north, bf16[9,8,384]{2,1,0:T(8,128)(2,1)S(1)} %collective-permute-done.1.south, f32[18,8,384]{2,1,0:T(8,128)S(1)} %get-tuple-element.11.parts, ...), custom_call_target="tpu_custom_call" | custom-call | tf_op jit(solution)/shard_map/arrival/pallas_call | solution.py:412
  11.0 13.6 %all-to-all-start = ((bf16[8,88,384]{2,1,0:T(8,128)(2,1)}), bf16[8,88,384]{2,1,0:T(8,128)(2,1)S(1)}, u32[]{:S(2)}, u32[]{:S(2)}) async-start(bf16[8,88,384]{2,1,0:T(8,128)(2,1)} %arrival.1), calls=%async_computation | async-start | bytes 1081344 | tf_op jit(solution)/shard_map/all_to_all | solution.py:473
  24.6 0.0 copy-done
  24.6 0.1 reshape.24
  24.7 0.6 dynamic_slice.8
  26.6 0.6 broadcast_in_dim.34
  27.2 0.0 copy-done.1
  27.2 0.1 broadcast_in_dim.40.limits
  27.3 0.2 dynamic-slice_reduce_fusion
  27.5 0.1 broadcast_in_dim.36
  27.6 0.2 broadcast_in_dim.37
  27.7 0.1 broadcast_in_dim.38.waves
  27.8 0.9 %fourier.1 = bf16[192,3200]{1,0:T(8,128)(2,1)S(1)} custom-call(s32[192,128]{1,0:T(8,128)S(1)} %broadcast_in_dim.38.waves), custom_call_target="tpu_custom_call" | custom-call | tf_op jit(solution)/shard_map/fourier/pallas_call | solution.py:369
  28.8 0.1 fusion.21
  28.9 2.9 %legendre.1.functions = bf16[768,512]{1,0:T(8,128)(2,1)S(1)} custom-call(f32[768]{0:T(1024)S(1)} %get-tuple-element.19.step_a, f32[768]{0:T(1024)S(1)} %get-tuple-element.18.step_c, f32[8,128]{1,0:T(8,128)S(1)} %get-tuple-element.17.cosine, f32[8,128]{1,0:T(8,128)S(1)} %get-tuple-element.16.log_start, f32[8,128]{1,0:T(8,128)S(1)} %get-tuple-element.15.weight), custom_call_target="tpu_custom_call" | custom-call | tf_op jit(solution)/shard_map/legendre/pallas_call | solution.py:381
  31.8 2.4 %all-to-all-done.cycles = bf16[8,88,384]{2,1,0:T(8,128)(2,1)S(1)} async-done(((bf16[8,88,384]{2,1,0:T(8,128)(2,1)}), bf16[8,88,384]{2,1,0:T(8,128)(2,1)S(1)}, u32[]{:S(2)}, u32[]{:S(2)}) %all-to-all-start) | async-done | bytes 540704 | tf_op jit(solution)/shard_map/all_to_all | solution.py:473
  34.2 0.7 %transform.1 = bf16[192,128]{1,0:T(8,128)(2,1)S(1)} custom-call(bf16[8,88,384]{2,1,0:T(8,128)(2,1)S(1)} %all-to-all-done.cycles, bf16[192,3200]{1,0:T(8,128)(2,1)S(1)} %fourier.1, s32[192,128]{1,0:T(8,128)S(1)} %broadcast_in_dim.38.waves, s32[1,128]{1,0:T(1,128)S(1)} %broadcast_in_dim.40.limits), custom_call_target="tpu_custom_call" | custom-call | tf_op jit(solution)/shard_map/transform/pallas_call | solution.py:427
  34.9 29.3 %all_to_all.10 = bf16[96,2,128]{2,1,0:T(2,128)(2,1)S(1)} all-to-all(bf16[96,2,128]{2,1,0:T(2,128)(2,1)S(1)} %bitcast.11), channel_id=1, replica_groups=mesh['lat'=96,'lon'=8] {'lat'}, dimensions={0} | all-to-all | bytes 98304 | tf_op jit(solution)/shard_map/all_to_all | solution.py:488
  64.2 1.1 %synthesis.1 = f32[9,2,768]{2,1,0:T(2,128)} custom-call(bf16[192,128]{1,0:T(8,128)(2,1)S(1)} %bitcast.10, bf16[768,512]{1,0:T(8,128)(2,1)S(1)} %legendre.1.functions), custom_call_target="tpu_custom_call" | custom-call | tf_op jit(solution)/shard_map/synthesis/pallas_call | solution.py:443
  (3 shorter events, 0.0 us)
Async XLA Ops:
  0.0 24.6 %copy-start = (s32[768]{0:T(1024)S(1)}, s32[768]{0:T(1024)}, u32[]{:S(2)}) copy-start(s32[768]{0:T(1024)} %param.11) | copy-start | bytes 9220
  0.0 27.2 %copy-start.1 = (s32[8]{0:T(128)S(1)}, s32[8]{0:T(128)}, u32[]{:S(2)}) copy-start(s32[8]{0:T(128)} %param.10) | copy-start | bytes 100
  0.0 7.8 %collective-permute-start.1 = (bf16[9,8,384]{2,1,0:T(8,128)(2,1)}, bf16[9,8,384]{2,1,0:T(8,128)(2,1)S(1)}, u32[]{:S(2)}, u32[]{:S(2)}) collective-permute-start(bf16[9,8,384]{2,1,0:T(8,128)(2,1)} %field.1), channel_id=1, source_target_pairs={{8,0},{16,8},{24,16},{32,24},{40,32},{48,40},{56,48},{64,56},{72,6... | collective-permute-start | bytes 165896 | tf_op jit(solution)/shard_map/ppermute | solution.py:467
  1.4 7.0 %collective-permute-start = (bf16[9,8,384]{2,1,0:T(8,128)(2,1)}, bf16[9,8,384]{2,1,0:T(8,128)(2,1)S(1)}, u32[]{:S(2)}, u32[]{:S(2)}) collective-permute-start(bf16[9,8,384]{2,1,0:T(8,128)(2,1)} %field.1), channel_id=1, source_target_pairs={{0,8},{8,16},{16,24},{24,32},{32,40},{40,48},{48,56},{56,64},{64,7... | collective-permute-start | bytes 165896 | tf_op jit(solution)/shard_map/ppermute | solution.py:466
  11.0 23.1 %all-to-all-start = ((bf16[8,88,384]{2,1,0:T(8,128)(2,1)}), bf16[8,88,384]{2,1,0:T(8,128)(2,1)S(1)}, u32[]{:S(2)}, u32[]{:S(2)}) async-start(bf16[8,88,384]{2,1,0:T(8,128)(2,1)} %arrival.1), calls=%async_computation | async-start | bytes 1081344 | tf_op jit(solution)/shard_map/all_to_all | solution.py:473

commit v5 on v4

--- a/solution.py
+++ b/solution.py
@@ -24,7 +24,7 @@
 )
 
 
-def fourier_kernel(waves, out, *, points):
+def fourier_kernel(waves, limits, following, out, bound, line, *, points):
     rows, group = waves.shape[0], 64
     scale = 1.0 / math.sqrt(points)
     row = lax.broadcasted_iota(jnp.int32, (group, LANES), 0)
@@ -64,6 +64,23 @@
         return carry
 
     lax.fori_loop(0, rows // group, block, 0)
+
+    band_rows = limits.shape[1]
+    line[...] = jnp.zeros_like(line)
+    line[:1, :band_rows] = limits[...].astype(jnp.float32)
+    own = line[...]
+    last = following[following.shape[0] - 1].astype(jnp.float32)
+    ahead = last[:, :LANES] * 256.0 + last[:, LANES : 2 * LANES]
+    width = band_rows
+    while width < LANES:
+        own = own + pltpu.roll(own, width, 1)
+        ahead = ahead + pltpu.roll(ahead, width, 1)
+        width *= 2
+    bound[...] = jnp.where(
+        place[:1] % band_rows < HALO,
+        pltpu.roll(own, LANES - HALO, 1)[:1],
+        pltpu.roll(ahead, HALO, 1)[HALO : HALO + 1],
+    )
 
 
 def legendre_kernel(step_a, step_c, cosine, log_start, weight, out, stage, *, waves, band_rows):
@@ -153,38 +170,66 @@
     return [high, middle, rest - middle]
 
 
-def prepare_kernel(field, departure, lat_weight, lon_weight, field_out, parts, planes):
+def pack_kernel(limits, field, departure, lat_weight, lon_weight, out, field_out, own, line):
+    channels = field.shape[0]
     cols = departure.shape[1]
-    field_out[...] = field[...]
-    cell = departure[...]
+    value = field[...]
+    field_out[...] = value
+    out[:channels] = value
+    cell = departure[...].astype(jnp.float32)
     a = lat_weight[...]
     b = lon_weight[...]
-    for d, part in enumerate(spread(cell // (2 * HALO), a) + spread(cell % (2 * HALO), b)):
-        parts[d] = part
-    total = None
-    for p, plane in enumerate([cell.astype(jnp.float32)] + split(a) + split(b)):
-        tall = [plane[:, t * LANES : (t + 1) * LANES] for t in range(cols // LANES)]
-        term = edges(tall, p + 1)
-        total = term if total is None else total + term
-    planes[...] = total
-
-
-def arrival_kernel(sector, field, north, south, parts, planes, out, grid, shifted, stage):
+    for p, plane in enumerate((cell, a, b)):
+        own[p] = plane
+    planes = [v[:HALO] for v in [cell] + split(a) + split(b)]
+    for p in range(0, len(planes) - 1, 2):
+        pair = jnp.concatenate(planes[p : p + 2], axis=0)
+        out[channels + p // 2] = pair.astype(jnp.bfloat16)
+    rows = limits.shape[1]
+    bound = limits[...].astype(jnp.float32)
+    high = jnp.floor(bound * (1.0 / 256.0))
+    line[:HALO] = planes[-1]
+    line[HALO:] = jnp.zeros_like(planes[-1])
+    line[HALO : HALO + 1, :rows] = high
+    line[HALO : HALO + 1, LANES : LANES + rows] = bound - high * 256.0
+    out[channels + len(planes) // 2] = line[...].astype(jnp.bfloat16)
+
+
+def arrival_kernel(place, field, own, following, out, grid, shifted, parts, stage):
     channels, rows, cols = field.shape
     tiles = cols // LANES
     count = 2 * HALO + 1
     used = channels * rows
     tall = rows + 2 * HALO
     lane = lax.broadcasted_iota(jnp.int32, (rows, LANES), 1)
+    row = lax.broadcasted_iota(jnp.int32, (rows, cols), 0)
+    last = jnp.concatenate([place[3]] * tiles, axis=1)
+    pairs = [following[channels + p].astype(jnp.float32) for p in range(4)]
+    ahead = [pairs[p // 2][p % 2 * HALO : (p % 2 + 1) * HALO] for p in range(7)]
+
+    def rows_of(plane, rest):
+        return jnp.concatenate([plane[HALO:], rest], axis=0)
+
+    cell = rows_of(own[0], ahead[0])
+    a = rows_of(own[1], ahead[1] + ahead[2] + ahead[3])
+    b = rows_of(own[2], ahead[4] + ahead[5] + ahead[6])
+    high = jnp.floor(cell * (1.0 / (2 * HALO)))
+    for e, part in enumerate(spread(high, a)):
+        parts[e] = jnp.where((row < HALO) == (row + e < rows), part, part * (1.0 - last))
+    for d, part in enumerate(spread(cell - high * (2 * HALO), b)):
+        parts[count + d] = part
+    total = None
+    for p, plane in enumerate([cell + last * (4 * HALO * HALO)] + split(a) + split(b)):
+        term = edges([plane[:, t * LANES : (t + 1) * LANES] for t in range(tiles)], p + 1)
+        total = term if total is None else total + term
+    planes = total
     for c in range(channels):
-        up = north[c].astype(jnp.float32)[rows - HALO :]
-        mid = field[c].astype(jnp.float32)
-        down = south[c].astype(jnp.float32)[:HALO]
+        here = field[c].astype(jnp.float32)
+        there = following[c].astype(jnp.float32)
         for t in range(tiles):
             span = slice(t * LANES, (t + 1) * LANES)
-            grid[c, t, 0:HALO, :] = up[:, span]
-            grid[c, t, HALO : HALO + rows, :] = mid[:, span]
-            grid[c, t, HALO + rows :, :] = down[:, span]
+            grid[c, t, :rows, :] = here[:, span]
+            grid[c, t, rows:, :] = there[:, span]
 
     def part(first):
         return lambda d, t: parts[first + d, :, t * LANES : (t + 1) * LANES]
@@ -207,15 +252,17 @@
 
     lax.fori_loop(0, channels, channel, 0)
     slots = LANES // WINDOW
-    turn = sector[0] * WINDOW
+    bits = [jnp.concatenate([place[k]] * 2, axis=0) > 0.0 for k in range(3)]
     for g in range(2):
         total = None
         for c in range(g * slots, min((g + 1) * slots, channels)):
             term = edges([grid[c, 0], grid[c, tiles - 1]], c - g * slots)
             total = term if total is None else total + term
         if g == 1:
-            total = total + jnp.concatenate([planes[...], jnp.zeros_like(planes[...])], axis=0)
-        stage[used : used + tall, g * LANES : (g + 1) * LANES] = pltpu.roll(total, turn, 1)
+            total = total + jnp.concatenate([planes, jnp.zeros_like(planes)], axis=0)
+        for k in range(3):
+            total = jnp.where(bits[k], pltpu.roll(total, WINDOW << k, 1), total)
+        stage[used : used + tall, g * LANES : (g + 1) * LANES] = total
     stage[used : used + tall, 2 * LANES :] = jnp.zeros((tall, cols - 2 * LANES), jnp.float32)
     value = stage[...].astype(jnp.bfloat16)
     for copy in range(out.shape[0]):
@@ -250,10 +297,16 @@
         return jnp.where(inner[:height] < 2 * HALO, left, right)
 
     cell, *weights = [window(channels + p, rows) for p in range(7)]
+    last = (cell >= 4 * HALO * HALO).astype(jnp.float32)
+    cell = cell - last * (4 * HALO * HALO)
+    row = lax.broadcasted_iota(jnp.int32, cell.shape, 0)
     a = weights[0] + weights[1] + weights[2]
     b = weights[3] + weights[4] + weights[5]
     high = jnp.floor(cell * (1.0 / (2 * HALO)))
-    row_parts = spread(high, a)
+    row_parts = [
+        jnp.where((row < HALO) == (row + e < rows), part, part * (1.0 - last))
+        for e, part in enumerate(spread(high, a))
+    ]
     col_parts = spread(cell - high * (2 * HALO), b)
     inside = (inner[:rows] >= HALO) & (inner[:rows] < 3 * HALO)
     for c in range(channels):
@@ -274,7 +327,7 @@
     spectrum = lax.dot_general(
         fourier[...], gathered, (((1,), (1,)), ((), ())), preferred_element_type=jnp.float32
     )
-    resolved = waves[:, :used] < limits[:, :used]
+    resolved = waves[:, :used].astype(jnp.float32) < limits[:, :used]
     out[:, :used] = jnp.where(resolved, spectrum, 0.0).astype(jnp.bfloat16)
     out[:, used:] = jnp.zeros((out.shape[0], out.shape[1] - used), jnp.bfloat16)
 
@@ -288,7 +341,7 @@
     target = lax.broadcasted_iota(jnp.int32, (parts * bands, LANES), 1)
     chosen = [
         (source == parts * band + e).astype(jnp.float32).astype(jnp.bfloat16)
-        for band in (target, bands - 1 - target)
+        for band in (target, jnp.where(target == bands - 1, target, bands - 2 - target))
         for e in range(parts)
     ]
     columns = lax.dot_general(
@@ -326,7 +379,8 @@
     spread = lax.optimization_barrier(jnp.broadcast_to(order, (band_rows, LANES)))
     order_real = spread.astype(jnp.float32)
     band = jnp.minimum(lax.broadcasted_iota(jnp.int32, (band_rows, LANES), 1), bands - 1)
-    cycle = band * band_rows + lax.broadcasted_iota(jnp.int32, (band_rows, LANES), 0)
+    cycle = band * band_rows + lax.broadcasted_iota(jnp.int32, (band_rows, LANES), 0) + HALO
+    cycle = cycle % total_lat
     angles = (cycle.astype(jnp.float32) + 0.5) * (math.pi / total_lat)
     sine = jnp.sin(angles)
     log_start = (
@@ -365,15 +419,19 @@
     return pl.BlockSpec(memory_space=pltpu.VMEM)
 
 
-def fourier_table(row_waves, points):
+def fourier_table(row_waves, limits, following, points):
     return pl.pallas_call(
         functools.partial(fourier_kernel, points=points),
-        out_shape=pltpu.VMEM((row_waves.shape[0], points + LANES), jnp.bfloat16),
-        in_specs=[vmem()],
-        out_specs=vmem(),
+        out_shape=(
+            pltpu.VMEM((row_waves.shape[0], points + LANES), jnp.bfloat16),
+            pltpu.VMEM((1, LANES), jnp.float32),
+        ),
+        in_specs=[vmem()] * 3,
+        out_specs=(vmem(),) * 2,
+        scratch_shapes=[pltpu.VMEM((following.shape[1], LANES), jnp.float32)],
         name="fourier",
         compiler_params=pltpu.CompilerParams(vmem_limit_bytes=GRANT),
-    )(near(row_waves))
+    )(*map(near, (row_waves, limits, following)))
 
 
 def legendre_table(order, bands, band_rows, waves):
@@ -389,38 +447,41 @@
     )(step_a, step_c, *map(near, planes))
 
 
-def prepare(prognostic, departure, lat_weight, lon_weight):
-    _, band_rows, sector_cols = prognostic.shape
+def pack(limits, prognostic, departure, lat_weight, lon_weight):
+    channels, band_rows, sector_cols = prognostic.shape
     return pl.pallas_call(
-        prepare_kernel,
+        pack_kernel,
         out_shape=(
+            pltpu.VMEM((channels + 4, band_rows, sector_cols), jnp.bfloat16),
             pltpu.VMEM(prognostic.shape, jnp.bfloat16),
-            pltpu.VMEM((2 * (2 * HALO + 1), band_rows, sector_cols), jnp.float32),
-            pltpu.VMEM((band_rows, LANES), jnp.float32),
+            pltpu.VMEM((3, band_rows, sector_cols), jnp.float32),
         ),
-        in_specs=[vmem()] * 4,
+        in_specs=[vmem()] * 5,
         out_specs=(vmem(),) * 3,
-        name="prepare",
-    )(prognostic, departure, lat_weight, lon_weight)
-
-
-def interpolate(sector, field, north, south, parts, planes, copies):
+        scratch_shapes=[pltpu.VMEM((band_rows, sector_cols), jnp.float32)],
+        name="pack",
+    )(limits, prognostic, departure, lat_weight, lon_weight)
+
+
+def interpolate(place, field, own, following, copies):
     channels, band_rows, sector_cols = field.shape
     tall = band_rows + 2 * HALO
     tiles = sector_cols // LANES
     height = channels * band_rows + tall
+    count = 2 * HALO + 1
     return pl.pallas_call(
         arrival_kernel,
         out_shape=pltpu.VMEM((copies, height, sector_cols), jnp.bfloat16),
-        in_specs=[smem()] + [vmem()] * 5,
+        in_specs=[vmem()] * 4,
         out_specs=vmem(),
         scratch_shapes=[
             pltpu.VMEM((channels, tiles, tall, LANES), jnp.float32),
-            pltpu.VMEM((2 * HALO + 1, tiles, tall, LANES), jnp.float32),
+            pltpu.VMEM((count, tiles, tall, LANES), jnp.float32),
+            pltpu.VMEM((2 * count, band_rows, sector_cols), jnp.float32),
             pltpu.VMEM((height, sector_cols), jnp.float32),
         ],
         name="arrival",
-    )(sector, *map(near, (field, north, south, parts, planes)))
+    )(*map(near, (place, field, own, following)))
 
 
 def transform(cycles, fourier, row_waves, limits, channels, band_rows):
@@ -463,13 +524,15 @@
     band_index = lax.axis_index("lat")
     sector_index = lax.axis_index("lon")
 
-    north = lax.ppermute(prognostic, "lat", [(i, i + 1) for i in range(bands - 1)])
-    south = lax.ppermute(prognostic, "lat", [(i + 1, i) for i in range(bands - 1)])
-
-    field, parts, planes = prepare(prognostic, departure, lat_weight, lon_weight)
-    arrival = interpolate(
-        sector_index.astype(jnp.int32).reshape(1), field, north, south, parts, planes, sectors
-    )
+    packed, field, own = pack(
+        cycle_waves[None], prognostic, departure, lat_weight, lon_weight
+    )
+    following = lax.ppermute(packed, "lat", [((i + 1) % bands, i) for i in range(bands)])
+    number = lax.broadcasted_iota(jnp.int32, (4, band_rows, LANES), 0)
+    place = jnp.where(
+        number < 3, (sector_index >> number) & 1, (band_index == bands - 1).astype(jnp.int32)
+    ).astype(jnp.float32)
+    arrival = interpolate(place, field, own, following, sectors)
     cycles = lax.all_to_all(arrival, "lon", split_axis=0, concat_axis=0, tiled=True)
 
     slot_waves = wave_order.reshape(bands, sectors)
@@ -477,10 +540,7 @@
     row_waves = jnp.broadcast_to(own_waves[:, :, None], (bands, 2, LANES)).reshape(
         2 * bands, LANES
     )
-    limits = jnp.broadcast_to(
-        cycle_waves[None, None, :], (1, LANES // band_rows, band_rows)
-    ).reshape(1, LANES)
-    fourier = fourier_table(row_waves, total_lon)
+    fourier, limits = fourier_table(row_waves, cycle_waves[None], following, total_lon)
     order = lax.dynamic_slice_in_dim(wave_order, band_index * sectors + sector_index, 1)
     functions = legendre_table(order, bands, band_rows, waves)
     cycles, functions = lax.optimization_barrier((cycles, functions))

time: 65.8 us -> 63.6 us (0.967)
  blocking collectives: 29.3 us -> 22.6 us
  starting transfers between devices: 20.4 us -> 24 us
    ppermute x2 -> x1, starting transfers between devices: 6.86 us -> 18 us  [shards(): lax.ppermute(packed, 'lat', [((i + 1) % bands, i) for i in range(bands)])]
    all_to_all x1, starting transfers between devices: 13.6 us -> 5.96 us  [shards(): lax.all_to_all(arrival, 'lon', split_axis=0, concat_axis=0, tiled=True)]
    all_to_all x1, blocking collectives: 29.3 us -> 22.6 us  [shards(): lax.all_to_all(masked.reshape(bands, 2, LANES), 'lat', split_axis=0, conc...]
    ppermute x2 -> x1, waiting for transfers between devices: 0.56 us -> 1.33 us  [shards(): lax.ppermute(packed, 'lat', [((i + 1) % bands, i) for i in range(bands)])]
  transfers between devices with their start and end apart: 3 -> 2, of which waited for: 2 -> 2; matrix products, arithmetic and copies ran while one was open for 3% -> 3% of each run, Pallas kernels for 7% -> 7%
where the time goes in v5:
time: 63.6 us; the launch traced here: 63.2 us
  starting transfers between devices  24 us (38%)
  blocking collectives  22.6 us (36%)
  Pallas kernels  9.8 us (15%)
  waiting for transfers between devices  3.37 us (5%)
  local copies, waits for them, and re-layouts  1.81 us (3%)
  between operations  1.41 us (2%)
    all_to_all x1, blocking collectives, shards(): lax.all_to_all(masked.reshape(bands, 2, LANES), 'lat', split_axis=0, conc...  22.6 us
    ppermute x1, starting transfers between devices, shards(): lax.ppermute(packed, 'lat', [((i + 1) % bands, i) for i in range(bands)])  18 us
    all_to_all x1, starting transfers between devices, shards(): lax.all_to_all(arrival, 'lon', split_axis=0, concat_axis=0, tiled=True)  5.96 us
    pallas_call x1, Pallas kernels, legendre_table(): pl.pallas_call(functools.partial(legendre_kernel, waves=waves, band_rows=...  2.93 us
    pallas_call x1, Pallas kernels, interpolate(): pl.pallas_call(arrival_kernel, out_shape=pltpu.VMEM((copies, height, sect...  2.86 us
    all_to_all x1, waiting for transfers between devices, shards(): lax.all_to_all(arrival, 'lon', split_axis=0, concat_axis=0, tiled=True)  2.04 us
    ppermute x1, waiting for transfers between devices, shards(): lax.ppermute(packed, 'lat', [((i + 1) % bands, i) for i in range(bands)])  1.33 us
  transfers between devices with their start and end apart: 2, of which 2 were waited for; matrix products, arithmetic and copies ran while one was open for 3% of the time, Pallas kernels for 7%

profile of v5, /device:TPU:1, one launch (start us, length us, event | category | flops | bytes accessed | tf_op | source)
XLA Modules:
  0.0 63.2 jit_solution(4587851234146566465)
XLA Ops:
  0.0 0.0 copy-start.1
  0.0 0.9 %pack.1 = (bf16[13,8,384]{2,1,0:T(8,128)(2,1)S(1)}, bf16[9,8,384]{2,1,0:T(8,128)(2,1)S(1)}, f32[3,8,384]{2,1,0:T(8,128)S(1)}) custom-call(s32[1,8]{1,0:T(1,128)} %bitcast.12, bf16[9,8,384]{2,1,0:T(8,128)(2,1)} %field.1, s32[8,384]{1,0:T(8,128)} %departure.1, f32[8,384]{1,0:T(8,128)} %lat_weight.1, f32[8,384]{1,0:T(8,128)} %lon_weight.1), custom_call_target="tpu_custom_call" | custom-call | tf_op jit(solution)/shard_map/pack/pallas_call | solution.py:452
  0.9 18.0 %collective-permute-start = (bf16[13,8,384]{2,1,0:T(8,128)(2,1)S(1)}, bf16[13,8,384]{2,1,0:T(8,128)(2,1)S(1)}, u32[]{:S(2)}, u32[]{:S(2)}) collective-permute-start(bf16[13,8,384]{2,1,0:T(8,128)(2,1)S(1)} %get-tuple-element.14), channel_id=1, source_target_pairs={{8,0},{16,8},{24,16},{32,24},{40,32},{48,40},{56,48},{64,56},{72,6... | collective-permute-start | bytes 239624 | tf_op jit(solution)/shard_map/ppermute | solution.py:530
  18.9 0.1 select_convert_fusion.place
  19.0 1.3 %collective-permute-done.following = bf16[13,8,384]{2,1,0:T(8,128)(2,1)S(1)} collective-permute-done((bf16[13,8,384]{2,1,0:T(8,128)(2,1)S(1)}, bf16[13,8,384]{2,1,0:T(8,128)(2,1)S(1)}, u32[]{:S(2)}, u32[]{:S(2)}) %collective-permute-start) | collective-permute-done | bytes 79904 | tf_op jit(solution)/shard_map/ppermute | solution.py:530
  20.3 2.9 %arrival.1 = bf16[8,88,384]{2,1,0:T(8,128)(2,1)} custom-call(f32[4,8,128]{2,1,0:T(8,128)S(1)} %select_convert_fusion.place, bf16[9,8,384]{2,1,0:T(8,128)(2,1)S(1)} %get-tuple-element.12.field, f32[3,8,384]{2,1,0:T(8,128)S(1)} %get-tuple-element.13.own, bf16[13,8,384]{2,1,0:T(8,128)(2,1)S(1)} %collective-permute-done.following), custom_call_target="tpu_custom_call" | custom-call | tf_op jit(solution)/shard_map/arrival/pallas_call | solution.py:472
  23.2 0.0 copy-start
  23.2 6.0 %all-to-all-start = ((bf16[8,88,384]{2,1,0:T(8,128)(2,1)}), bf16[8,88,384]{2,1,0:T(8,128)(2,1)S(1)}, u32[]{:S(2)}, u32[]{:S(2)}) async-start(bf16[8,88,384]{2,1,0:T(8,128)(2,1)} %arrival.1), calls=%async_computation | async-start | bytes 1081344 | tf_op jit(solution)/shard_map/all_to_all | solution.py:536
  29.2 0.0 copy-done.1
  29.2 0.1 reshape.13
  29.3 0.6 dynamic_slice.8
  31.1 0.6 %broadcast_in_dim.36 = s32[8,128]{1,0:T(8,128)S(1)} broadcast(s32[]{:T(128)} %bitcast.4), dimensions={} | broadcast | bytes 4100 | tf_op jit(solution)/shard_map/broadcast_in_dim | solution.py:379
  31.8 0.2 dynamic-slice_reduce_fusion
  32.0 0.1 broadcast_in_dim.38
  32.1 0.2 broadcast_in_dim.39
  32.3 0.1 broadcast_multiply_fusion
  32.3 2.9 %legendre.1.functions = bf16[768,512]{1,0:T(8,128)(2,1)S(1)} custom-call(f32[768]{0:T(1024)S(1)} %get-tuple-element.23.step_a, f32[768]{0:T(1024)S(1)} %get-tuple-element.22.step_c, f32[8,128]{1,0:T(8,128)S(1)} %get-tuple-element.21.cosine, f32[8,128]{1,0:T(8,128)S(1)} %get-tuple-element.20.log_start, f32[8,128]{1,0:T(8,128)S(1)} %get-tuple-element.19.weight), custom_call_target="tpu_custom_call" | custom-call | tf_op jit(solution)/shard_map/legendre/pallas_call | solution.py:439
  35.3 0.1 broadcast_in_dim.40.waves
  35.4 0.0 copy-done
  35.4 1.3 %fourier.1 = (bf16[192,3200]{1,0:T(8,128)(2,1)S(1)}, f32[1,128]{1,0:T(1,128)S(1)}) custom-call(s32[192,128]{1,0:T(8,128)S(1)} %broadcast_in_dim.40.waves, s32[1,8]{1,0:T(1,128)S(1)} %bitcast.13, bf16[13,8,384]{2,1,0:T(8,128)(2,1)S(1)} %collective-permute-done.following), custom_call_target="tpu_custom_call" | custom-call | tf_op jit(solution)/shard_map/fourier/pallas_call | solution.py:423
  36.6 2.0 %all-to-all-done.cycles = bf16[8,88,384]{2,1,0:T(8,128)(2,1)S(1)} async-done(((bf16[8,88,384]{2,1,0:T(8,128)(2,1)}), bf16[8,88,384]{2,1,0:T(8,128)(2,1)S(1)}, u32[]{:S(2)}, u32[]{:S(2)}) %all-to-all-start) | async-done | bytes 540704 | tf_op jit(solution)/shard_map/all_to_all | solution.py:536
  38.7 0.7 %transform.1 = bf16[192,128]{1,0:T(8,128)(2,1)S(1)} custom-call(bf16[8,88,384]{2,1,0:T(8,128)(2,1)S(1)} %all-to-all-done.cycles, bf16[192,3200]{1,0:T(8,128)(2,1)S(1)} %get-tuple-element.16.fourier, s32[192,128]{1,0:T(8,128)S(1)} %broadcast_in_dim.40.waves, f32[1,128]{1,0:T(1,128)S(1)} %get-tuple-element.17.limits), custom_call_target="tpu_custom_call" | custom-call | tf_op jit(solution)/shard_map/transform/pallas_call | solution.py:488
  39.4 22.6 %all_to_all.10 = bf16[96,2,128]{2,1,0:T(2,128)(2,1)S(1)} all-to-all(bf16[96,2,128]{2,1,0:T(2,128)(2,1)S(1)} %bitcast.11), channel_id=1, replica_groups=mesh['lat'=96,'lon'=8] {'lat'}, dimensions={0} | all-to-all | bytes 98304 | tf_op jit(solution)/shard_map/all_to_all | solution.py:548
  62.0 1.1 %synthesis.1 = f32[9,2,768]{2,1,0:T(2,128)} custom-call(bf16[192,128]{1,0:T(8,128)(2,1)S(1)} %bitcast.10, bf16[768,512]{1,0:T(8,128)(2,1)S(1)} %legendre.1.functions), custom_call_target="tpu_custom_call" | custom-call | tf_op jit(solution)/shard_map/synthesis/pallas_call | solution.py:504
  (4 shorter events, 0.0 us)
Async XLA Ops:
  0.0 29.2 %copy-start.1 = (s32[768]{0:T(1024)S(1)}, s32[768]{0:T(1024)}, u32[]{:S(2)}) copy-start(s32[768]{0:T(1024)} %param.11) | copy-start | bytes 9220
  0.9 19.5 %collective-permute-start = (bf16[13,8,384]{2,1,0:T(8,128)(2,1)S(1)}, bf16[13,8,384]{2,1,0:T(8,128)(2,1)S(1)}, u32[]{:S(2)}, u32[]{:S(2)}) collective-permute-start(bf16[13,8,384]{2,1,0:T(8,128)(2,1)S(1)} %get-tuple-element.14), channel_id=1, source_target_pairs={{8,0},{16,8},{24,16},{32,24},{40,32},{48,40},{56,48},{64,56},{72,6... | collective-permute-start | bytes 239624 | tf_op jit(solution)/shard_map/ppermute | solution.py:530
  23.2 12.2 %copy-start = (s32[8]{0:T(128)S(1)}, s32[8]{0:T(128)}, u32[]{:S(2)}) copy-start(s32[8]{0:T(128)} %param.10) | copy-start | bytes 100
  23.2 15.5 %all-to-all-start = ((bf16[8,88,384]{2,1,0:T(8,128)(2,1)}), bf16[8,88,384]{2,1,0:T(8,128)(2,1)S(1)}, u32[]{:S(2)}, u32[]{:S(2)}) async-start(bf16[8,88,384]{2,1,0:T(8,128)(2,1)} %arrival.1), calls=%async_computation | async-start | bytes 1081344 | tf_op jit(solution)/shard_map/all_to_all | solution.py:536

commit v6 on v5

--- a/solution.py
+++ b/solution.py
@@ -92,10 +92,17 @@
         current, last, log_scale = carry
         base = t * BLOCK
         size = jnp.exp(log_scale + start) * scale
-        for u in range(BLOCK):
+        for u in range(0, BLOCK, 2):
+            first_a = step_a[base + u] * cos
+            second_a = step_a[base + u + 1] * cos
+            first_c = step_c[base + u]
+            middle = first_a * current - first_c * last
+            fresh = (second_a * first_a - step_c[base + u + 1]) * current - (
+                second_a * first_c
+            ) * last
             stage[band_rows * u : band_rows * (u + 1), :] = current * size
-            fresh = (step_a[base + u] * cos) * current - step_c[base + u] * last
-            last = current
+            stage[band_rows * (u + 1) : band_rows * (u + 2), :] = middle * size
+            last = middle
             current = fresh
         row = pl.multiple_of(base, BLOCK)
         for r in range(band_rows // 2):
@@ -234,10 +241,10 @@
     def part(first):
         return lambda d, t: parts[first + d, :, t * LANES : (t + 1) * LANES]
 
-    def channel(c, carry):
+    for c in range(channels):
         sums = stencil(
             lambda: [grid[c, t] for t in range(tiles)],
-            shifted,
+            shifted.at[c % 2],
             part(0),
             part(count),
             tiles,
@@ -247,10 +254,7 @@
         sums[-1] = jnp.where(lane >= LANES - HALO, 0.0, sums[-1])
         for t in range(tiles):
             span = slice(t * LANES, (t + 1) * LANES)
-            stage[pl.ds(pl.multiple_of(c * rows, rows), rows), span] = sums[t]
-        return carry
-
-    lax.fori_loop(0, channels, channel, 0)
+            stage[c * rows : (c + 1) * rows, span] = sums[t]
     slots = LANES // WINDOW
     bits = [jnp.concatenate([place[k]] * 2, axis=0) > 0.0 for k in range(3)]
     for g in range(2):
@@ -476,7 +480,7 @@
         out_specs=vmem(),
         scratch_shapes=[
             pltpu.VMEM((channels, tiles, tall, LANES), jnp.float32),
-            pltpu.VMEM((count, tiles, tall, LANES), jnp.float32),
+            pltpu.VMEM((2, count, tiles, tall, LANES), jnp.float32),
             pltpu.VMEM((2 * count, band_rows, sector_cols), jnp.float32),
             pltpu.VMEM((height, sector_cols), jnp.float32),
         ],
@@ -532,16 +536,17 @@
     place = jnp.where(
         number < 3, (sector_index >> number) & 1, (band_index == bands - 1).astype(jnp.int32)
     ).astype(jnp.float32)
+    slot_waves = wave_order.reshape(bands, sectors)
+    own_waves = lax.dynamic_slice_in_dim(slot_waves, sector_index, 1, axis=1)
+    order = lax.dynamic_slice_in_dim(wave_order, band_index * sectors + sector_index, 1)
+    following, own_waves, order = lax.optimization_barrier((following, own_waves, order))
     arrival = interpolate(place, field, own, following, sectors)
     cycles = lax.all_to_all(arrival, "lon", split_axis=0, concat_axis=0, tiled=True)
 
-    slot_waves = wave_order.reshape(bands, sectors)
-    own_waves = lax.dynamic_slice_in_dim(slot_waves, sector_index, 1, axis=1)
     row_waves = jnp.broadcast_to(own_waves[:, :, None], (bands, 2, LANES)).reshape(
         2 * bands, LANES
     )
     fourier, limits = fourier_table(row_waves, cycle_waves[None], following, total_lon)
-    order = lax.dynamic_slice_in_dim(wave_order, band_index * sectors + sector_index, 1)
     functions = legendre_table(order, bands, band_rows, waves)
     cycles, functions = lax.optimization_barrier((cycles, functions))
     masked = transform(cycles, fourier, row_waves, limits, prognostic.shape[0], band_rows)

time: 63.6 us -> 62.6 us (0.984)
  Pallas kernels: 9.8 us -> 8.21 us
  local copies, waits for them, and re-layouts: 1.81 us -> 3.08 us
  starting transfers between devices: 24 us -> 23.3 us
    all_to_all x1, waiting for transfers between devices: 2.04 us -> 3.54 us  [shards(): lax.all_to_all(arrival, 'lon', split_axis=0, concat_axis=0, tiled=True)]
    ppermute x1, waiting for transfers between devices: 1.33 us -> 0.01 us  [shards(): lax.ppermute(packed, 'lat', [((i + 1) % bands, i) for i in range(bands)])]
    pallas_call x1, Pallas kernels: 2.86 us -> 2.01 us  [interpolate(): pl.pallas_call(arrival_kernel, out_shape=pltpu.VMEM((copies, height, sect...]
    pallas_call x1, Pallas kernels: 2.93 us -> 2.2 us  [legendre_table(): pl.pallas_call(functools.partial(legendre_kernel, waves=waves, band_rows=...]
    all_to_all x1, starting transfers between devices: 5.96 us -> 5.25 us  [shards(): lax.all_to_all(arrival, 'lon', split_axis=0, concat_axis=0, tiled=True)]
    reshape x1, local copies, waits for them, and re-layouts: 0.08 us -> 0.77 us  [shards(): slot_waves = wave_order.reshape(bands, sectors)]
    dynamic_slice x1, local copies, waits for them, and re-layouts: 0.59 us -> 1.27 us  [shards(): lax.dynamic_slice_in_dim(wave_order, band_index * sectors + sector_index, 1)]
  transfers between devices with their start and end apart: 2 -> 2, of which waited for: 2 -> 1; matrix products, arithmetic and copies ran while one was open for 3% -> 5% of each run, Pallas kernels for 7% -> 6%
where the time goes in v6:
time: 62.6 us; the launch traced here: 62.2 us
  starting transfers between devices  23.3 us (37%)
  blocking collectives  22.4 us (36%)
  Pallas kernels  8.21 us (13%)
  waiting for transfers between devices  3.54 us (6%)
  local copies, waits for them, and re-layouts  3.08 us (5%)
  between operations  1.42 us (2%)
    all_to_all x1, blocking collectives, shards(): lax.all_to_all(masked.reshape(bands, 2, LANES), 'lat', split_axis=0, conc...  22.4 us
    ppermute x1, starting transfers between devices, shards(): lax.ppermute(packed, 'lat', [((i + 1) % bands, i) for i in range(bands)])  18 us
    all_to_all x1, starting transfers between devices, shards(): lax.all_to_all(arrival, 'lon', split_axis=0, concat_axis=0, tiled=True)  5.25 us
    all_to_all x1, waiting for transfers between devices, shards(): lax.all_to_all(arrival, 'lon', split_axis=0, concat_axis=0, tiled=True)  3.54 us
    pallas_call x1, Pallas kernels, legendre_table(): pl.pallas_call(functools.partial(legendre_kernel, waves=waves, band_rows=...  2.2 us
    pallas_call x1, Pallas kernels, interpolate(): pl.pallas_call(arrival_kernel, out_shape=pltpu.VMEM((copies, height, sect...  2.01 us
    dynamic_slice x1, local copies, waits for them, and re-layouts, shards(): lax.dynamic_slice_in_dim(wave_order, band_index * sectors + sector_index, 1)  1.27 us
    pallas_call x1, Pallas kernels, fourier_table(): pl.pallas_call(functools.partial(fourier_kernel, points=points), out_shap...  1.26 us
  transfers between devices with their start and end apart: 2, of which 1 were waited for; matrix products, arithmetic and copies ran while one was open for 5% of the time, Pallas kernels for 6%

profile of v6, /device:TPU:1, one launch (start us, length us, event | category | flops | bytes accessed | tf_op | source)
XLA Modules:
  0.0 62.2 jit_solution(12390482485651789838)
XLA Ops:
  0.0 0.0 copy-start
  0.0 0.9 %pack.1 = (bf16[13,8,384]{2,1,0:T(8,128)(2,1)S(1)}, bf16[9,8,384]{2,1,0:T(8,128)(2,1)S(1)}, f32[3,8,384]{2,1,0:T(8,128)S(1)}) custom-call(s32[1,8]{1,0:T(1,128)} %bitcast.12, bf16[9,8,384]{2,1,0:T(8,128)(2,1)} %field.1, s32[8,384]{1,0:T(8,128)} %departure.1, f32[8,384]{1,0:T(8,128)} %lat_weight.1, f32[8,384]{1,0:T(8,128)} %lon_weight.1), custom_call_target="tpu_custom_call" | custom-call | tf_op jit(solution)/shard_map/pack/pallas_call | solution.py:456
  0.9 18.0 %collective-permute-start = (bf16[13,8,384]{2,1,0:T(8,128)(2,1)S(1)}, bf16[13,8,384]{2,1,0:T(8,128)(2,1)S(1)}, u32[]{:S(2)}, u32[]{:S(2)}) collective-permute-start(bf16[13,8,384]{2,1,0:T(8,128)(2,1)S(1)} %get-tuple-element.17), channel_id=1, source_target_pairs={{8,0},{16,8},{24,16},{32,24},{40,32},{48,40},{56,48},{64,56},{72,6... | collective-permute-start | bytes 239624 | tf_op jit(solution)/shard_map/ppermute | solution.py:534
  18.9 0.8 %reshape.13 = s32[96,8]{1,0:T(8,128)S(1)} reshape(s32[768]{0:T(1024)} %param.11) | data formatting | bytes 6144 | tf_op jit(solution)/shard_map/reshape | solution.py:539
  19.7 1.3 %dynamic_slice.7 = s32[1]{0:T(128)} dynamic-slice(s32[768]{0:T(1024)} %param.11, s32[]{:T(128)S(6)} %select_n.30), dynamic_slice_sizes={1} | dynamic-slice | bytes 12 | tf_op jit(solution)/shard_map/dynamic_slice | solution.py:541
  21.0 0.1 select_convert_fusion.place
  21.1 0.1 constant_dynamic-slice_fusion
  21.1 0.0 collective-permute-done.following
  21.2 2.0 %arrival.1 = bf16[8,88,384]{2,1,0:T(8,128)(2,1)} custom-call(f32[4,8,128]{2,1,0:T(8,128)S(1)} %select_convert_fusion.place, bf16[9,8,384]{2,1,0:T(8,128)(2,1)S(1)} %get-tuple-element.15.field, f32[3,8,384]{2,1,0:T(8,128)S(1)} %get-tuple-element.16.own, bf16[13,8,384]{2,1,0:T(8,128)(2,1)S(1)} %collective-permute-done.following), custom_call_target="tpu_custom_call" | custom-call | tf_op jit(solution)/shard_map/arrival/pallas_call | solution.py:476
  23.2 5.3 %all-to-all-start = ((bf16[8,88,384]{2,1,0:T(8,128)(2,1)}), bf16[8,88,384]{2,1,0:T(8,128)(2,1)S(1)}, u32[]{:S(2)}, u32[]{:S(2)}) async-start(bf16[8,88,384]{2,1,0:T(8,128)(2,1)} %arrival.1), calls=%async_computation | async-start | bytes 1081344 | tf_op jit(solution)/shard_map/all_to_all | solution.py:544
  29.7 0.1 reduce
  29.8 0.7 %broadcast_in_dim.36 = s32[8,128]{1,0:T(8,128)S(1)} broadcast(s32[]{:T(128)} %bitcast.4), dimensions={} | broadcast | bytes 4100 | tf_op jit(solution)/shard_map/broadcast_in_dim | solution.py:383
  30.5 0.1 broadcast_in_dim.38
  30.6 0.1 broadcast_in_dim.39
  30.7 0.1 broadcast_in_dim.40.waves
  30.8 0.0 copy-done
  30.8 1.3 %fourier.1 = (bf16[192,3200]{1,0:T(8,128)(2,1)S(1)}, f32[1,128]{1,0:T(1,128)S(1)}) custom-call(s32[192,128]{1,0:T(8,128)S(1)} %broadcast_in_dim.40.waves, s32[1,8]{1,0:T(1,128)S(1)} %bitcast.13, bf16[13,8,384]{2,1,0:T(8,128)(2,1)S(1)} %collective-permute-done.following), custom_call_target="tpu_custom_call" | custom-call | tf_op jit(solution)/shard_map/fourier/pallas_call | solution.py:427
  32.1 0.1 broadcast_multiply_fusion
  32.2 2.2 %legendre.1.functions = bf16[768,512]{1,0:T(8,128)(2,1)S(1)} custom-call(f32[768]{0:T(1024)S(1)} %get-tuple-element.29.step_a, f32[768]{0:T(1024)S(1)} %get-tuple-element.28.step_c, f32[8,128]{1,0:T(8,128)S(1)} %get-tuple-element.27.cosine, f32[8,128]{1,0:T(8,128)S(1)} %get-tuple-element.26.log_start, f32[8,128]{1,0:T(8,128)S(1)} %get-tuple-element.25.weight), custom_call_target="tpu_custom_call" | custom-call | tf_op jit(solution)/shard_map/legendre/pallas_call | solution.py:443
  34.4 3.5 %all-to-all-done.cycles = bf16[8,88,384]{2,1,0:T(8,128)(2,1)S(1)} async-done(((bf16[8,88,384]{2,1,0:T(8,128)(2,1)}), bf16[8,88,384]{2,1,0:T(8,128)(2,1)S(1)}, u32[]{:S(2)}, u32[]{:S(2)}) %all-to-all-start) | async-done | bytes 540704 | tf_op jit(solution)/shard_map/all_to_all | solution.py:544
  37.9 0.7 %transform.1 = bf16[192,128]{1,0:T(8,128)(2,1)S(1)} custom-call(bf16[8,88,384]{2,1,0:T(8,128)(2,1)S(1)} %all-to-all-done.cycles, bf16[192,3200]{1,0:T(8,128)(2,1)S(1)} %get-tuple-element.22.fourier, s32[192,128]{1,0:T(8,128)S(1)} %broadcast_in_dim.40.waves, f32[1,128]{1,0:T(1,128)S(1)} %get-tuple-element.23.limits), custom_call_target="tpu_custom_call" | custom-call | tf_op jit(solution)/shard_map/transform/pallas_call | solution.py:492
  38.7 22.4 %all_to_all.10 = bf16[96,2,128]{2,1,0:T(2,128)(2,1)S(1)} all-to-all(bf16[96,2,128]{2,1,0:T(2,128)(2,1)S(1)} %bitcast.11), channel_id=1, replica_groups=mesh['lat'=96,'lon'=8] {'lat'}, dimensions={0} | all-to-all | bytes 98304 | tf_op jit(solution)/shard_map/all_to_all | solution.py:553
  61.0 1.1 %synthesis.1 = f32[9,2,768]{2,1,0:T(2,128)} custom-call(bf16[192,128]{1,0:T(8,128)(2,1)S(1)} %bitcast.10, bf16[768,512]{1,0:T(8,128)(2,1)S(1)} %legendre.1.functions), custom_call_target="tpu_custom_call" | custom-call | tf_op jit(solution)/shard_map/synthesis/pallas_call | solution.py:508
  (4 shorter events, 0.0 us)
Async XLA Ops:
  0.0 30.8 %copy-start = (s32[8]{0:T(128)S(1)}, s32[8]{0:T(128)}, u32[]{:S(2)}) copy-start(s32[8]{0:T(128)} %param.10) | copy-start | bytes 100
  0.9 20.3 %collective-permute-start = (bf16[13,8,384]{2,1,0:T(8,128)(2,1)S(1)}, bf16[13,8,384]{2,1,0:T(8,128)(2,1)S(1)}, u32[]{:S(2)}, u32[]{:S(2)}) collective-permute-start(bf16[13,8,384]{2,1,0:T(8,128)(2,1)S(1)} %get-tuple-element.17), channel_id=1, source_target_pairs={{8,0},{16,8},{24,16},{32,24},{40,32},{48,40},{56,48},{64,56},{72,6... | collective-permute-start | bytes 239624 | tf_op jit(solution)/shard_map/ppermute | solution.py:534
  23.2 14.8 %all-to-all-start = ((bf16[8,88,384]{2,1,0:T(8,128)(2,1)}), bf16[8,88,384]{2,1,0:T(8,128)(2,1)S(1)}, u32[]{:S(2)}, u32[]{:S(2)}) async-start(bf16[8,88,384]{2,1,0:T(8,128)(2,1)} %arrival.1), calls=%async_computation | async-start | bytes 1081344 | tf_op jit(solution)/shard_map/all_to_all | solution.py:544

commit v7 on v6

--- a/solution.py
+++ b/solution.py
@@ -536,13 +536,12 @@
     place = jnp.where(
         number < 3, (sector_index >> number) & 1, (band_index == bands - 1).astype(jnp.int32)
     ).astype(jnp.float32)
+    arrival = interpolate(place, field, own, following, sectors)
+    cycles = lax.all_to_all(arrival, "lon", split_axis=0, concat_axis=0, tiled=True)
+
     slot_waves = wave_order.reshape(bands, sectors)
     own_waves = lax.dynamic_slice_in_dim(slot_waves, sector_index, 1, axis=1)
     order = lax.dynamic_slice_in_dim(wave_order, band_index * sectors + sector_index, 1)
-    following, own_waves, order = lax.optimization_barrier((following, own_waves, order))
-    arrival = interpolate(place, field, own, following, sectors)
-    cycles = lax.all_to_all(arrival, "lon", split_axis=0, concat_axis=0, tiled=True)
-
     row_waves = jnp.broadcast_to(own_waves[:, :, None], (bands, 2, LANES)).reshape(
         2 * bands, LANES
     )

time: 62.6 us -> 62.7 us (level)
  local copies, waits for them, and re-layouts: 3.08 us -> 1.81 us
  starting transfers between devices: 23.3 us -> 24 us
    ppermute x1, waiting for transfers between devices: 0.01 us -> 1.33 us  [shards(): lax.ppermute(packed, 'lat', [((i + 1) % bands, i) for i in range(bands)])]
    all_to_all x1, waiting for transfers between devices: 3.54 us -> 2.78 us  [shards(): lax.all_to_all(arrival, 'lon', split_axis=0, concat_axis=0, tiled=True)]
    all_to_all x1, starting transfers between devices: 5.25 us -> 5.96 us  [shards(): lax.all_to_all(arrival, 'lon', split_axis=0, concat_axis=0, tiled=True)]
    reshape x1, local copies, waits for them, and re-layouts: 0.77 us -> 0.08 us  [shards(): slot_waves = wave_order.reshape(bands, sectors)]
    dynamic_slice x1, local copies, waits for them, and re-layouts: 1.27 us -> 0.59 us  [shards(): lax.dynamic_slice_in_dim(wave_order, band_index * sectors + sector_index, 1)]
  transfers between devices with their start and end apart: 2 -> 2, of which waited for: 1 -> 2; matrix products, arithmetic and copies ran while one was open for 5% -> 3% of each run, Pallas kernels for 6% -> 6%
where the time goes in v7:
time: 62.7 us; the launch traced here: 62.3 us
  starting transfers between devices  24 us (38%)
  blocking collectives  22.6 us (36%)
  Pallas kernels  8.21 us (13%)
  waiting for transfers between devices  4.1 us (7%)
  local copies, waits for them, and re-layouts  1.81 us (3%)
  between operations  1.41 us (2%)
    all_to_all x1, blocking collectives, shards(): lax.all_to_all(masked.reshape(bands, 2, LANES), 'lat', split_axis=0, conc...  22.6 us
    ppermute x1, starting transfers between devices, shards(): lax.ppermute(packed, 'lat', [((i + 1) % bands, i) for i in range(bands)])  18 us
    all_to_all x1, starting transfers between devices, shards(): lax.all_to_all(arrival, 'lon', split_axis=0, concat_axis=0, tiled=True)  5.96 us
    all_to_all x1, waiting for transfers between devices, shards(): lax.all_to_all(arrival, 'lon', split_axis=0, concat_axis=0, tiled=True)  2.78 us
    pallas_call x1, Pallas kernels, legendre_table(): pl.pallas_call(functools.partial(legendre_kernel, waves=waves, band_rows=...  2.2 us
    pallas_call x1, Pallas kernels, interpolate(): pl.pallas_call(arrival_kernel, out_shape=pltpu.VMEM((copies, height, sect...  2 us
    ppermute x1, waiting for transfers between devices, shards(): lax.ppermute(packed, 'lat', [((i + 1) % bands, i) for i in range(bands)])  1.33 us
    pallas_call x1, Pallas kernels, fourier_table(): pl.pallas_call(functools.partial(fourier_kernel, points=points), out_shap...  1.26 us
  transfers between devices with their start and end apart: 2, of which 2 were waited for; matrix products, arithmetic and copies ran while one was open for 3% of the time, Pallas kernels for 6%

profile of v7, /device:TPU:1, one launch (start us, length us, event | category | flops | bytes accessed | tf_op | source)
XLA Modules:
  0.0 62.3 jit_solution(4057812747010992344)
XLA Ops:
  0.0 0.0 copy-start.1
  0.0 0.9 %pack.1 = (bf16[13,8,384]{2,1,0:T(8,128)(2,1)S(1)}, bf16[9,8,384]{2,1,0:T(8,128)(2,1)S(1)}, f32[3,8,384]{2,1,0:T(8,128)S(1)}) custom-call(s32[1,8]{1,0:T(1,128)} %bitcast.12, bf16[9,8,384]{2,1,0:T(8,128)(2,1)} %field.1, s32[8,384]{1,0:T(8,128)} %departure.1, f32[8,384]{1,0:T(8,128)} %lat_weight.1, f32[8,384]{1,0:T(8,128)} %lon_weight.1), custom_call_target="tpu_custom_call" | custom-call | tf_op jit(solution)/shard_map/pack/pallas_call | solution.py:456
  0.9 18.0 %collective-permute-start = (bf16[13,8,384]{2,1,0:T(8,128)(2,1)S(1)}, bf16[13,8,384]{2,1,0:T(8,128)(2,1)S(1)}, u32[]{:S(2)}, u32[]{:S(2)}) collective-permute-start(bf16[13,8,384]{2,1,0:T(8,128)(2,1)S(1)} %get-tuple-element.14), channel_id=1, source_target_pairs={{8,0},{16,8},{24,16},{32,24},{40,32},{48,40},{56,48},{64,56},{72,6... | collective-permute-start | bytes 239624 | tf_op jit(solution)/shard_map/ppermute | solution.py:534
  18.9 0.1 select_convert_fusion.place
  19.0 1.3 %collective-permute-done.following = bf16[13,8,384]{2,1,0:T(8,128)(2,1)S(1)} collective-permute-done((bf16[13,8,384]{2,1,0:T(8,128)(2,1)S(1)}, bf16[13,8,384]{2,1,0:T(8,128)(2,1)S(1)}, u32[]{:S(2)}, u32[]{:S(2)}) %collective-permute-start) | collective-permute-done | bytes 79904 | tf_op jit(solution)/shard_map/ppermute | solution.py:534
  20.3 2.0 %arrival.1 = bf16[8,88,384]{2,1,0:T(8,128)(2,1)} custom-call(f32[4,8,128]{2,1,0:T(8,128)S(1)} %select_convert_fusion.place, bf16[9,8,384]{2,1,0:T(8,128)(2,1)S(1)} %get-tuple-element.12.field, f32[3,8,384]{2,1,0:T(8,128)S(1)} %get-tuple-element.13.own, bf16[13,8,384]{2,1,0:T(8,128)(2,1)S(1)} %collective-permute-done.following), custom_call_target="tpu_custom_call" | custom-call | tf_op jit(solution)/shard_map/arrival/pallas_call | solution.py:476
  22.3 0.0 copy-start
  22.3 6.0 %all-to-all-start = ((bf16[8,88,384]{2,1,0:T(8,128)(2,1)}), bf16[8,88,384]{2,1,0:T(8,128)(2,1)S(1)}, u32[]{:S(2)}, u32[]{:S(2)}) async-start(bf16[8,88,384]{2,1,0:T(8,128)(2,1)} %arrival.1), calls=%async_computation | async-start | bytes 1081344 | tf_op jit(solution)/shard_map/all_to_all | solution.py:540
  28.3 0.0 copy-done.1
  28.3 0.1 reshape.13
  28.4 0.6 dynamic_slice.8
  30.3 0.6 %broadcast_in_dim.36 = s32[8,128]{1,0:T(8,128)S(1)} broadcast(s32[]{:T(128)} %bitcast.4), dimensions={} | broadcast | bytes 4100 | tf_op jit(solution)/shard_map/broadcast_in_dim | solution.py:383
  30.9 0.2 dynamic-slice_reduce_fusion
  31.1 0.1 broadcast_in_dim.38
  31.2 0.2 broadcast_in_dim.39
  31.4 0.1 broadcast_multiply_fusion
  31.5 2.2 %legendre.1.functions = bf16[768,512]{1,0:T(8,128)(2,1)S(1)} custom-call(f32[768]{0:T(1024)S(1)} %get-tuple-element.23.step_a, f32[768]{0:T(1024)S(1)} %get-tuple-element.22.step_c, f32[8,128]{1,0:T(8,128)S(1)} %get-tuple-element.21.cosine, f32[8,128]{1,0:T(8,128)S(1)} %get-tuple-element.20.log_start, f32[8,128]{1,0:T(8,128)S(1)} %get-tuple-element.19.weight), custom_call_target="tpu_custom_call" | custom-call | tf_op jit(solution)/shard_map/legendre/pallas_call | solution.py:443
  33.7 0.1 broadcast_in_dim.40.waves
  33.8 0.0 copy-done
  33.8 1.3 %fourier.1 = (bf16[192,3200]{1,0:T(8,128)(2,1)S(1)}, f32[1,128]{1,0:T(1,128)S(1)}) custom-call(s32[192,128]{1,0:T(8,128)S(1)} %broadcast_in_dim.40.waves, s32[1,8]{1,0:T(1,128)S(1)} %bitcast.13, bf16[13,8,384]{2,1,0:T(8,128)(2,1)S(1)} %collective-permute-done.following), custom_call_target="tpu_custom_call" | custom-call | tf_op jit(solution)/shard_map/fourier/pallas_call | solution.py:427
  35.0 2.8 %all-to-all-done.cycles = bf16[8,88,384]{2,1,0:T(8,128)(2,1)S(1)} async-done(((bf16[8,88,384]{2,1,0:T(8,128)(2,1)}), bf16[8,88,384]{2,1,0:T(8,128)(2,1)S(1)}, u32[]{:S(2)}, u32[]{:S(2)}) %all-to-all-start) | async-done | bytes 540704 | tf_op jit(solution)/shard_map/all_to_all | solution.py:540
  37.8 0.7 %transform.1 = bf16[192,128]{1,0:T(8,128)(2,1)S(1)} custom-call(bf16[8,88,384]{2,1,0:T(8,128)(2,1)S(1)} %all-to-all-done.cycles, bf16[192,3200]{1,0:T(8,128)(2,1)S(1)} %get-tuple-element.16.fourier, s32[192,128]{1,0:T(8,128)S(1)} %broadcast_in_dim.40.waves, f32[1,128]{1,0:T(1,128)S(1)} %get-tuple-element.17.limits), custom_call_target="tpu_custom_call" | custom-call | tf_op jit(solution)/shard_map/transform/pallas_call | solution.py:492
  38.6 22.6 %all_to_all.10 = bf16[96,2,128]{2,1,0:T(2,128)(2,1)S(1)} all-to-all(bf16[96,2,128]{2,1,0:T(2,128)(2,1)S(1)} %bitcast.11), channel_id=1, replica_groups=mesh['lat'=96,'lon'=8] {'lat'}, dimensions={0} | all-to-all | bytes 98304 | tf_op jit(solution)/shard_map/all_to_all | solution.py:552
  61.2 1.1 %synthesis.1 = f32[9,2,768]{2,1,0:T(2,128)} custom-call(bf16[192,128]{1,0:T(8,128)(2,1)S(1)} %bitcast.10, bf16[768,512]{1,0:T(8,128)(2,1)S(1)} %legendre.1.functions), custom_call_target="tpu_custom_call" | custom-call | tf_op jit(solution)/shard_map/synthesis/pallas_call | solution.py:508
  (4 shorter events, 0.0 us)
Async XLA Ops:
  0.0 28.3 %copy-start.1 = (s32[768]{0:T(1024)S(1)}, s32[768]{0:T(1024)}, u32[]{:S(2)}) copy-start(s32[768]{0:T(1024)} %param.11) | copy-start | bytes 9220
  0.9 19.5 %collective-permute-start = (bf16[13,8,384]{2,1,0:T(8,128)(2,1)S(1)}, bf16[13,8,384]{2,1,0:T(8,128)(2,1)S(1)}, u32[]{:S(2)}, u32[]{:S(2)}) collective-permute-start(bf16[13,8,384]{2,1,0:T(8,128)(2,1)S(1)} %get-tuple-element.14), channel_id=1, source_target_pairs={{8,0},{16,8},{24,16},{32,24},{40,32},{48,40},{56,48},{64,56},{72,6... | collective-permute-start | bytes 239624 | tf_op jit(solution)/shard_map/ppermute | solution.py:534
  22.3 11.4 %copy-start = (s32[8]{0:T(128)S(1)}, s32[8]{0:T(128)}, u32[]{:S(2)}) copy-start(s32[8]{0:T(128)} %param.10) | copy-start | bytes 100
  22.3 15.5 %all-to-all-start = ((bf16[8,88,384]{2,1,0:T(8,128)(2,1)}), bf16[8,88,384]{2,1,0:T(8,128)(2,1)S(1)}, u32[]{:S(2)}, u32[]{:S(2)}) async-start(bf16[8,88,384]{2,1,0:T(8,128)(2,1)} %arrival.1), calls=%async_computation | async-start | bytes 1081344 | tf_op jit(solution)/shard_map/all_to_all | solution.py:540

commit v8 on v7

--- a/solution.py
+++ b/solution.py
@@ -207,7 +207,7 @@
     tiles = cols // LANES
     count = 2 * HALO + 1
     used = channels * rows
-    tall = rows + 2 * HALO
+    pitch = used + rows
     lane = lax.broadcasted_iota(jnp.int32, (rows, LANES), 1)
     row = lax.broadcasted_iota(jnp.int32, (rows, cols), 0)
     last = jnp.concatenate([place[3]] * tiles, axis=1)
@@ -253,8 +253,7 @@
         sums[0] = jnp.where(lane < HALO, 0.0, sums[0])
         sums[-1] = jnp.where(lane >= LANES - HALO, 0.0, sums[-1])
         for t in range(tiles):
-            span = slice(t * LANES, (t + 1) * LANES)
-            stage[c * rows : (c + 1) * rows, span] = sums[t]
+            stage[t * pitch + c * rows : t * pitch + (c + 1) * rows, :] = sums[t]
     slots = LANES // WINDOW
     bits = [jnp.concatenate([place[k]] * 2, axis=0) > 0.0 for k in range(3)]
     for g in range(2):
@@ -266,8 +265,11 @@
             total = total + jnp.concatenate([planes, jnp.zeros_like(planes)], axis=0)
         for k in range(3):
             total = jnp.where(bits[k], pltpu.roll(total, WINDOW << k, 1), total)
-        stage[used : used + tall, g * LANES : (g + 1) * LANES] = total
-    stage[used : used + tall, 2 * LANES :] = jnp.zeros((tall, cols - 2 * LANES), jnp.float32)
+        if g == 0:
+            stage[used:pitch, :] = total[:rows]
+            stage[pitch + used : 2 * pitch, :] = total[rows:]
+        else:
+            stage[2 * pitch + used :, :] = total
     value = stage[...].astype(jnp.bfloat16)
     for copy in range(out.shape[0]):
         out[copy] = value
@@ -281,12 +283,20 @@
     slots = LANES // WINDOW
     slot = lax.broadcasted_iota(jnp.int32, (tall, LANES), 1) // WINDOW
     inner = lax.broadcasted_iota(jnp.int32, (tall, LANES), 1) % WINDOW
+    pitch = used + rows
+    tiles = cycles.shape[1] // pitch
+
+    def piece(sector, first, count):
+        return cycles[sector, first : first + count, :].astype(jnp.float32)
+
     pieces = [
         [
-            cycles[sector, used : used + tall, g * LANES : (g + 1) * LANES].astype(jnp.float32)
+            jnp.concatenate(
+                [piece(sector, used, rows), piece(sector, pitch + used, rows)], axis=0
+            )
             for sector in range(sectors)
-        ]
-        for g in range(2)
+        ],
+        [piece(sector, 2 * pitch + used, tall) for sector in range(sectors)],
     ]
 
     def window(index, height):
@@ -324,7 +334,11 @@
         )
         stage[c * rows : (c + 1) * rows, :] = jnp.where(inside, total, 0.0)
     gathered = jnp.concatenate(
-        [cycles[sector, :used, :] for sector in range(sectors)]
+        [
+            cycles[sector, t * pitch : t * pitch + used, :]
+            for sector in range(sectors)
+            for t in range(tiles)
+        ]
         + [stage[...].astype(jnp.bfloat16)],
         axis=1,
     )
@@ -471,18 +485,18 @@
     channels, band_rows, sector_cols = field.shape
     tall = band_rows + 2 * HALO
     tiles = sector_cols // LANES
-    height = channels * band_rows + tall
+    height = tiles * (channels + 1) * band_rows + band_rows
     count = 2 * HALO + 1
     return pl.pallas_call(
         arrival_kernel,
-        out_shape=pltpu.VMEM((copies, height, sector_cols), jnp.bfloat16),
+        out_shape=pltpu.VMEM((copies, height, LANES), jnp.bfloat16),
         in_specs=[vmem()] * 4,
         out_specs=vmem(),
         scratch_shapes=[
             pltpu.VMEM((channels, tiles, tall, LANES), jnp.float32),
             pltpu.VMEM((2, count, tiles, tall, LANES), jnp.float32),
             pltpu.VMEM((2 * count, band_rows, sector_cols), jnp.float32),
-            pltpu.VMEM((height, sector_cols), jnp.float32),
+            pltpu.VMEM((height, LANES), jnp.float32),
         ],
         name="arrival",
     )(*map(near, (place, field, own, following)))

time: 62.7 us -> 62.3 us (level)
  blocking collectives: 22.6 us -> 20.1 us
  waiting for transfers between devices: 4.1 us -> 5.49 us
  local copies, waits for them, and re-layouts: 1.81 us -> 3.18 us
  starting transfers between devices: 24 us -> 23.3 us
    all_to_all x1, waiting for transfers between devices: 2.78 us -> 5.48 us  [shards(): lax.all_to_all(arrival, 'lon', split_axis=0, concat_axis=0, tiled=True)]
    all_to_all x1, blocking collectives: 22.6 us -> 20.1 us  [shards(): lax.all_to_all(masked.reshape(bands, 2, LANES), 'lat', split_axis=0, conc...]
    ppermute x1, waiting for transfers between devices: 1.33 us -> 0.01 us  [shards(): lax.ppermute(packed, 'lat', [((i + 1) % bands, i) for i in range(bands)])]
    all_to_all x1, starting transfers between devices: 5.96 us -> 5.25 us  [shards(): lax.all_to_all(arrival, 'lon', split_axis=0, concat_axis=0, tiled=True)]
    reshape x1, local copies, waits for them, and re-layouts: 0.08 us -> 0.77 us  [shards(): slot_waves = wave_order.reshape(bands, sectors)]
    dynamic_slice x1, local copies, waits for them, and re-layouts: 0.59 us -> 1.27 us  [shards(): lax.dynamic_slice_in_dim(wave_order, band_index * sectors + sector_index, 1)]
  transfers between devices with their start and end apart: 2 -> 2, of which waited for: 2 -> 1; matrix products, arithmetic and copies ran while one was open for 3% -> 5% of each run, Pallas kernels for 6% -> 6%
where the time goes in v8:
time: 62.3 us; the launch traced here: 61.9 us
  starting transfers between devices  23.3 us (37%)
  blocking collectives  20.1 us (32%)
  Pallas kernels  8.22 us (13%)
  waiting for transfers between devices  5.49 us (9%)
  local copies, waits for them, and re-layouts  3.18 us (5%)
  between operations  1.42 us (2%)
    all_to_all x1, blocking collectives, shards(): lax.all_to_all(masked.reshape(bands, 2, LANES), 'lat', split_axis=0, conc...  20.1 us
    ppermute x1, starting transfers between devices, shards(): lax.ppermute(packed, 'lat', [((i + 1) % bands, i) for i in range(bands)])  18 us
    all_to_all x1, waiting for transfers between devices, shards(): lax.all_to_all(arrival, 'lon', split_axis=0, concat_axis=0, tiled=True)  5.48 us
    all_to_all x1, starting transfers between devices, shards(): lax.all_to_all(arrival, 'lon', split_axis=0, concat_axis=0, tiled=True)  5.25 us
    pallas_call x1, Pallas kernels, legendre_table(): pl.pallas_call(functools.partial(legendre_kernel, waves=waves, band_rows=...  2.2 us
    pallas_call x1, Pallas kernels, interpolate(): pl.pallas_call(arrival_kernel, out_shape=pltpu.VMEM((copies, height, LANE...  2.03 us
    dynamic_slice x1, local copies, waits for them, and re-layouts, shards(): lax.dynamic_slice_in_dim(wave_order, band_index * sectors + sector_index, 1)  1.27 us
    pallas_call x1, Pallas kernels, fourier_table(): pl.pallas_call(functools.partial(fourier_kernel, points=points), out_shap...  1.26 us
  transfers between devices with their start and end apart: 2, of which 1 were waited for; matrix products, arithmetic and copies ran while one was open for 5% of the time, Pallas kernels for 6%

profile of v8, /device:TPU:1, one launch (start us, length us, event | category | flops | bytes accessed | tf_op | source)
XLA Modules:
  0.0 61.9 jit_solution(3946739298203651651)
XLA Ops:
  0.0 0.8 %pack.1 = (bf16[13,8,384]{2,1,0:T(8,128)(2,1)S(1)}, bf16[9,8,384]{2,1,0:T(8,128)(2,1)S(1)}, f32[3,8,384]{2,1,0:T(8,128)S(1)}) custom-call(s32[1,8]{1,0:T(1,128)} %bitcast.12, bf16[9,8,384]{2,1,0:T(8,128)(2,1)} %field.1, s32[8,384]{1,0:T(8,128)} %departure.1, f32[8,384]{1,0:T(8,128)} %lat_weight.1, f32[8,384]{1,0:T(8,128)} %lon_weight.1), custom_call_target="tpu_custom_call" | custom-call | tf_op jit(solution)/shard_map/pack/pallas_call | solution.py:470
  0.8 18.0 %collective-permute-start = (bf16[13,8,384]{2,1,0:T(8,128)(2,1)S(1)}, bf16[13,8,384]{2,1,0:T(8,128)(2,1)S(1)}, u32[]{:S(2)}, u32[]{:S(2)}) collective-permute-start(bf16[13,8,384]{2,1,0:T(8,128)(2,1)S(1)} %get-tuple-element.14), channel_id=1, source_target_pairs={{8,0},{16,8},{24,16},{32,24},{40,32},{48,40},{56,48},{64,56},{72,6... | collective-permute-start | bytes 239624 | tf_op jit(solution)/shard_map/ppermute | solution.py:548
  18.9 0.1 select_convert_fusion.place
  19.0 0.8 %reshape.13 = s32[96,8]{1,0:T(8,128)S(1)} reshape(s32[768]{0:T(1024)} %param.11) | data formatting | bytes 6144 | tf_op jit(solution)/shard_map/reshape | solution.py:556
  19.8 1.3 %dynamic_slice.8 = s32[1]{0:T(128)} dynamic-slice(s32[768]{0:T(1024)} %param.11, s32[]{:T(128)S(6)} %select_n.29), dynamic_slice_sizes={1} | dynamic-slice | bytes 12 | tf_op jit(solution)/shard_map/dynamic_slice | solution.py:558
  22.4 0.6 %broadcast_in_dim.36 = s32[8,128]{1,0:T(8,128)S(1)} broadcast(s32[]{:T(128)} %bitcast.4), dimensions={} | broadcast | bytes 4100 | tf_op jit(solution)/shard_map/broadcast_in_dim | solution.py:397
  23.0 0.2 dynamic-slice_reduce_fusion
  23.2 0.1 broadcast_in_dim.38
  23.3 0.2 broadcast_in_dim.39
  23.4 0.0 collective-permute-done.following
  23.4 0.0 copy-start
  23.4 2.0 %arrival.1 = bf16[8,248,128]{2,1,0:T(8,128)(2,1)} custom-call(f32[4,8,128]{2,1,0:T(8,128)S(1)} %select_convert_fusion.place, bf16[9,8,384]{2,1,0:T(8,128)(2,1)S(1)} %get-tuple-element.12.field, f32[3,8,384]{2,1,0:T(8,128)S(1)} %get-tuple-element.13.own, bf16[13,8,384]{2,1,0:T(8,128)(2,1)S(1)} %collective-permute-done.following), custom_call_target="tpu_custom_call" | custom-call | tf_op jit(solution)/shard_map/arrival/pallas_call | solution.py:490
  25.5 5.3 %all-to-all-start = ((bf16[8,248,128]{2,1,0:T(8,128)(2,1)}), bf16[8,248,128]{2,1,0:T(8,128)(2,1)S(1)}, u32[]{:S(2)}, u32[]{:S(2)}) async-start(bf16[8,248,128]{2,1,0:T(8,128)(2,1)} %arrival.1), calls=%async_computation | async-start | bytes 1015808 | tf_op jit(solution)/shard_map/all_to_all | solution.py:554
  30.8 0.1 broadcast_multiply_fusion
  30.9 2.2 %legendre.1.functions = bf16[768,512]{1,0:T(8,128)(2,1)S(1)} custom-call(f32[768]{0:T(1024)S(1)} %get-tuple-element.23.step_a, f32[768]{0:T(1024)S(1)} %get-tuple-element.22.step_c, f32[8,128]{1,0:T(8,128)S(1)} %get-tuple-element.21.cosine, f32[8,128]{1,0:T(8,128)S(1)} %get-tuple-element.20.log_start, f32[8,128]{1,0:T(8,128)S(1)} %get-tuple-element.19.weight), custom_call_target="tpu_custom_call" | custom-call | tf_op jit(solution)/shard_map/legendre/pallas_call | solution.py:457
  33.1 0.1 broadcast_in_dim.40.waves
  33.1 0.0 copy-done
  33.2 1.3 %fourier.1 = (bf16[192,3200]{1,0:T(8,128)(2,1)S(1)}, f32[1,128]{1,0:T(1,128)S(1)}) custom-call(s32[192,128]{1,0:T(8,128)S(1)} %broadcast_in_dim.40.waves, s32[1,8]{1,0:T(1,128)S(1)} %bitcast.13, bf16[13,8,384]{2,1,0:T(8,128)(2,1)S(1)} %collective-permute-done.following), custom_call_target="tpu_custom_call" | custom-call | tf_op jit(solution)/shard_map/fourier/pallas_call | solution.py:441
  34.4 5.5 %all-to-all-done.cycles = bf16[8,248,128]{2,1,0:T(8,128)(2,1)S(1)} async-done(((bf16[8,248,128]{2,1,0:T(8,128)(2,1)}), bf16[8,248,128]{2,1,0:T(8,128)(2,1)S(1)}, u32[]{:S(2)}, u32[]{:S(2)}) %all-to-all-start) | async-done | bytes 507936 | tf_op jit(solution)/shard_map/all_to_all | solution.py:554
  39.9 0.7 %transform.1 = bf16[192,128]{1,0:T(8,128)(2,1)S(1)} custom-call(bf16[8,248,128]{2,1,0:T(8,128)(2,1)S(1)} %all-to-all-done.cycles, bf16[192,3200]{1,0:T(8,128)(2,1)S(1)} %get-tuple-element.16.fourier, s32[192,128]{1,0:T(8,128)S(1)} %broadcast_in_dim.40.waves, f32[1,128]{1,0:T(1,128)S(1)} %get-tuple-element.17.limits), custom_call_target="tpu_custom_call" | custom-call | tf_op jit(solution)/shard_map/transform/pallas_call | solution.py:506
  40.6 20.1 %all_to_all.10 = bf16[96,2,128]{2,1,0:T(2,128)(2,1)S(1)} all-to-all(bf16[96,2,128]{2,1,0:T(2,128)(2,1)S(1)} %bitcast.11), channel_id=1, replica_groups=mesh['lat'=96,'lon'=8] {'lat'}, dimensions={0} | all-to-all | bytes 98304 | tf_op jit(solution)/shard_map/all_to_all | solution.py:566
  60.7 1.1 %synthesis.1 = f32[9,2,768]{2,1,0:T(2,128)} custom-call(bf16[192,128]{1,0:T(8,128)(2,1)S(1)} %bitcast.10, bf16[768,512]{1,0:T(8,128)(2,1)S(1)} %legendre.1.functions), custom_call_target="tpu_custom_call" | custom-call | tf_op jit(solution)/shard_map/synthesis/pallas_call | solution.py:522
  (4 shorter events, 0.0 us)
Async XLA Ops:
  0.8 22.6 %collective-permute-start = (bf16[13,8,384]{2,1,0:T(8,128)(2,1)S(1)}, bf16[13,8,384]{2,1,0:T(8,128)(2,1)S(1)}, u32[]{:S(2)}, u32[]{:S(2)}) collective-permute-start(bf16[13,8,384]{2,1,0:T(8,128)(2,1)S(1)} %get-tuple-element.14), channel_id=1, source_target_pairs={{8,0},{16,8},{24,16},{32,24},{40,32},{48,40},{56,48},{64,56},{72,6... | collective-permute-start | bytes 239624 | tf_op jit(solution)/shard_map/ppermute | solution.py:548
  23.4 9.7 %copy-start = (s32[8]{0:T(128)S(1)}, s32[8]{0:T(128)}, u32[]{:S(2)}) copy-start(s32[8]{0:T(128)} %param.10) | copy-start | bytes 100
  25.5 14.4 %all-to-all-start = ((bf16[8,248,128]{2,1,0:T(8,128)(2,1)}), bf16[8,248,128]{2,1,0:T(8,128)(2,1)S(1)}, u32[]{:S(2)}, u32[]{:S(2)}) async-start(bf16[8,248,128]{2,1,0:T(8,128)(2,1)} %arrival.1), calls=%async_computation | async-start | bytes 1015808 | tf_op jit(solution)/shard_map/all_to_all | solution.py:554

commit v9 on v8

--- a/solution.py
+++ b/solution.py
@@ -244,7 +244,7 @@
     for c in range(channels):
         sums = stencil(
             lambda: [grid[c, t] for t in range(tiles)],
-            shifted.at[c % 2],
+            shifted.at[c % shifted.shape[0]],
             part(0),
             part(count),
             tiles,
@@ -277,7 +277,7 @@
 
 def transform_kernel(cycles, fourier, waves, limits, out, shifted, stage):
     sectors = cycles.shape[0]
-    used, rows = stage.shape[0], shifted.shape[2] - 2 * HALO
+    used, rows = stage.shape[0], shifted.shape[3] - 2 * HALO
     tall = rows + 2 * HALO
     channels = used // rows
     slots = LANES // WINDOW
@@ -326,7 +326,7 @@
     for c in range(channels):
         (total,) = stencil(
             lambda: [window(c, tall)],
-            shifted,
+            shifted.at[c % shifted.shape[0]],
             lambda e, t: row_parts[e],
             lambda d, t: col_parts[d],
             1,
@@ -494,7 +494,7 @@
         out_specs=vmem(),
         scratch_shapes=[
             pltpu.VMEM((channels, tiles, tall, LANES), jnp.float32),
-            pltpu.VMEM((2, count, tiles, tall, LANES), jnp.float32),
+            pltpu.VMEM((3, count, tiles, tall, LANES), jnp.float32),
             pltpu.VMEM((2 * count, band_rows, sector_cols), jnp.float32),
             pltpu.VMEM((height, LANES), jnp.float32),
         ],
@@ -509,7 +509,7 @@
         in_specs=[vmem()] * 4,
         out_specs=vmem(),
         scratch_shapes=[
-            pltpu.VMEM((2 * HALO + 1, 1, band_rows + 2 * HALO, LANES), jnp.float32),
+            pltpu.VMEM((3, 2 * HALO + 1, 1, band_rows + 2 * HALO, LANES), jnp.float32),
             pltpu.VMEM((channels * band_rows, LANES), jnp.float32),
         ],
         name="transform",

time: 62.3 us -> 62.2 us (level)
  no operation moved by 1% of the time
where the time goes in v9:
time: 62.2 us; the launch traced here: 61.7 us
  starting transfers between devices  23.3 us (37%)
  blocking collectives  20.1 us (32%)
  Pallas kernels  8.07 us (13%)
  waiting for transfers between devices  5.49 us (9%)
  local copies, waits for them, and re-layouts  3.18 us (5%)
  between operations  1.42 us (2%)
    all_to_all x1, blocking collectives, shards(): lax.all_to_all(masked.reshape(bands, 2, LANES), 'lat', split_axis=0, conc...  20.1 us
    ppermute x1, starting transfers between devices, shards(): lax.ppermute(packed, 'lat', [((i + 1) % bands, i) for i in range(bands)])  18 us
    all_to_all x1, waiting for transfers between devices, shards(): lax.all_to_all(arrival, 'lon', split_axis=0, concat_axis=0, tiled=True)  5.48 us
    all_to_all x1, starting transfers between devices, shards(): lax.all_to_all(arrival, 'lon', split_axis=0, concat_axis=0, tiled=True)  5.25 us
    pallas_call x1, Pallas kernels, legendre_table(): pl.pallas_call(functools.partial(legendre_kernel, waves=waves, band_rows=...  2.2 us
    pallas_call x1, Pallas kernels, interpolate(): pl.pallas_call(arrival_kernel, out_shape=pltpu.VMEM((copies, height, LANE...  1.94 us
    dynamic_slice x1, local copies, waits for them, and re-layouts, shards(): lax.dynamic_slice_in_dim(wave_order, band_index * sectors + sector_index, 1)  1.27 us
    pallas_call x1, Pallas kernels, fourier_table(): pl.pallas_call(functools.partial(fourier_kernel, points=points), out_shap...  1.26 us
  transfers between devices with their start and end apart: 2, of which 1 were waited for; matrix products, arithmetic and copies ran while one was open for 5% of the time, Pallas kernels for 6%

profile of v9, /device:TPU:1, one launch (start us, length us, event | category | flops | bytes accessed | tf_op | source)
XLA Modules:
  0.0 61.7 jit_solution(4416771476629759851)
XLA Ops:
  0.0 0.8 %pack.1 = (bf16[13,8,384]{2,1,0:T(8,128)(2,1)S(1)}, bf16[9,8,384]{2,1,0:T(8,128)(2,1)S(1)}, f32[3,8,384]{2,1,0:T(8,128)S(1)}) custom-call(s32[1,8]{1,0:T(1,128)} %bitcast.12, bf16[9,8,384]{2,1,0:T(8,128)(2,1)} %field.1, s32[8,384]{1,0:T(8,128)} %departure.1, f32[8,384]{1,0:T(8,128)} %lat_weight.1, f32[8,384]{1,0:T(8,128)} %lon_weight.1), custom_call_target="tpu_custom_call" | custom-call | tf_op jit(solution)/shard_map/pack/pallas_call | solution.py:470
  0.8 18.0 %collective-permute-start = (bf16[13,8,384]{2,1,0:T(8,128)(2,1)S(1)}, bf16[13,8,384]{2,1,0:T(8,128)(2,1)S(1)}, u32[]{:S(2)}, u32[]{:S(2)}) collective-permute-start(bf16[13,8,384]{2,1,0:T(8,128)(2,1)S(1)} %get-tuple-element.14), channel_id=1, source_target_pairs={{8,0},{16,8},{24,16},{32,24},{40,32},{48,40},{56,48},{64,56},{72,6... | collective-permute-start | bytes 239624 | tf_op jit(solution)/shard_map/ppermute | solution.py:548
  18.9 0.1 select_convert_fusion.place
  19.0 0.8 %reshape.13 = s32[96,8]{1,0:T(8,128)S(1)} reshape(s32[768]{0:T(1024)} %param.11) | data formatting | bytes 6144 | tf_op jit(solution)/shard_map/reshape | solution.py:556
  19.8 1.3 %dynamic_slice.8 = s32[1]{0:T(128)} dynamic-slice(s32[768]{0:T(1024)} %param.11, s32[]{:T(128)S(6)} %select_n.29), dynamic_slice_sizes={1} | dynamic-slice | bytes 12 | tf_op jit(solution)/shard_map/dynamic_slice | solution.py:558
  22.4 0.6 %broadcast_in_dim.36 = s32[8,128]{1,0:T(8,128)S(1)} broadcast(s32[]{:T(128)} %bitcast.4), dimensions={} | broadcast | bytes 4100 | tf_op jit(solution)/shard_map/broadcast_in_dim | solution.py:397
  23.0 0.2 dynamic-slice_reduce_fusion
  23.2 0.1 broadcast_in_dim.38
  23.3 0.2 broadcast_in_dim.39
  23.4 0.0 collective-permute-done.following
  23.4 0.0 copy-start
  23.4 1.9 %arrival.1 = bf16[8,248,128]{2,1,0:T(8,128)(2,1)} custom-call(f32[4,8,128]{2,1,0:T(8,128)S(1)} %select_convert_fusion.place, bf16[9,8,384]{2,1,0:T(8,128)(2,1)S(1)} %get-tuple-element.12.field, f32[3,8,384]{2,1,0:T(8,128)S(1)} %get-tuple-element.13.own, bf16[13,8,384]{2,1,0:T(8,128)(2,1)S(1)} %collective-permute-done.following), custom_call_target="tpu_custom_call" | custom-call | tf_op jit(solution)/shard_map/arrival/pallas_call | solution.py:490
  25.4 5.3 %all-to-all-start = ((bf16[8,248,128]{2,1,0:T(8,128)(2,1)}), bf16[8,248,128]{2,1,0:T(8,128)(2,1)S(1)}, u32[]{:S(2)}, u32[]{:S(2)}) async-start(bf16[8,248,128]{2,1,0:T(8,128)(2,1)} %arrival.1), calls=%async_computation | async-start | bytes 1015808 | tf_op jit(solution)/shard_map/all_to_all | solution.py:554
  30.7 0.1 broadcast_multiply_fusion
  30.8 2.2 %legendre.1.functions = bf16[768,512]{1,0:T(8,128)(2,1)S(1)} custom-call(f32[768]{0:T(1024)S(1)} %get-tuple-element.23.step_a, f32[768]{0:T(1024)S(1)} %get-tuple-element.22.step_c, f32[8,128]{1,0:T(8,128)S(1)} %get-tuple-element.21.cosine, f32[8,128]{1,0:T(8,128)S(1)} %get-tuple-element.20.log_start, f32[8,128]{1,0:T(8,128)S(1)} %get-tuple-element.19.weight), custom_call_target="tpu_custom_call" | custom-call | tf_op jit(solution)/shard_map/legendre/pallas_call | solution.py:457
  33.0 0.1 broadcast_in_dim.40.waves
  33.0 0.0 copy-done
  33.1 1.3 %fourier.1 = (bf16[192,3200]{1,0:T(8,128)(2,1)S(1)}, f32[1,128]{1,0:T(1,128)S(1)}) custom-call(s32[192,128]{1,0:T(8,128)S(1)} %broadcast_in_dim.40.waves, s32[1,8]{1,0:T(1,128)S(1)} %bitcast.13, bf16[13,8,384]{2,1,0:T(8,128)(2,1)S(1)} %collective-permute-done.following), custom_call_target="tpu_custom_call" | custom-call | tf_op jit(solution)/shard_map/fourier/pallas_call | solution.py:441
  34.3 5.5 %all-to-all-done.cycles = bf16[8,248,128]{2,1,0:T(8,128)(2,1)S(1)} async-done(((bf16[8,248,128]{2,1,0:T(8,128)(2,1)}), bf16[8,248,128]{2,1,0:T(8,128)(2,1)S(1)}, u32[]{:S(2)}, u32[]{:S(2)}) %all-to-all-start) | async-done | bytes 507936 | tf_op jit(solution)/shard_map/all_to_all | solution.py:554
  39.8 0.7 %transform.1 = bf16[192,128]{1,0:T(8,128)(2,1)S(1)} custom-call(bf16[8,248,128]{2,1,0:T(8,128)(2,1)S(1)} %all-to-all-done.cycles, bf16[192,3200]{1,0:T(8,128)(2,1)S(1)} %get-tuple-element.16.fourier, s32[192,128]{1,0:T(8,128)S(1)} %broadcast_in_dim.40.waves, f32[1,128]{1,0:T(1,128)S(1)} %get-tuple-element.17.limits), custom_call_target="tpu_custom_call" | custom-call | tf_op jit(solution)/shard_map/transform/pallas_call | solution.py:506
  40.5 20.1 %all_to_all.10 = bf16[96,2,128]{2,1,0:T(2,128)(2,1)S(1)} all-to-all(bf16[96,2,128]{2,1,0:T(2,128)(2,1)S(1)} %bitcast.11), channel_id=1, replica_groups=mesh['lat'=96,'lon'=8] {'lat'}, dimensions={0} | all-to-all | bytes 98304 | tf_op jit(solution)/shard_map/all_to_all | solution.py:566
  60.6 1.1 %synthesis.1 = f32[9,2,768]{2,1,0:T(2,128)} custom-call(bf16[192,128]{1,0:T(8,128)(2,1)S(1)} %bitcast.10, bf16[768,512]{1,0:T(8,128)(2,1)S(1)} %legendre.1.functions), custom_call_target="tpu_custom_call" | custom-call | tf_op jit(solution)/shard_map/synthesis/pallas_call | solution.py:522
  (4 shorter events, 0.0 us)
Async XLA Ops:
  0.8 22.6 %collective-permute-start = (bf16[13,8,384]{2,1,0:T(8,128)(2,1)S(1)}, bf16[13,8,384]{2,1,0:T(8,128)(2,1)S(1)}, u32[]{:S(2)}, u32[]{:S(2)}) collective-permute-start(bf16[13,8,384]{2,1,0:T(8,128)(2,1)S(1)} %get-tuple-element.14), channel_id=1, source_target_pairs={{8,0},{16,8},{24,16},{32,24},{40,32},{48,40},{56,48},{64,56},{72,6... | collective-permute-start | bytes 239624 | tf_op jit(solution)/shard_map/ppermute | solution.py:548
  23.4 9.6 %copy-start = (s32[8]{0:T(128)S(1)}, s32[8]{0:T(128)}, u32[]{:S(2)}) copy-start(s32[8]{0:T(128)} %param.10) | copy-start | bytes 100
  25.4 14.4 %all-to-all-start = ((bf16[8,248,128]{2,1,0:T(8,128)(2,1)}), bf16[8,248,128]{2,1,0:T(8,128)(2,1)S(1)}, u32[]{:S(2)}, u32[]{:S(2)}) async-start(bf16[8,248,128]{2,1,0:T(8,128)(2,1)} %arrival.1), calls=%async_computation | async-start | bytes 1015808 | tf_op jit(solution)/shard_map/all_to_all | solution.py:554

commit v10 on v9

--- a/solution.py
+++ b/solution.py
@@ -494,7 +494,7 @@
         out_specs=vmem(),
         scratch_shapes=[
             pltpu.VMEM((channels, tiles, tall, LANES), jnp.float32),
-            pltpu.VMEM((3, count, tiles, tall, LANES), jnp.float32),
+            pltpu.VMEM((4, count, tiles, tall, LANES), jnp.float32),
             pltpu.VMEM((2 * count, band_rows, sector_cols), jnp.float32),
             pltpu.VMEM((height, LANES), jnp.float32),
         ],
@@ -509,7 +509,7 @@
         in_specs=[vmem()] * 4,
         out_specs=vmem(),
         scratch_shapes=[
-            pltpu.VMEM((3, 2 * HALO + 1, 1, band_rows + 2 * HALO, LANES), jnp.float32),
+            pltpu.VMEM((9, 2 * HALO + 1, 1, band_rows + 2 * HALO, LANES), jnp.float32),
             pltpu.VMEM((channels * band_rows, LANES), jnp.float32),
         ],
         name="transform",

time: 62.2 us -> 62 us (level)
  no operation moved by 1% of the time
where the time goes in v10:
time: 62 us; the launch traced here: 61.6 us
  starting transfers between devices  23.3 us (38%)
  blocking collectives  20.1 us (32%)
  Pallas kernels  7.92 us (13%)
  waiting for transfers between devices  5.49 us (9%)
  local copies, waits for them, and re-layouts  3.18 us (5%)
  between operations  1.42 us (2%)
    all_to_all x1, blocking collectives, shards(): lax.all_to_all(masked.reshape(bands, 2, LANES), 'lat', split_axis=0, conc...  20.1 us
    ppermute x1, starting transfers between devices, shards(): lax.ppermute(packed, 'lat', [((i + 1) % bands, i) for i in range(bands)])  18 us
    all_to_all x1, waiting for transfers between devices, shards(): lax.all_to_all(arrival, 'lon', split_axis=0, concat_axis=0, tiled=True)  5.48 us
    all_to_all x1, starting transfers between devices, shards(): lax.all_to_all(arrival, 'lon', split_axis=0, concat_axis=0, tiled=True)  5.25 us
    pallas_call x1, Pallas kernels, legendre_table(): pl.pallas_call(functools.partial(legendre_kernel, waves=waves, band_rows=...  2.2 us
    pallas_call x1, Pallas kernels, interpolate(): pl.pallas_call(arrival_kernel, out_shape=pltpu.VMEM((copies, height, LANE...  1.86 us
    dynamic_slice x1, local copies, waits for them, and re-layouts, shards(): lax.dynamic_slice_in_dim(wave_order, band_index * sectors + sector_index, 1)  1.27 us
    pallas_call x1, Pallas kernels, fourier_table(): pl.pallas_call(functools.partial(fourier_kernel, points=points), out_shap...  1.26 us
  transfers between devices with their start and end apart: 2, of which 1 were waited for; matrix products, arithmetic and copies ran while one was open for 5% of the time, Pallas kernels for 6%

profile of v10, /device:TPU:1, one launch (start us, length us, event | category | flops | bytes accessed | tf_op | source)
XLA Modules:
  0.0 61.6 jit_solution(9916651642251436202)
XLA Ops:
  0.0 0.8 %pack.1 = (bf16[13,8,384]{2,1,0:T(8,128)(2,1)S(1)}, bf16[9,8,384]{2,1,0:T(8,128)(2,1)S(1)}, f32[3,8,384]{2,1,0:T(8,128)S(1)}) custom-call(s32[1,8]{1,0:T(1,128)} %bitcast.12, bf16[9,8,384]{2,1,0:T(8,128)(2,1)} %field.1, s32[8,384]{1,0:T(8,128)} %departure.1, f32[8,384]{1,0:T(8,128)} %lat_weight.1, f32[8,384]{1,0:T(8,128)} %lon_weight.1), custom_call_target="tpu_custom_call" | custom-call | tf_op jit(solution)/shard_map/pack/pallas_call | solution.py:470
  0.8 18.0 %collective-permute-start = (bf16[13,8,384]{2,1,0:T(8,128)(2,1)S(1)}, bf16[13,8,384]{2,1,0:T(8,128)(2,1)S(1)}, u32[]{:S(2)}, u32[]{:S(2)}) collective-permute-start(bf16[13,8,384]{2,1,0:T(8,128)(2,1)S(1)} %get-tuple-element.14), channel_id=1, source_target_pairs={{8,0},{16,8},{24,16},{32,24},{40,32},{48,40},{56,48},{64,56},{72,6... | collective-permute-start | bytes 239624 | tf_op jit(solution)/shard_map/ppermute | solution.py:548
  18.9 0.1 select_convert_fusion.place
  19.0 0.8 %reshape.13 = s32[96,8]{1,0:T(8,128)S(1)} reshape(s32[768]{0:T(1024)} %param.11) | data formatting | bytes 6144 | tf_op jit(solution)/shard_map/reshape | solution.py:556
  19.8 1.3 %dynamic_slice.8 = s32[1]{0:T(128)} dynamic-slice(s32[768]{0:T(1024)} %param.11, s32[]{:T(128)S(6)} %select_n.29), dynamic_slice_sizes={1} | dynamic-slice | bytes 12 | tf_op jit(solution)/shard_map/dynamic_slice | solution.py:558
  22.4 0.6 %broadcast_in_dim.36 = s32[8,128]{1,0:T(8,128)S(1)} broadcast(s32[]{:T(128)} %bitcast.4), dimensions={} | broadcast | bytes 4100 | tf_op jit(solution)/shard_map/broadcast_in_dim | solution.py:397
  23.0 0.2 dynamic-slice_reduce_fusion
  23.2 0.1 broadcast_in_dim.38
  23.3 0.2 broadcast_in_dim.39
  23.4 0.0 collective-permute-done.following
  23.4 0.0 copy-start
  23.4 1.9 %arrival.1 = bf16[8,248,128]{2,1,0:T(8,128)(2,1)} custom-call(f32[4,8,128]{2,1,0:T(8,128)S(1)} %select_convert_fusion.place, bf16[9,8,384]{2,1,0:T(8,128)(2,1)S(1)} %get-tuple-element.12.field, f32[3,8,384]{2,1,0:T(8,128)S(1)} %get-tuple-element.13.own, bf16[13,8,384]{2,1,0:T(8,128)(2,1)S(1)} %collective-permute-done.following), custom_call_target="tpu_custom_call" | custom-call | tf_op jit(solution)/shard_map/arrival/pallas_call | solution.py:490
  25.3 5.3 %all-to-all-start = ((bf16[8,248,128]{2,1,0:T(8,128)(2,1)}), bf16[8,248,128]{2,1,0:T(8,128)(2,1)S(1)}, u32[]{:S(2)}, u32[]{:S(2)}) async-start(bf16[8,248,128]{2,1,0:T(8,128)(2,1)} %arrival.1), calls=%async_computation | async-start | bytes 1015808 | tf_op jit(solution)/shard_map/all_to_all | solution.py:554
  30.6 0.1 broadcast_multiply_fusion
  30.7 2.2 %legendre.1.functions = bf16[768,512]{1,0:T(8,128)(2,1)S(1)} custom-call(f32[768]{0:T(1024)S(1)} %get-tuple-element.23.step_a, f32[768]{0:T(1024)S(1)} %get-tuple-element.22.step_c, f32[8,128]{1,0:T(8,128)S(1)} %get-tuple-element.21.cosine, f32[8,128]{1,0:T(8,128)S(1)} %get-tuple-element.20.log_start, f32[8,128]{1,0:T(8,128)S(1)} %get-tuple-element.19.weight), custom_call_target="tpu_custom_call" | custom-call | tf_op jit(solution)/shard_map/legendre/pallas_call | solution.py:457
  32.9 0.1 broadcast_in_dim.40.waves
  33.0 0.0 copy-done
  33.0 1.3 %fourier.1 = (bf16[192,3200]{1,0:T(8,128)(2,1)S(1)}, f32[1,128]{1,0:T(1,128)S(1)}) custom-call(s32[192,128]{1,0:T(8,128)S(1)} %broadcast_in_dim.40.waves, s32[1,8]{1,0:T(1,128)S(1)} %bitcast.13, bf16[13,8,384]{2,1,0:T(8,128)(2,1)S(1)} %collective-permute-done.following), custom_call_target="tpu_custom_call" | custom-call | tf_op jit(solution)/shard_map/fourier/pallas_call | solution.py:441
  34.2 5.5 %all-to-all-done.cycles = bf16[8,248,128]{2,1,0:T(8,128)(2,1)S(1)} async-done(((bf16[8,248,128]{2,1,0:T(8,128)(2,1)}), bf16[8,248,128]{2,1,0:T(8,128)(2,1)S(1)}, u32[]{:S(2)}, u32[]{:S(2)}) %all-to-all-start) | async-done | bytes 507936 | tf_op jit(solution)/shard_map/all_to_all | solution.py:554
  39.7 0.6 transform.1
  40.3 20.1 %all_to_all.10 = bf16[96,2,128]{2,1,0:T(2,128)(2,1)S(1)} all-to-all(bf16[96,2,128]{2,1,0:T(2,128)(2,1)S(1)} %bitcast.11), channel_id=1, replica_groups=mesh['lat'=96,'lon'=8] {'lat'}, dimensions={0} | all-to-all | bytes 98304 | tf_op jit(solution)/shard_map/all_to_all | solution.py:566
  60.4 1.1 %synthesis.1 = f32[9,2,768]{2,1,0:T(2,128)} custom-call(bf16[192,128]{1,0:T(8,128)(2,1)S(1)} %bitcast.10, bf16[768,512]{1,0:T(8,128)(2,1)S(1)} %legendre.1.functions), custom_call_target="tpu_custom_call" | custom-call | tf_op jit(solution)/shard_map/synthesis/pallas_call | solution.py:522
  (4 shorter events, 0.0 us)
Async XLA Ops:
  0.8 22.6 %collective-permute-start = (bf16[13,8,384]{2,1,0:T(8,128)(2,1)S(1)}, bf16[13,8,384]{2,1,0:T(8,128)(2,1)S(1)}, u32[]{:S(2)}, u32[]{:S(2)}) collective-permute-start(bf16[13,8,384]{2,1,0:T(8,128)(2,1)S(1)} %get-tuple-element.14), channel_id=1, source_target_pairs={{8,0},{16,8},{24,16},{32,24},{40,32},{48,40},{56,48},{64,56},{72,6... | collective-permute-start | bytes 239624 | tf_op jit(solution)/shard_map/ppermute | solution.py:548
  23.4 9.6 %copy-start = (s32[8]{0:T(128)S(1)}, s32[8]{0:T(128)}, u32[]{:S(2)}) copy-start(s32[8]{0:T(128)} %param.10) | copy-start | bytes 100
  25.3 14.4 %all-to-all-start = ((bf16[8,248,128]{2,1,0:T(8,128)(2,1)}), bf16[8,248,128]{2,1,0:T(8,128)(2,1)S(1)}, u32[]{:S(2)}, u32[]{:S(2)}) async-start(bf16[8,248,128]{2,1,0:T(8,128)(2,1)} %arrival.1), calls=%async_computation | async-start | bytes 1015808 | tf_op jit(solution)/shard_map/all_to_all | solution.py:554
